TPU v7x, 512 devices: a whole 4x8x8 slice. The times are simulated.
512 devices in a mesh: mem: 64 (over z, y), ctx: 8 (over x, core).
Axes of the slice: x: 4, y: 8, z: 8, core: 2. Of those that a mesh axis runs over, the one named last changes fastest.
Arguments:
- queries: bfloat16 [32768, 4096], P(('mem', 'ctx')), may hold values from -400 to 400, as said below
- local_keys: bfloat16 [32768, 1024], P(('mem', 'ctx')), may hold values from -6 to 6
- local_values: bfloat16 [32768, 1024], P(('mem', 'ctx')), may hold values from -6 to 6
- mem_keys: bfloat16 [8192, 1024], P('mem'), may hold values from -6 to 6
- mem_values: bfloat16 [8192, 1024], P('mem'), may hold values from -6 to 6
- block_ids: int32 [2048, 16], P(('mem', 'ctx')), may hold values from 0 to 255, as said below
- gate_bias: float32 [32], replicated, may hold values from -3 to 3
Outputs:
- attended: bfloat16 [32768, 4096], P(('mem', 'ctx'))
Inputs may be any that keep to these rules, and one draw needn't show every extreme that they name: `block_ids`: the 16 blocks of one query block lie on 16 different indices of mem, block j lying on index j // 4; the 4 query blocks of rows q * 4 to (q + 1) * 4 - 1 together name every index of mem exactly once; some blocks are asked for far more often than others. `queries`: each query head's entries may carry a common scale.
All inputs are finite; a program needn't handle non-finite values.
Results may differ from a plain program's by a relative error of at most 0.005.
Values may be sent and summed in bfloat16 or wider, within the bound.
No kernel may reach another device: no remote copies, remote signals or barrier semaphores. Data moves between devices by JAX's collectives and lax.ppermute only.
A program may use at most 64 MiB of HBM per device.

v0:
```python
import jax
import jax.numpy as jnp
from jax import lax
from jax.sharding import PartitionSpec as P

HEADS = 32
KV_HEADS = 8
HEAD_DIM = 128
BLOCK = 32
TOPB = 16


def shifted(value, axis, steps):
    count = lax.axis_size(axis)
    leading, last = (max(0, -steps), min(count, count - steps))
    return lax.ppermute(value, axis, [(source, source + steps) for source in range(leading, last)])


def absorb(state, pair, start, query_heads, query_pos, scale):
    high, total, summed = state
    length = pair.shape[1]
    kv_heads = query_heads.shape[1]
    head_dim = query_heads.shape[3]
    keys = pair[0].reshape(length, kv_heads, head_dim)
    values = pair[1].reshape(length, kv_heads, head_dim)
    scores = (
        jnp.einsum("qhgd,khd->hgqk", query_heads, keys, preferred_element_type=jnp.float32) * scale
    )
    key_pos = start + jnp.arange(length, dtype=jnp.int32)
    allowed = (key_pos[None, :] <= query_pos[:, None])[None, None]
    scores = jnp.where(allowed, scores, -1e30)
    new_high = jnp.maximum(high, jnp.max(scores, axis=-1))
    factor = jnp.exp(high - new_high)
    weights = jnp.where(allowed, jnp.exp(scores - new_high[..., None]), 0.0)
    total = total * factor + jnp.sum(weights, axis=-1)
    summed = summed * jnp.transpose(factor, (2, 0, 1))[..., None] + jnp.einsum(
        "hgqk,khd->qhgd", weights.astype(jnp.bfloat16), values, preferred_element_type=jnp.float32
    )
    return (new_high, total, summed)


def body(queries, local_keys, local_values, mem_keys, mem_values, block_ids, gate_bias):
    groups = HEADS // KV_HEADS
    scale = HEAD_DIM ** (-0.5)
    tok_rows = queries.shape[0]
    width = mem_keys.shape[1]
    held_blocks = mem_keys.shape[0] // BLOCK
    members = lax.axis_size("mem")
    blocks_here = block_ids.shape[0]
    block_rows = tok_rows // blocks_here
    query_heads = queries.reshape(tok_rows, KV_HEADS, groups, HEAD_DIM)
    ctx_count = lax.axis_size("ctx")
    place = lax.axis_index("ctx")
    wanted_ids = block_ids.reshape(blocks_here * TOPB)
    owners = wanted_ids // held_blocks
    slots = wanted_ids % held_blocks
    matches = owners[None, :] == jnp.arange(members, dtype=jnp.int32)[:, None]
    wanted = jnp.sum(jnp.where(matches, slots[None, :], 0), axis=1).reshape(members, 1)
    asked = lax.all_to_all(wanted, "mem", split_axis=0, concat_axis=0, tiled=True)
    picks = asked[:, 0]
    picks = jnp.clip(picks, 0, held_blocks - 1)
    key_blocks = mem_keys.reshape(held_blocks, BLOCK, width)
    value_blocks = mem_values.reshape(held_blocks, BLOCK, width)
    got_keys, got_values = (
        lax.all_to_all(key_blocks[picks], "mem", split_axis=0, concat_axis=0, tiled=True),
        lax.all_to_all(value_blocks[picks], "mem", split_axis=0, concat_axis=0, tiled=True),
    )
    fetched_keys = got_keys[owners].reshape(blocks_here, TOPB * BLOCK, KV_HEADS, HEAD_DIM)
    fetched_values = got_values[owners].reshape(blocks_here, TOPB * BLOCK, KV_HEADS, HEAD_DIM)
    block_heads = query_heads.reshape(blocks_here, block_rows, KV_HEADS, groups, HEAD_DIM)

    def memory_block(items):
        heads_here, keys_here, values_here = items
        mem_scores = (
            jnp.einsum("qhgd,khd->hgqk", heads_here, keys_here, preferred_element_type=jnp.float32)
            * scale
        )
        mem_top = jnp.max(mem_scores, axis=-1, keepdims=True)
        mem_weights = jnp.exp(mem_scores - mem_top)
        mem_total = jnp.sum(mem_weights, axis=-1)
        product = jnp.einsum(
            "hgqk,khd->qhgd",
            mem_weights.astype(jnp.bfloat16),
            values_here,
            preferred_element_type=jnp.float32,
        )
        return product / jnp.transpose(mem_total, (2, 0, 1))[..., None]

    mem_out = lax.map(memory_block, (block_heads, fetched_keys, fetched_values)).reshape(
        tok_rows, KV_HEADS, groups, HEAD_DIM
    )
    stacked = jnp.stack([local_keys, local_values])
    query_pos = place * tok_rows + jnp.arange(tok_rows, dtype=jnp.int32)
    initial = (
        jnp.full((KV_HEADS, groups, tok_rows), -1e30, jnp.float32),
        jnp.zeros((KV_HEADS, groups, tok_rows), jnp.float32),
        jnp.zeros((tok_rows, KV_HEADS, groups, HEAD_DIM), jnp.float32),
    )
    current = stacked
    state = initial
    for step in range(ctx_count):
        if step > 0:
            current = shifted(current, "ctx", 1)

        def take_step(old, pair=current, start=(place - step) * tok_rows):
            return absorb(old, pair, start, query_heads, query_pos, scale)

        state = lax.cond(step <= place, take_step, lambda old: old, state)
    high, total, summed = state
    local_out = summed / jnp.transpose(total, (2, 0, 1))[..., None]
    gate = jax.nn.sigmoid(gate_bias).reshape(KV_HEADS, groups)[None, :, :, None]
    mixed = gate * mem_out + (1.0 - gate) * local_out
    return mixed.reshape(tok_rows, HEADS * HEAD_DIM).astype(jnp.bfloat16)


def solution(mesh):
    return jax.shard_map(
        body,
        mesh=mesh,
        in_specs=(
            P(("mem", "ctx"), None),
            P(("mem", "ctx"), None),
            P(("mem", "ctx"), None),
            P("mem", None),
            P("mem", None),
            P(("mem", "ctx"), None),
            P(),
        ),
        out_specs=P(("mem", "ctx"), None),
        check_vma=False,
    )
```

profile of v0, /device:TPU:118, one launch (start us, length us, event | category | flops | bytes accessed | tf_op | source)
XLA Modules:
  0.0 327.4 jit_solution(8013192343661380087)
XLA Ops:
  1.0 23.0 %all_to_all.19 = s32[64,1,1]{2,1,0:T(1,128)S(1)} all-to-all(s32[64,1,1]{2,1,0:T(1,128)S(1)} %copy.157), channel_id=1, replica_groups=mesh['mem'=64,'ctx'=8] {'mem'}, dimensions={0} | all-to-all | bytes 512 | tf_op jit(solution)/shard_map/all_to_all | solution.py:59
  28.0 9.6 %all-to-all-start.1 = ((bf16[64,32,1024]{2,1,0:T(8,128)(2,1)}), bf16[64,32,1024]{2,1,0:T(8,128)(2,1)}, u32[]{:S(2)}, u32[]{:S(2)}) async-start(bf16[64,32,1024]{2,1,0:T(8,128)(2,1)} %gather_fusion), calls=%async_computation.1 | async-start | bytes 8388608 | tf_op jit(solution)/shard_map/all_to_all | solution.py:66
  37.7 2.8 gather_fusion.2
  40.5 130.5 %all-to-all-done.1 = bf16[64,32,1024]{2,1,0:T(8,128)(2,1)} async-done(((bf16[64,32,1024]{2,1,0:T(8,128)(2,1)}), bf16[64,32,1024]{2,1,0:T(8,128)(2,1)}, u32[]{:S(2)}, u32[]{:S(2)}) %all-to-all-start.1) | async-done | bytes 4194336 | tf_op jit(solution)/shard_map/all_to_all | solution.py:66
  171.0 8.1 %all-to-all-start.2 = ((bf16[64,32,1024]{2,1,0:T(8,128)(2,1)}), bf16[64,32,1024]{2,1,0:T(8,128)(2,1)}, u32[]{:S(2)}, u32[]{:S(2)}) async-start(bf16[64,32,1024]{2,1,0:T(8,128)(2,1)} %gather_fusion.2), calls=%async_computation.2 | async-start | bytes 8388608 | tf_op jit(solution)/shard_map/all_to_all | solution.py:65
  181.1 5.8 %collective-permute-done = bf16[2,64,1024]{2,1,0:T(8,128)(2,1)S(1)} collective-permute-done((bf16[2,64,1024]{2,1,0:T(8,128)(2,1)S(1)}, bf16[2,64,1024]{2,1,0:T(8,128)(2,1)S(1)}, u32[]{:S(2)}, u32[]{:S(2)}) %collective-permute-start) | collective-permute-done | bytes 262176 | tf_op jit(solution)/shard_map/ppermute | solution.py:16
  188.8 5.8 %collective-permute-done.1 = bf16[2,64,1024]{2,1,0:T(8,128)(2,1)S(1)} collective-permute-done((bf16[2,64,1024]{2,1,0:T(8,128)(2,1)S(1)}, bf16[2,64,1024]{2,1,0:T(8,128)(2,1)S(1)}, u32[]{:S(2)}, u32[]{:S(2)}) %collective-permute-start.1) | collective-permute-done | bytes 262176 | tf_op jit(solution)/shard_map/ppermute | solution.py:16
  196.5 5.8 %collective-permute-done.2 = bf16[2,64,1024]{2,1,0:T(8,128)(2,1)S(1)} collective-permute-done((bf16[2,64,1024]{2,1,0:T(8,128)(2,1)S(1)}, bf16[2,64,1024]{2,1,0:T(8,128)(2,1)S(1)}, u32[]{:S(2)}, u32[]{:S(2)}) %collective-permute-start.2) | collective-permute-done | bytes 262176 | tf_op jit(solution)/shard_map/ppermute | solution.py:16
  204.1 5.8 %collective-permute-done.3 = bf16[2,64,1024]{2,1,0:T(8,128)(2,1)S(1)} collective-permute-done((bf16[2,64,1024]{2,1,0:T(8,128)(2,1)S(1)}, bf16[2,64,1024]{2,1,0:T(8,128)(2,1)S(1)}, u32[]{:S(2)}, u32[]{:S(2)}) %collective-permute-start.3) | collective-permute-done | bytes 262176 | tf_op jit(solution)/shard_map/ppermute | solution.py:16
  211.9 5.7 %collective-permute-done.4 = bf16[2,64,1024]{2,1,0:T(8,128)(2,1)S(1)} collective-permute-done((bf16[2,64,1024]{2,1,0:T(8,128)(2,1)S(1)}, bf16[2,64,1024]{2,1,0:T(8,128)(2,1)S(1)}, u32[]{:S(2)}, u32[]{:S(2)}) %collective-permute-start.4) | collective-permute-done | bytes 262176 | tf_op jit(solution)/shard_map/ppermute | solution.py:16
  220.1 5.3 %collective-permute-done.5 = bf16[2,64,1024]{2,1,0:T(8,128)(2,1)} collective-permute-done((bf16[2,64,1024]{2,1,0:T(8,128)(2,1)S(1)}, bf16[2,64,1024]{2,1,0:T(8,128)(2,1)}, u32[]{:S(2)}, u32[]{:S(2)}) %collective-permute-start.5) | collective-permute-done | bytes 262176 | tf_op jit(solution)/shard_map/ppermute | solution.py:16
  229.3 5.0 %conditional.8 = (f32[8,4,64]{2,1,0:T(4,128)}, f32[8,4,64]{2,1,0:T(4,128)S(1)}, f32[64,8,4,128]{3,0,2,1:T(8,128)S(1)}) conditional(s32[]{:T(128)} %convert_element_type.66, () %tuple.67, (s32[]{:T(128)}, s32[64]{0:T(128)}, bf16[64,1024]{1,0:T(8,128)(2,1)S(1)}, bf16[64,8,4,128]{3,2,1,0:T(4,128)(2,1)S(1)}, bf16[64,1024]{1,0:T(8,128)(2,1)S(1)}) %tuple.194), branch_computations={%region_5.6_spmd, %region_6.9_spmd} | conditional | flops 68563008 | bytes 4039452 | solution.py:108
  235.5 5.4 %conditional.9 = ((f32[8,4,64]{2,1,0:T(4,128)}, f32[8,4,64]{2,1,0:T(4,128)S(1)}, f32[64,8,4,128]{3,0,2,1:T(8,128)S(1)})) conditional(s32[]{:T(128)} %convert_element_type.65, (f32[8,4,64]{2,1,0:T(4,128)}, f32[8,4,64]{2,1,0:T(4,128)S(1)}, f32[64,8,4,128]{3,0,2,1:T(8,128)S(1)}) %conditional.8, (s32[]{:T(128)}, s32[64]{0:T(128)}, ...), branch_computations={%region_9.10_spmd, %region_10.13_spmd} | conditional | flops 68823104 | bytes 5653284 | solution.py:108
  241.0 5.4 %conditional.10 = ((f32[8,4,64]{2,1,0:T(4,128)}, f32[8,4,64]{2,1,0:T(4,128)S(1)}, f32[64,8,4,128]{3,0,2,1:T(8,128)S(1)})) conditional(s32[]{:T(128)} %convert_element_type.64, (f32[8,4,64]{2,1,0:T(4,128)}, f32[8,4,64]{2,1,0:T(4,128)S(1)}, f32[64,8,4,128]{3,0,2,1:T(8,128)S(1)}) %get-tuple-element.722, (s32[]{:T(128)}, s32[64]{0:T(128)}, ...), branch_computations={%region_13.14_spmd, %region_14.17_spmd} | conditional | flops 68823104 | bytes 5653284 | solution.py:108
  246.4 5.6 %conditional.11 = ((f32[8,4,64]{2,1,0:T(4,128)}, f32[8,4,64]{2,1,0:T(4,128)S(1)}, f32[64,8,4,128]{3,0,2,1:T(8,128)S(1)})) conditional(s32[]{:T(128)} %convert_element_type.63, (f32[8,4,64]{2,1,0:T(4,128)}, f32[8,4,64]{2,1,0:T(4,128)S(1)}, f32[64,8,4,128]{3,0,2,1:T(8,128)S(1)}) %get-tuple-element.723, (s32[]{:T(128)}, s32[64]{0:T(128)}, ...), branch_computations={%region_17.18_spmd, %region_18.21_spmd} | conditional | flops 68823104 | bytes 5653284 | solution.py:108
  252.0 5.4 %conditional.12 = ((f32[8,4,64]{2,1,0:T(4,128)}, f32[8,4,64]{2,1,0:T(4,128)S(1)}, f32[64,8,4,128]{3,0,2,1:T(8,128)S(1)})) conditional(s32[]{:T(128)} %convert_element_type.62, (f32[8,4,64]{2,1,0:T(4,128)}, f32[8,4,64]{2,1,0:T(4,128)S(1)}, f32[64,8,4,128]{3,0,2,1:T(8,128)S(1)}) %get-tuple-element.724, (s32[]{:T(128)}, s32[64]{0:T(128)}, ...), branch_computations={%region_21.22_spmd, %region_22.25_spmd} | conditional | flops 68823104 | bytes 5653284 | solution.py:108
  257.5 5.4 %conditional.13 = ((f32[8,4,64]{2,1,0:T(4,128)}, f32[8,4,64]{2,1,0:T(4,128)S(1)}, f32[64,8,4,128]{3,0,2,1:T(8,128)S(1)})) conditional(s32[]{:T(128)} %convert_element_type.61, (f32[8,4,64]{2,1,0:T(4,128)}, f32[8,4,64]{2,1,0:T(4,128)S(1)}, f32[64,8,4,128]{3,0,2,1:T(8,128)S(1)}) %get-tuple-element.725, (s32[]{:T(128)}, s32[64]{0:T(128)}, ...), branch_computations={%region_25.26_spmd, %region_26.29_spmd} | conditional | flops 68823104 | bytes 5653284 | solution.py:108
  262.9 7.0 %conditional.14 = ((f32[8,4,64]{2,1,0:T(4,128)}, f32[8,4,64]{2,1,0:T(4,128)S(1)}, f32[64,8,4,128]{3,0,2,1:T(8,128)S(1)})) conditional(s32[]{:T(128)} %convert_element_type.60, (f32[8,4,64]{2,1,0:T(4,128)}, f32[8,4,64]{2,1,0:T(4,128)S(1)}, f32[64,8,4,128]{3,0,2,1:T(8,128)S(1)}) %get-tuple-element.726, (s32[]{:T(128)}, s32[64]{0:T(128)}, ...), branch_computations={%region_29.30_spmd, %region_30.33_spmd} | conditional | flops 68823104 | bytes 5653308 | solution.py:108
  270.2 5.1 %gather_fusion.1 = bf16[64,32,1024]{2,1,0:T(8,128)(2,1)} fusion(bf16[64,32,1024]{2,1,0:T(8,128)(2,1)} %all-to-all-done.1, s32[1024]{0:T(1024)} %pad_clamp_fusion), kind=kCustom, calls=%fused_computation.1 | custom fusion | bytes 8388864 | tf_op jit(solution)/shard_map/gather | solution.py:69
  275.2 5.2 %copy.250 = bf16[256,8,8,128]{3,2,1,0:T(8,128)(2,1)} copy(bf16[256,8,8,128]{3,1,2,0:T(8,128)(2,1)} %bitcast.286) | data formatting | bytes 8388608
  280.5 21.7 %all-to-all-done.2 = bf16[64,32,1024]{2,1,0:T(8,128)(2,1)} async-done(((bf16[64,32,1024]{2,1,0:T(8,128)(2,1)}), bf16[64,32,1024]{2,1,0:T(8,128)(2,1)}, u32[]{:S(2)}, u32[]{:S(2)}) %all-to-all-start.2) | async-done | bytes 4194336 | tf_op jit(solution)/shard_map/all_to_all | solution.py:65
  302.2 5.1 %gather_fusion.3 = bf16[64,32,1024]{2,1,0:T(8,128)(2,1)} fusion(bf16[64,32,1024]{2,1,0:T(8,128)(2,1)} %all-to-all-done.2, s32[1024]{0:T(1024)} %pad_clamp_fusion), kind=kCustom, calls=%fused_computation.3 | custom fusion | bytes 8388864 | tf_op jit(solution)/shard_map/gather | solution.py:68
  307.3 5.2 %copy.251 = bf16[256,8,8,128]{3,2,1,0:T(8,128)(2,1)} copy(bf16[256,8,8,128]{3,1,2,0:T(8,128)(2,1)} %bitcast.285) | data formatting | bytes 8388608
  312.5 12.9 %while.10 = (s32[]{:T(128)}, f32[4,16,8,4,128]{4,1,0,3,2:T(8,128)S(1)}, bf16[4,512,8,128]{3,2,1,0:T(8,128)(2,1)}, bf16[4,512,8,128]{3,2,1,0:T(8,128)(2,1)}, bf16[4,16,8,4,128]{4,3,2,1,0:T(4,128)(2,1)S(1)}, /*index=5*/s32[]{:T(128)}) while((s32[]{:T(128)}, f32[4,16,8,4,128]{4,1,0,3,2:T(8,128)S(1)}, bf16[4,512,8,128]{3,2,1,0:T(8,128)(2,1)}, ...), condition=%wide.region_4.5_spmd, body=%wide.region_1.4_spmd.sunk | while | flops 135855104 | bytes 10131545 | solution.py:89
  (154 shorter events, 76.2 us)
Async XLA Ops:
  0.0 25.3 %copy-start = (bf16[128,1024]{1,0:T(8,128)(2,1)S(1)}, bf16[128,1024]{1,0:T(8,128)(2,1)}, u32[]{:S(2)}) copy-start(bf16[128,1024]{1,0:T(8,128)(2,1)} %param.29) | copy-start | bytes 786436
  28.0 9.6 %copy-start.1 = (bf16[128,1024]{1,0:T(8,128)(2,1)S(1)}, bf16[128,1024]{1,0:T(8,128)(2,1)}, u32[]{:S(2)}) copy-start(bf16[128,1024]{1,0:T(8,128)(2,1)} %param.28) | copy-start | bytes 786436
  28.0 143.0 %all-to-all-start.1 = ((bf16[64,32,1024]{2,1,0:T(8,128)(2,1)}), bf16[64,32,1024]{2,1,0:T(8,128)(2,1)}, u32[]{:S(2)}, u32[]{:S(2)}) async-start(bf16[64,32,1024]{2,1,0:T(8,128)(2,1)} %gather_fusion), calls=%async_computation.1 | async-start | bytes 8388608 | tf_op jit(solution)/shard_map/all_to_all | solution.py:66
  40.5 138.6 %copy-start.3 = (bf16[64,1024]{1,0:T(8,128)(2,1)S(1)}, bf16[64,1024]{1,0:T(8,128)(2,1)}, u32[]{:S(2)}) copy-start(bf16[64,1024]{1,0:T(8,128)(2,1)} %param.26) | copy-start | bytes 393220
  40.5 138.7 %copy-start.4 = (bf16[64,1024]{1,0:T(8,128)(2,1)S(1)}, bf16[64,1024]{1,0:T(8,128)(2,1)}, u32[]{:S(2)}) copy-start(bf16[64,1024]{1,0:T(8,128)(2,1)} %param.27) | copy-start | bytes 393220
  40.5 171.4 %copy-start.12 = (s32[4,16]{1,0:T(4,128)S(1)}, s32[4,16]{1,0:T(4,128)}, u32[]{:S(2)}) copy-start(s32[4,16]{1,0:T(4,128)} %param.30) | copy-start | bytes 772
  40.5 179.6 %copy-start.13 = (f32[32]{0:T(128)S(1)}, f32[32]{0:T(128)}, u32[]{:S(2)}) copy-start(f32[32]{0:T(128)} %param.31) | copy-start | bytes 388
  40.5 187.3 %copy-start.2 = (bf16[64,4096]{1,0:T(8,128)(2,1)S(1)}, bf16[64,4096]{1,0:T(8,128)(2,1)}, u32[]{:S(2)}) copy-start(bf16[64,4096]{1,0:T(8,128)(2,1)} %param.25) | copy-start | bytes 1572868
  171.0 131.2 %all-to-all-start.2 = ((bf16[64,32,1024]{2,1,0:T(8,128)(2,1)}), bf16[64,32,1024]{2,1,0:T(8,128)(2,1)}, u32[]{:S(2)}, u32[]{:S(2)}) async-start(bf16[64,32,1024]{2,1,0:T(8,128)(2,1)} %gather_fusion.2), calls=%async_computation.2 | async-start | bytes 8388608 | tf_op jit(solution)/shard_map/all_to_all | solution.py:65
  179.2 7.7 %collective-permute-start = (bf16[2,64,1024]{2,1,0:T(8,128)(2,1)S(1)}, bf16[2,64,1024]{2,1,0:T(8,128)(2,1)S(1)}, u32[]{:S(2)}, u32[]{:S(2)}) collective-permute-start(bf16[2,64,1024]{2,1,0:T(8,128)(2,1)S(1)} %pad_maximum_fusion), channel_id=1, source_target_pairs={{0,1},{1,2},{2,3},{3,4},{4,5},{5,6},{6,7},{8,9},{9,10},{10,11},{11... | collective-permute-start | bytes 786440 | tf_op jit(solution)/shard_map/ppermute | solution.py:16
  186.8 1.9 copy-start.9
  186.8 7.7 %collective-permute-start.1 = (bf16[2,64,1024]{2,1,0:T(8,128)(2,1)S(1)}, bf16[2,64,1024]{2,1,0:T(8,128)(2,1)S(1)}, u32[]{:S(2)}, u32[]{:S(2)}) collective-permute-start(bf16[2,64,1024]{2,1,0:T(8,128)(2,1)S(1)} %collective-permute-done), channel_id=1, source_target_pairs={{0,1},{1,2},{2,3},{3,4},{4,5},{5,6},{6,7},{8,9},{9,10},{10,11},{11... | collective-permute-start | bytes 786440 | tf_op jit(solution)/shard_map/ppermute | solution.py:16
  194.5 1.9 copy-start.8
  194.5 7.7 %collective-permute-start.2 = (bf16[2,64,1024]{2,1,0:T(8,128)(2,1)S(1)}, bf16[2,64,1024]{2,1,0:T(8,128)(2,1)S(1)}, u32[]{:S(2)}, u32[]{:S(2)}) collective-permute-start(bf16[2,64,1024]{2,1,0:T(8,128)(2,1)S(1)} %collective-permute-done.1), channel_id=1, source_target_pairs={{0,1},{1,2},{2,3},{3,4},{4,5},{5,6},{6,7},{8,9},{9,10},{10,11},{11... | collective-permute-start | bytes 786440 | tf_op jit(solution)/shard_map/ppermute | solution.py:16
  202.2 1.9 copy-start.7
  202.2 7.7 %collective-permute-start.3 = (bf16[2,64,1024]{2,1,0:T(8,128)(2,1)S(1)}, bf16[2,64,1024]{2,1,0:T(8,128)(2,1)S(1)}, u32[]{:S(2)}, u32[]{:S(2)}) collective-permute-start(bf16[2,64,1024]{2,1,0:T(8,128)(2,1)S(1)} %collective-permute-done.2), channel_id=1, source_target_pairs={{0,1},{1,2},{2,3},{3,4},{4,5},{5,6},{6,7},{8,9},{9,10},{10,11},{11... | collective-permute-start | bytes 786440 | tf_op jit(solution)/shard_map/ppermute | solution.py:16
  209.9 17.9 %copy-start.6 = (bf16[2,64,1024]{2,1,0:T(8,128)(2,1)}, bf16[2,64,1024]{2,1,0:T(8,128)(2,1)S(1)}, u32[]{:S(2)}) copy-start(bf16[2,64,1024]{2,1,0:T(8,128)(2,1)S(1)} %collective-permute-done.3) | copy-start | bytes 786436
  209.9 7.7 %collective-permute-start.4 = (bf16[2,64,1024]{2,1,0:T(8,128)(2,1)S(1)}, bf16[2,64,1024]{2,1,0:T(8,128)(2,1)S(1)}, u32[]{:S(2)}, u32[]{:S(2)}) collective-permute-start(bf16[2,64,1024]{2,1,0:T(8,128)(2,1)S(1)} %collective-permute-done.3), channel_id=1, source_target_pairs={{0,1},{1,2},{2,3},{3,4},{4,5},{5,6},{6,7},{8,9},{9,10},{10,11},{11... | collective-permute-start | bytes 786440 | tf_op jit(solution)/shard_map/ppermute | solution.py:16
  217.6 11.7 %copy-start.5 = (bf16[2,64,1024]{2,1,0:T(8,128)(2,1)}, bf16[2,64,1024]{2,1,0:T(8,128)(2,1)S(1)}, u32[]{:S(2)}) copy-start(bf16[2,64,1024]{2,1,0:T(8,128)(2,1)S(1)} %collective-permute-done.4) | copy-start | bytes 786436
  217.6 7.8 %collective-permute-start.5 = (bf16[2,64,1024]{2,1,0:T(8,128)(2,1)S(1)}, bf16[2,64,1024]{2,1,0:T(8,128)(2,1)}, u32[]{:S(2)}, u32[]{:S(2)}) collective-permute-start(bf16[2,64,1024]{2,1,0:T(8,128)(2,1)S(1)} %collective-permute-done.4), channel_id=1, source_target_pairs={{0,1},{1,2},{2,3},{3,4},{4,5},{5,6},{6,7},{8,9},{9,10},{10,11},{11... | collective-permute-start | bytes 786440 | tf_op jit(solution)/shard_map/ppermute | solution.py:16
  225.4 44.6 %collective-permute-start.6 = (bf16[2,64,1024]{2,1,0:T(8,128)(2,1)}, bf16[2,64,1024]{2,1,0:T(8,128)(2,1)}, u32[]{:S(2)}, u32[]{:S(2)}) collective-permute-start(bf16[2,64,1024]{2,1,0:T(8,128)(2,1)} %collective-permute-done.5), channel_id=1, source_target_pairs={{0,1},{1,2},{2,3},{3,4},{4,5},{5,6},{6,7},{8,9},{9,10},{10,11},{11... | collective-permute-start | bytes 786440 | tf_op jit(solution)/shard_map/ppermute | solution.py:16
  312.5 12.9 %copy-start.10 = (f32[8,4]{1,0:T(8,128)S(1)}, f32[8,4]{1,0:T(8,128)}, u32[]{:S(2)}) copy-start(f32[8,4]{1,0:T(8,128)} %mul.191) | copy-start | bytes 388
  312.5 12.9 %copy-start.11 = (f32[8,4]{1,0:T(8,128)S(1)}, f32[8,4]{1,0:T(8,128)}, u32[]{:S(2)}) copy-start(f32[8,4]{1,0:T(8,128)} %broadcast_subtract_fusion) | copy-start | bytes 388
where the time goes:
time: 329 us; the launch traced here: 327 us
  waiting for transfers between devices  186 us (57%)
  local copies, waits for them, and re-layouts  47.6 us (14%)
  starting transfers between devices  31.1 us (9%)
  other arithmetic  23.2 us (7%)
  blocking collectives  23 us (7%)
  matrix products  15.2 us (5%)
    all_to_all x1, waiting for transfers between devices, body(): lax.all_to_all(value_blocks[picks], 'mem', split_axis=0, concat_axis=0, t...  131 us
    ppermute x7, waiting for transfers between devices, shifted(): lax.ppermute(value, axis, [(source, source + steps) for source in range(l...  33.9 us
    all_to_all x1, blocking collectives, body(): lax.all_to_all(wanted, 'mem', split_axis=0, concat_axis=0, tiled=True)  23 us
    all_to_all x1, waiting for transfers between devices, body(): lax.all_to_all(key_blocks[picks], 'mem', split_axis=0, concat_axis=0, til...  21.7 us
    ppermute x7, starting transfers between devices, shifted(): lax.ppermute(value, axis, [(source, source + steps) for source in range(l...  13.4 us
    unnamed x30, local copies, waits for them, and re-layouts  10.5 us
    cond x26, local copies, waits for them, and re-layouts  10.5 us
    all_to_all x1, starting transfers between devices, body(): lax.all_to_all(value_blocks[picks], 'mem', split_axis=0, concat_axis=0, t...  9.61 us
  transfers between devices with their start and end apart: 9, of which 8 were waited for; matrix products, arithmetic and copies ran while one was open for 17% of the time, Pallas kernels for 0%

commit v1 on v0

v1 whole, which is shorter than its diff:
```python
import functools

import jax
import jax.numpy as jnp
from jax import lax
from jax.experimental import pallas as pl
from jax.experimental.pallas import tpu as pltpu
from jax.sharding import PartitionSpec as P

HEADS = 32
KV_HEADS = 8
GROUPS = HEADS // KV_HEADS
HEAD_DIM = 128
BLOCK = 32
TOPB = 16
QBLOCK = 16
LANES = GROUPS * HEAD_DIM
EXP2_SCALE = HEAD_DIM ** (-0.5) * 1.4426950408889634
NEG = -1e30
TILE = 128


def product(left, right, contract_right):
    return lax.dot_general(
        left, right, (((1,), (contract_right,)), ((), ())), preferred_element_type=jnp.float32
    )


def softmax_parts(scores):
    top = jnp.max(scores, axis=-1, keepdims=True)
    weights = jnp.exp2((scores - top) * EXP2_SCALE)
    return weights, jnp.sum(weights, axis=-1, keepdims=True)


def heads_to_rows(rows):
    return jnp.concatenate(
        [rows[:, h * HEAD_DIM : (h + 1) * HEAD_DIM] for h in range(GROUPS)], axis=0
    )


def local_kernel(qkv_ref, out_ref):
    span = qkv_ref.shape[0]
    for tile in range(span // TILE):
        lo, hi = tile * TILE, (tile + 1) * TILE
        query = heads_to_rows(qkv_ref[lo:hi, :LANES])
        keys = qkv_ref[:hi, LANES : LANES + HEAD_DIM]
        values = qkv_ref[:hi, LANES + HEAD_DIM : LANES + 2 * HEAD_DIM]
        scores = product(query, keys, 1)
        row = lax.broadcasted_iota(jnp.int32, scores.shape, 0) % TILE + lo
        col = lax.broadcasted_iota(jnp.int32, scores.shape, 1)
        scores = jnp.where(col <= row, scores, NEG)
        weights, total = softmax_parts(scores)
        summed = product(weights.astype(jnp.bfloat16), values, 0) / total
        for h in range(GROUPS):
            out_ref[lo:hi, h * HEAD_DIM : (h + 1) * HEAD_DIM] = summed[
                h * TILE : (h + 1) * TILE
            ]


def memory_kernel(ids_ref, bias_ref, qkv_ref, keys_ref, values_ref, local_ref, out_ref):
    head = lax.axis_index("ctx")
    gates = [
        jax.nn.sigmoid(jnp.full((1, HEAD_DIM), bias_ref[head * GROUPS + h], jnp.float32))
        for h in range(GROUPS)
    ]
    query_blocks = qkv_ref.shape[0] // QBLOCK

    def one_block(index, carry):
        lo = pl.multiple_of(index * QBLOCK, QBLOCK)
        query = heads_to_rows(qkv_ref[pl.ds(lo, QBLOCK), :LANES])
        starts = [pl.multiple_of(ids_ref[index, j] * BLOCK, BLOCK) for j in range(TOPB)]
        keys = jnp.concatenate([keys_ref[pl.ds(s, BLOCK), :] for s in starts], axis=0)
        values = jnp.concatenate([values_ref[pl.ds(s, BLOCK), :] for s in starts], axis=0)
        weights, total = softmax_parts(product(query, keys, 1))
        summed = product(weights.astype(jnp.bfloat16), values, 0) / total
        for h in range(GROUPS):
            lanes = slice(h * HEAD_DIM, (h + 1) * HEAD_DIM)
            local_out = local_ref[pl.ds(lo, QBLOCK), lanes]
            mixed = gates[h] * summed[h * QBLOCK : (h + 1) * QBLOCK] + (1.0 - gates[h]) * local_out
            out_ref[pl.ds(lo, QBLOCK), lanes] = mixed.astype(jnp.bfloat16)
        return carry

    lax.fori_loop(0, query_blocks, one_block, 0, unroll=2)


def body(queries, local_keys, local_values, mem_keys, mem_values, block_ids, gate_bias):
    tokens = queries.shape[0]
    members = lax.axis_size("ctx")
    head = lax.axis_index("ctx")
    span = tokens * members
    start = head * HEAD_DIM
    own_keys = lax.dynamic_slice_in_dim(mem_keys, start, HEAD_DIM, 1)
    own_values = lax.dynamic_slice_in_dim(mem_values, start, HEAD_DIM, 1)
    all_keys = lax.all_gather(own_keys, "mem", axis=0, tiled=True)
    all_values = lax.all_gather(own_values, "mem", axis=0, tiled=True)
    ids = lax.all_gather(block_ids, "ctx", axis=0, tiled=True)
    packed = jnp.concatenate(
        [
            queries.reshape(tokens, members, LANES),
            local_keys.reshape(tokens, members, HEAD_DIM),
            local_values.reshape(tokens, members, HEAD_DIM),
        ],
        axis=2,
    )
    packed = jnp.transpose(packed, (1, 0, 2))
    qkv = lax.all_to_all(packed, "ctx", split_axis=0, concat_axis=0, tiled=True)
    qkv = qkv.reshape(span, LANES + 2 * HEAD_DIM)
    vmem = pl.BlockSpec(memory_space=pltpu.VMEM)
    smem = pl.BlockSpec(memory_space=pltpu.SMEM)
    local_out = pl.pallas_call(
        local_kernel,
        out_shape=jax.ShapeDtypeStruct((span, LANES), jnp.float32),
        in_specs=[vmem],
        out_specs=vmem,
        cost_estimate=pl.CostEstimate(
            flops=4 * span * LANES * span, bytes_accessed=2 << 20, transcendentals=span * span * 4
        ),
    )(qkv)
    mixed = pl.pallas_call(
        memory_kernel,
        out_shape=jax.ShapeDtypeStruct((span, LANES), jnp.bfloat16),
        in_specs=[smem, smem, vmem, vmem, vmem, vmem],
        out_specs=vmem,
        cost_estimate=pl.CostEstimate(
            flops=4 * span * LANES * TOPB * BLOCK,
            bytes_accessed=7 << 20,
            transcendentals=span * GROUPS * TOPB * BLOCK,
        ),
    )(ids, gate_bias, qkv, all_keys, all_values, local_out)
    back = lax.all_to_all(
        mixed.reshape(members, tokens, LANES), "ctx", split_axis=0, concat_axis=0, tiled=True
    )
    return jnp.transpose(back, (1, 0, 2)).reshape(tokens, HEADS * HEAD_DIM)


def solution(mesh):
    return jax.shard_map(
        body,
        mesh=mesh,
        in_specs=(
            P(("mem", "ctx"), None),
            P(("mem", "ctx"), None),
            P(("mem", "ctx"), None),
            P("mem", None),
            P("mem", None),
            P(("mem", "ctx"), None),
            P(),
        ),
        out_specs=P(("mem", "ctx"), None),
        check_vma=False,
    )
```

time: 329 us -> 220 us (0.67)
  the two profiles are of different devices: /device:TPU:118 before, /device:TPU:1 now
where the time goes in v1:
time: 220 us; the launch traced here: 219 us
  waiting for transfers between devices  133 us (60%)
  blocking collectives  36.7 us (17%)
  Pallas kernels  17.6 us (8%)
  between operations  13.4 us (6%)
  starting transfers between devices  10.4 us (5%)
  local copies, waits for them, and re-layouts  6.82 us (3%)
    all_gather x1, waiting for transfers between devices, body(): all_values = lax.all_gather(own_values, 'mem', axis=0, tiled=True)  83.6 us
    all_gather x1, waiting for transfers between devices, body(): all_keys = lax.all_gather(own_keys, 'mem', axis=0, tiled=True)  49.7 us
    all_gather x1, blocking collectives, body(): ids = lax.all_gather(block_ids, 'ctx', axis=0, tiled=True)  18.5 us
    all_to_all x1, blocking collectives, body(): lax.all_to_all(mixed.reshape(members, tokens, LANES), 'ctx', split_axis=0...  18.2 us
    pallas_call x1, Pallas kernels, body(): pl.pallas_call(memory_kernel, out_shape=jax.ShapeDtypeStruct((span, LANES...  13.9 us
    all_to_all x1, starting transfers between devices, body(): qkv = lax.all_to_all(packed, 'ctx', split_axis=0, concat_axis=0, tiled=True)  10.3 us
  transfers between devices with their start and end apart: 3, of which 2 were waited for; matrix products, arithmetic and copies ran while one was open for 2% of the time, Pallas kernels for 2%

profile of v1, /device:TPU:1, one launch (start us, length us, event | category | flops | bytes accessed | tf_op | source)
XLA Modules:
  0.0 219.1 jit_solution(2883681370337584679)
XLA Ops:
  6.5 0.0 copy-start
  6.5 0.0 all-gather.4.cloned.1.call-start
  6.5 0.9 copy-done
  7.5 0.6 constant_dynamic-slice_fusion.1
  8.1 0.0 all-gather.4.cloned.1.call-update
  8.1 0.0 all-gather.6.cloned.1.call-start
  8.2 1.4 constant_dynamic-slice_fusion
  9.6 0.0 all-gather.6.cloned.1.call-update
  9.6 1.1 copy.23
  10.7 1.0 copy_bitcast_fusion.1
  11.7 0.0 copy-start.2
  11.7 1.0 maximum_bitcast_fusion
  12.7 10.3 %all-to-all-start = ((bf16[8,64,768]{2,1,0:T(8,128)(2,1)}), bf16[8,64,768]{2,1,0:T(8,128)(2,1)S(1)}, u32[]{:S(2)}, u32[]{:S(2)}) async-start(bf16[8,64,768]{2,1,0:T(8,128)(2,1)} %maximum_bitcast_fusion), calls=%async_computation | async-start | bytes 1572864 | tf_op jit(solution)/shard_map/all_to_all | solution.py:106
  23.0 0.0 copy-done.2
  23.0 18.5 %all-gather = s32[8,4,16]{2,1,0:T(4,128)} all-gather(s32[1,4,16]{2,1,0:T(4,128)S(1)} %bitcast.30), channel_id=1, replica_groups=mesh['mem'=64,'ctx'=8] {'ctx'}, dimensions={0}, use_global_device_ids=true | all-gather | bytes 2304 | tf_op jit(solution)/shard_map/all_gather | solution.py:96
  41.5 0.0 all-to-all-done
  41.5 0.0 copy-start.1
  41.5 0.9 copy-done.1
  42.4 3.7 %shard_map.73.local_ref = f32[512,512]{1,0:T(8,128)} custom-call(bf16[512,768]{1,0:T(8,128)(2,1)} %bitcast.23), custom_call_target="tpu_custom_call" | custom-call | flops 536870912 | bytes 2097152 | tf_op jit(solution)/shard_map/pallas_call | solution.py:110
  46.1 49.7 %all-gather.4.cloned.1.call-done.keys_ref = bf16[8192,128]{1,0:T(8,128)(2,1)} async-done(((bf16[128,128]{1,0:T(8,128)(2,1)}), bf16[8192,128]{1,0:T(8,128)(2,1)}) %all-gather.4.cloned.1.call-update) | async-done | bytes 2097168 | tf_op jit(solution)/shard_map/all_gather | solution.py:94
  95.7 83.6 %all-gather.6.cloned.1.call-done.values_ref = bf16[8192,128]{1,0:T(8,128)(2,1)} async-done(((bf16[128,128]{1,0:T(8,128)(2,1)}), bf16[8192,128]{1,0:T(8,128)(2,1)}) %all-gather.6.cloned.1.call-update) | async-done | bytes 2097168 | tf_op jit(solution)/shard_map/all_gather | solution.py:95
  179.4 13.9 %shard_map.74 = bf16[512,512]{1,0:T(8,128)(2,1)} custom-call(s32[32,16]{1,0:T(8,128)} %bitcast.29, f32[32]{0:T(128)} %bias_ref.1, bf16[512,768]{1,0:T(8,128)(2,1)} %bitcast.24, bf16[8192,128]{1,0:T(8,128)(2,1)} %all-gather.4.cloned.1.call-done.keys_ref, bf16[8192,128]{1,0:T(8,128)(2,1)} %all-gather.6.cloned.1.call-done.values_ref, ...), custom_call_target="tpu_custom_call" | custom-call | flops 536870912 | bytes 7340032 | tf_op jit(solution)/shard_map/pallas_call | solution.py:119
  193.2 18.2 %all_to_all.10 = bf16[8,64,512]{2,1,0:T(8,128)(2,1)S(1)} all-to-all(bf16[8,64,512]{2,1,0:T(8,128)(2,1)} %bitcast.27), channel_id=1, replica_groups=mesh['mem'=64,'ctx'=8] {'ctx'}, dimensions={0} | all-to-all | bytes 1048576 | tf_op jit(solution)/shard_map/all_to_all | solution.py:130
  211.4 0.8 copy.19
Async XLA Ops:
  6.5 1.0 copy-start
  6.5 89.2 %all-gather.4.cloned.1.call-start = ((), (), s32[]{:S(2)}) async-start(), calls=%async_computation.2 | async-start | bytes 2129920 | tf_op jit(solution)/shard_map/all_gather | solution.py:94
  8.1 171.2 %all-gather.6.cloned.1.call-start = ((), (), s32[]{:S(2)}) async-start(), calls=%async_computation.3 | async-start | bytes 2129920 | tf_op jit(solution)/shard_map/all_gather | solution.py:95
  11.7 11.3 %copy-start.2 = (s32[4,16]{1,0:T(4,128)S(1)}, s32[4,16]{1,0:T(4,128)}, u32[]{:S(2)}) copy-start(s32[4,16]{1,0:T(4,128)} %param.12) | copy-start | bytes 772
  12.7 28.8 %all-to-all-start = ((bf16[8,64,768]{2,1,0:T(8,128)(2,1)}), bf16[8,64,768]{2,1,0:T(8,128)(2,1)S(1)}, u32[]{:S(2)}, u32[]{:S(2)}) async-start(bf16[8,64,768]{2,1,0:T(8,128)(2,1)} %maximum_bitcast_fusion), calls=%async_computation | async-start | bytes 1572864 | tf_op jit(solution)/shard_map/all_to_all | solution.py:106
  41.5 0.9 copy-start.1
Sparse Core Ops, SparseCore 0:
  10.4 85.2 all-gather.3
  98.8 80.4 all-gather.5

commit v2 on v1

--- a/solution.py
+++ b/solution.py
@@ -57,20 +57,35 @@
             ]
 
 
-def memory_kernel(ids_ref, bias_ref, qkv_ref, keys_ref, values_ref, local_ref, out_ref):
+def memory_kernel(starts_ref, bias_ref, qkv_ref, local_ref, *refs):
+    chunks, (out_ref, store_ref, sems) = refs[:-3], refs[-3:]
+    copies, row = [], 0
+    for i, chunk in enumerate(chunks):
+        rows = chunk.shape[0]
+        copies.append(
+            pltpu.make_async_copy(chunk, store_ref.at[pl.ds(row, rows)], sems.at[i])
+        )
+        copies[-1].start()
+        row += rows
     head = lax.axis_index("ctx")
     gates = [
         jax.nn.sigmoid(jnp.full((1, HEAD_DIM), bias_ref[head * GROUPS + h], jnp.float32))
         for h in range(GROUPS)
     ]
     query_blocks = qkv_ref.shape[0] // QBLOCK
+    for copy in copies:
+        copy.wait()
 
     def one_block(index, carry):
         lo = pl.multiple_of(index * QBLOCK, QBLOCK)
         query = heads_to_rows(qkv_ref[pl.ds(lo, QBLOCK), :LANES])
-        starts = [pl.multiple_of(ids_ref[index, j] * BLOCK, BLOCK) for j in range(TOPB)]
-        keys = jnp.concatenate([keys_ref[pl.ds(s, BLOCK), :] for s in starts], axis=0)
-        values = jnp.concatenate([values_ref[pl.ds(s, BLOCK), :] for s in starts], axis=0)
+        starts = [pl.multiple_of(starts_ref[index, j], BLOCK) for j in range(TOPB)]
+        keys = jnp.concatenate(
+            [store_ref[pl.ds(s, BLOCK), :HEAD_DIM] for s in starts], axis=0
+        )
+        values = jnp.concatenate(
+            [store_ref[pl.ds(s, BLOCK), HEAD_DIM:] for s in starts], axis=0
+        )
         weights, total = softmax_parts(product(query, keys, 1))
         summed = product(weights.astype(jnp.bfloat16), values, 0) / total
         for h in range(GROUPS):
@@ -83,30 +98,105 @@
     lax.fori_loop(0, query_blocks, one_block, 0, unroll=2)
 
 
+BOTH = ("mem", "ctx")
+SIDE = 8
+CTX = 8
+
+
+def device(z, y, ctx):
+    return (z * SIDE + y) * CTX + ctx
+
+
+def ring_of(ctx):
+    return ctx % 2
+
+
+def first_groups():
+    groups = []
+    for ctx in range(CTX):
+        for other in range(SIDE):
+            if ring_of(ctx) == 0:
+                groups.append([device(z, other, ctx) for z in range(SIDE)])
+            else:
+                groups.append([device(other, y, ctx) for y in range(SIDE)])
+    return groups
+
+
+def shifted(value, step):
+    pairs = []
+    for z in range(SIDE):
+        for y in range(SIDE):
+            for ctx in range(CTX):
+                if ring_of(ctx) == 0:
+                    target = device(z, (y + step) % SIDE, ctx)
+                else:
+                    target = device((z + step) % SIDE, y, ctx)
+                pairs.append((device(z, y, ctx), target))
+    return lax.ppermute(value, BOTH, pairs)
+
+
+def gathered(own):
+    rows = own.shape[0]
+    spread = jnp.broadcast_to(own[None], (SIDE,) + own.shape)
+    chunk = lax.all_to_all(
+        spread, BOTH, split_axis=0, concat_axis=0, tiled=True, axis_index_groups=first_groups()
+    ).reshape(SIDE * rows, own.shape[1])
+    ahead, behind = [chunk], [chunk]
+    for _ in range(SIDE // 2 - 1):
+        ahead.append(shifted(ahead[-1], 1))
+        behind.append(shifted(behind[-1], -1))
+    half = chunk.shape[0] // 2
+    last_ahead = shifted(ahead[-1][:half], 1)
+    last_behind = shifted(behind[-1][half:], -1)
+    return ahead + [last_ahead, last_behind] + behind[:0:-1]
+
+
+def block_rows(ids, held, rows):
+    holder, slot = ids // held, ids % held
+    z, y = holder // SIDE, holder % SIDE
+    mem = lax.axis_index("mem")
+    own_z, own_y = mem // SIDE, mem % SIDE
+    first = ring_of(lax.axis_index("ctx")) == 0
+    back = jnp.where(first, own_y - y, own_z - z) % SIDE
+    inner = jnp.where(first, z, y)
+    return (back * SIDE + inner) * rows + slot * BLOCK
+
+
 def body(queries, local_keys, local_values, mem_keys, mem_values, block_ids, gate_bias):
     tokens = queries.shape[0]
     members = lax.axis_size("ctx")
     head = lax.axis_index("ctx")
     span = tokens * members
+    rows = mem_keys.shape[0]
     start = head * HEAD_DIM
-    own_keys = lax.dynamic_slice_in_dim(mem_keys, start, HEAD_DIM, 1)
-    own_values = lax.dynamic_slice_in_dim(mem_values, start, HEAD_DIM, 1)
-    all_keys = lax.all_gather(own_keys, "mem", axis=0, tiled=True)
-    all_values = lax.all_gather(own_values, "mem", axis=0, tiled=True)
-    ids = lax.all_gather(block_ids, "ctx", axis=0, tiled=True)
+    own = jnp.concatenate(
+        [
+            lax.dynamic_slice_in_dim(mem_keys, start, HEAD_DIM, 1),
+            lax.dynamic_slice_in_dim(mem_values, start, HEAD_DIM, 1),
+        ],
+        axis=1,
+    )
+    chunks = gathered(own)
+    id_lanes = jnp.broadcast_to(
+        block_ids.reshape(tokens, 1, 1).astype(jnp.bfloat16), (tokens, members, HEAD_DIM)
+    )
     packed = jnp.concatenate(
         [
             queries.reshape(tokens, members, LANES),
             local_keys.reshape(tokens, members, HEAD_DIM),
             local_values.reshape(tokens, members, HEAD_DIM),
+            id_lanes,
         ],
         axis=2,
     )
     packed = jnp.transpose(packed, (1, 0, 2))
     qkv = lax.all_to_all(packed, "ctx", split_axis=0, concat_axis=0, tiled=True)
-    qkv = qkv.reshape(span, LANES + 2 * HEAD_DIM)
+    qkv = qkv.reshape(span, LANES + 3 * HEAD_DIM)
+    ids = qkv[:, LANES + 2 * HEAD_DIM].astype(jnp.int32).reshape(span // QBLOCK, TOPB)
+    starts = block_rows(ids, rows // BLOCK, rows)
     vmem = pl.BlockSpec(memory_space=pltpu.VMEM)
     smem = pl.BlockSpec(memory_space=pltpu.SMEM)
+    hbm = pl.BlockSpec(memory_space=pl.ANY)
     local_out = pl.pallas_call(
         local_kernel,
         out_shape=jax.ShapeDtypeStruct((span, LANES), jnp.float32),
@@ -119,14 +209,18 @@
     mixed = pl.pallas_call(
         memory_kernel,
         out_shape=jax.ShapeDtypeStruct((span, LANES), jnp.bfloat16),
-        in_specs=[smem, smem, vmem, vmem, vmem, vmem],
+        in_specs=[smem, smem, vmem, vmem] + [hbm] * len(chunks),
         out_specs=vmem,
+        scratch_shapes=[
+            pltpu.VMEM((SIDE * SIDE * rows, 2 * HEAD_DIM), jnp.bfloat16),
+            pltpu.SemaphoreType.DMA((len(chunks),)),
+        ],
         cost_estimate=pl.CostEstimate(
             flops=4 * span * LANES * TOPB * BLOCK,
             bytes_accessed=7 << 20,
             transcendentals=span * GROUPS * TOPB * BLOCK,
         ),
-    )(ids, gate_bias, qkv, all_keys, all_values, local_out)
+    )(starts, gate_bias, qkv, local_out, *chunks)
     back = lax.all_to_all(
         mixed.reshape(members, tokens, LANES), "ctx", split_axis=0, concat_axis=0, tiled=True
     )

time: 220 us -> 110 us (0.50)
  waiting for transfers between devices: 133 us -> 14.2 us
  starting transfers between devices: 10.4 us -> 36.4 us
  between operations: 13.4 us -> 0.26 us
  local copies, waits for them, and re-layouts: 6.82 us -> 2.87 us
    all_gather x2 -> x0, waiting for transfers between devices: 133 us -> none  [the longest x1 83.6 us: body(): all_values = lax.all_gather(own_values, 'mem', axis=0, tiled=True)]
    ppermute x0 -> x8, starting transfers between devices: none -> 31.2 us  [shifted(): return lax.ppermute(value, BOTH, pairs)]
    all_to_all x0 -> x1, blocking collectives: none -> 19.7 us  [gathered(): lax.all_to_all(spread, BOTH, split_axis=0, concat_axis=0, tiled=True, axi...]
    all_gather x1 -> x0, blocking collectives: 18.5 us -> none  [body(): ids = lax.all_gather(block_ids, 'ctx', axis=0, tiled=True)]
    all_to_all x1, waiting for transfers between devices: 0.01 us -> 7.92 us  [body(): qkv = lax.all_to_all(packed, 'ctx', split_axis=0, concat_axis=0, tiled=True)]
    ppermute x0 -> x8, waiting for transfers between devices: none -> 6.23 us  [shifted(): return lax.ppermute(value, BOTH, pairs)]
    all_to_all x1, starting transfers between devices: 10.3 us -> 5.19 us  [body(): qkv = lax.all_to_all(packed, 'ctx', split_axis=0, concat_axis=0, tiled=True)]
    all_to_all x1, blocking collectives: 18.2 us -> 15.8 us  [body(): lax.all_to_all(mixed.reshape(members, tokens, LANES), 'ctx', split_axis=0...]
  transfers between devices with their start and end apart: 3 -> 9, of which waited for: 2 -> 3; matrix products, arithmetic and copies ran while one was open for 2% -> 2% of each run, Pallas kernels for 2% -> 3%
where the time goes in v2:
time: 110 us
  starting transfers between devices  36.4 us (33%)
  blocking collectives  35.5 us (32%)
  Pallas kernels  18.6 us (17%)
  waiting for transfers between devices  14.2 us (13%)
  local copies, waits for them, and re-layouts  2.87 us (3%)
  other arithmetic  1.87 us (2%)
    ppermute x8, starting transfers between devices, shifted(): return lax.ppermute(value, BOTH, pairs)  31.2 us
    all_to_all x1, blocking collectives, gathered(): lax.all_to_all(spread, BOTH, split_axis=0, concat_axis=0, tiled=True, axi...  19.7 us
    all_to_all x1, blocking collectives, body(): lax.all_to_all(mixed.reshape(members, tokens, LANES), 'ctx', split_axis=0...  15.8 us
    pallas_call x1, Pallas kernels, body(): pl.pallas_call(memory_kernel, out_shape=jax.ShapeDtypeStruct((span, LANES...  14.9 us
    all_to_all x1, waiting for transfers between devices, body(): qkv = lax.all_to_all(packed, 'ctx', split_axis=0, concat_axis=0, tiled=True)  7.92 us
    ppermute x8, waiting for transfers between devices, shifted(): return lax.ppermute(value, BOTH, pairs)  6.23 us
    all_to_all x1, starting transfers between devices, body(): qkv = lax.all_to_all(packed, 'ctx', split_axis=0, concat_axis=0, tiled=True)  5.19 us
    pallas_call x1, Pallas kernels, body(): pl.pallas_call(local_kernel, out_shape=jax.ShapeDtypeStruct((span, LANES)...  3.74 us
  transfers between devices with their start and end apart: 9, of which 3 were waited for; matrix products, arithmetic and copies ran while one was open for 2% of the time, Pallas kernels for 3%

profile of v2, /device:TPU:1, one launch (start us, length us, event | category | flops | bytes accessed | tf_op | source)
XLA Modules:
  0.0 109.8 jit_solution(13054724923386665765)
XLA Ops:
  0.0 0.8 constant_dynamic-slice_fusion
  0.9 19.7 %all_to_all.15 = bf16[8,128,256]{2,1,0:T(8,128)(2,1)S(1)} all-to-all(bf16[8,128,256]{2,1,0:T(8,128)(2,1)S(1)} %broadcast_in_dim.5), channel_id=1, replica_groups={{0,64,128,192,256,320,384,448},{8,72,136,200,264,328,392,456},{16,80,14..., dimensions={0} | all-to-all | bytes 1048576 | tf_op jit(solution)/shard_map/all_to_all | solution.py:141
  20.7 10.7 %collective-permute-start.4 = (bf16[1024,256]{1,0:T(8,128)(2,1)S(1)}, bf16[1024,256]{1,0:T(8,128)(2,1)S(1)}, u32[]{:S(2)}, u32[]{:S(2)}) collective-permute-start(bf16[1024,256]{1,0:T(8,128)(2,1)S(1)} %bitcast.27), channel_id=1, source_target_pairs={{0,56},{1,449},{2,58},{3,451},{4,60},{5,453},{6,62},{7,455},{8,0},... | collective-permute-start | bytes 1572872 | tf_op jit(solution)/shard_map/ppermute | solution.py:135
  31.3 1.9 %collective-permute-start = (bf16[1024,256]{1,0:T(8,128)(2,1)S(1)}, bf16[1024,256]{1,0:T(8,128)(2,1)S(1)}, u32[]{:S(2)}, u32[]{:S(2)}) collective-permute-start(bf16[1024,256]{1,0:T(8,128)(2,1)S(1)} %bitcast.28), channel_id=1, source_target_pairs={{0,8},{1,65},{2,10},{3,67},{4,12},{5,69},{6,14},{7,71},{8,16},{9,7... | collective-permute-start | bytes 1572872 | tf_op jit(solution)/shard_map/ppermute | solution.py:135
  33.3 0.1 convert_element_type.19
  33.5 3.9 %collective-permute-done.4.refs_8_ = bf16[1024,256]{1,0:T(8,128)(2,1)S(1)} collective-permute-done((bf16[1024,256]{1,0:T(8,128)(2,1)S(1)}, bf16[1024,256]{1,0:T(8,128)(2,1)S(1)}, u32[]{:S(2)}, u32[]{:S(2)}) %collective-permute-start.4) | collective-permute-done | bytes 524320 | tf_op jit(solution)/shard_map/ppermute | solution.py:135
  37.4 5.3 %collective-permute-start.5 = (bf16[1024,256]{1,0:T(8,128)(2,1)S(1)}, bf16[1024,256]{1,0:T(8,128)(2,1)}, u32[]{:S(2)}, u32[]{:S(2)}) collective-permute-start(bf16[1024,256]{1,0:T(8,128)(2,1)S(1)} %collective-permute-done.4.refs_8_), channel_id=1, source_target_pairs={{0,56},{1,449},{2,58},{3,451},{4,60},{5,453},{6,62},{7,455},{8,0},... | collective-permute-start | bytes 1572872 | tf_op jit(solution)/shard_map/ppermute | solution.py:135
  42.8 1.9 %collective-permute-start.1 = (bf16[1024,256]{1,0:T(8,128)(2,1)S(1)}, bf16[1024,256]{1,0:T(8,128)(2,1)}, u32[]{:S(2)}, u32[]{:S(2)}) collective-permute-start(bf16[1024,256]{1,0:T(8,128)(2,1)S(1)} %collective-permute-done.refs_1_), channel_id=1, source_target_pairs={{0,8},{1,65},{2,10},{3,67},{4,12},{5,69},{6,14},{7,71},{8,16},{9,7... | collective-permute-start | bytes 1572872 | tf_op jit(solution)/shard_map/ppermute | solution.py:135
  44.7 0.1 broadcast_in_dim.4
  44.8 1.1 maximum_bitcast_fusion
  45.9 5.2 %all-to-all-start = ((bf16[8,64,896]{2,1,0:T(8,128)(2,1)}), bf16[8,64,896]{2,1,0:T(8,128)(2,1)S(1)}, u32[]{:S(2)}, u32[]{:S(2)}) async-start(bf16[8,64,896]{2,1,0:T(8,128)(2,1)} %maximum_bitcast_fusion), calls=%async_computation | async-start | bytes 1835008 | tf_op jit(solution)/shard_map/all_to_all | solution.py:193
  51.0 3.8 %collective-permute-start.6 = (bf16[1024,256]{1,0:T(8,128)(2,1)}, bf16[1024,256]{1,0:T(8,128)(2,1)S(1)}, u32[]{:S(2)}, u32[]{:S(2)}) collective-permute-start(bf16[1024,256]{1,0:T(8,128)(2,1)} %collective-permute-done.5.refs_7_), channel_id=1, source_target_pairs={{0,56},{1,449},{2,58},{3,451},{4,60},{5,453},{6,62},{7,455},{8,0},... | collective-permute-start | bytes 1572872 | tf_op jit(solution)/shard_map/ppermute | solution.py:135
  54.9 1.9 %collective-permute-start.2 = (bf16[1024,256]{1,0:T(8,128)(2,1)}, bf16[1024,256]{1,0:T(8,128)(2,1)S(1)}, u32[]{:S(2)}, u32[]{:S(2)}) collective-permute-start(bf16[1024,256]{1,0:T(8,128)(2,1)} %collective-permute-done.1.refs_2_), channel_id=1, source_target_pairs={{0,8},{1,65},{2,10},{3,67},{4,12},{5,69},{6,14},{7,71},{8,16},{9,7... | collective-permute-start | bytes 1572872 | tf_op jit(solution)/shard_map/ppermute | solution.py:135
  56.8 7.9 %all-to-all-done = bf16[8,64,896]{2,1,0:T(8,128)(2,1)S(1)} async-done(((bf16[8,64,896]{2,1,0:T(8,128)(2,1)}), bf16[8,64,896]{2,1,0:T(8,128)(2,1)S(1)}, u32[]{:S(2)}, u32[]{:S(2)}) %all-to-all-start) | async-done | bytes 917536 | tf_op jit(solution)/shard_map/all_to_all | solution.py:193
  64.7 0.1 convert_reduce_fusion
  65.0 3.8 %collective-permute-start.7 = (bf16[512,256]{1,0:T(8,128)(2,1)S(1)}, bf16[512,256]{1,0:T(8,128)(2,1)S(1)}, u32[]{:S(2)}, u32[]{:S(2)}) collective-permute-start(bf16[512,256]{1,0:T(8,128)(2,1)S(1)} %slice.14), channel_id=1, source_target_pairs={{0,56},{1,449},{2,58},{3,451},{4,60},{5,453},{6,62},{7,455},{8,0},... | collective-permute-start | bytes 786440 | tf_op jit(solution)/shard_map/ppermute | solution.py:135
  68.9 1.9 %collective-permute-start.3 = (bf16[512,256]{1,0:T(8,128)(2,1)S(1)}, bf16[512,256]{1,0:T(8,128)(2,1)S(1)}, u32[]{:S(2)}, u32[]{:S(2)}) collective-permute-start(bf16[512,256]{1,0:T(8,128)(2,1)S(1)} %slice.13), channel_id=1, source_target_pairs={{0,8},{1,65},{2,10},{3,67},{4,12},{5,69},{6,14},{7,71},{8,16},{9,7... | collective-permute-start | bytes 786440 | tf_op jit(solution)/shard_map/ppermute | solution.py:135
  70.8 3.7 %shard_map.73.local_ref = f32[512,512]{1,0:T(8,128)} custom-call(bf16[512,896]{1,0:T(8,128)(2,1)} %bitcast.23), custom_call_target="tpu_custom_call" | custom-call | flops 536870912 | bytes 2097152 | tf_op jit(solution)/shard_map/pallas_call | solution.py:200
  74.6 0.7 fusion.4.starts_ref
  75.2 2.3 %collective-permute-done.3.refs_4_ = bf16[512,256]{1,0:T(8,128)(2,1)S(1)} collective-permute-done((bf16[512,256]{1,0:T(8,128)(2,1)S(1)}, bf16[512,256]{1,0:T(8,128)(2,1)S(1)}, u32[]{:S(2)}, u32[]{:S(2)}) %collective-permute-start.3) | collective-permute-done | bytes 262176 | tf_op jit(solution)/shard_map/ppermute | solution.py:135
  77.5 0.7 copy-done.9
  78.2 14.9 %shard_map.74 = bf16[512,512]{1,0:T(8,128)(2,1)} custom-call(s32[32,16]{1,0:T(8,128)} %fusion.4.starts_ref, f32[32]{0:T(128)} %bias_ref.1, bf16[512,896]{1,0:T(8,128)(2,1)} %bitcast.24, f32[512,512]{1,0:T(8,128)} %shard_map.73.local_ref, bf16[1024,256]{1,0:T(8,128)(2,1)} %bitcast.29, bf16[1024,256]{1,0:T(8,128)(2,1)} %copy-done.7, ...), custom_call_target="tpu_custom_call" | custom-call | flops 536870912 | bytes 7340032 | tf_op jit(solution)/shard_map/pallas_call | solution.py:209
  93.1 15.8 %all_to_all.16 = bf16[8,64,512]{2,1,0:T(8,128)(2,1)S(1)} all-to-all(bf16[8,64,512]{2,1,0:T(8,128)(2,1)} %bitcast.30), channel_id=1, replica_groups=mesh['mem'=64,'ctx'=8] {'ctx'}, dimensions={0} | all-to-all | bytes 1048576 | tf_op jit(solution)/shard_map/all_to_all | solution.py:224
  108.9 0.8 copy.19
  (37 shorter events, 0.3 us)
Async XLA Ops:
  0.0 33.4 %copy-start = (bf16[64,1024]{1,0:T(8,128)(2,1)S(1)}, bf16[64,1024]{1,0:T(8,128)(2,1)}, u32[]{:S(2)}) copy-start(bf16[64,1024]{1,0:T(8,128)(2,1)} %param.8) | copy-start | bytes 393220
  0.0 33.2 %copy-start.11 = (s32[4,16]{1,0:T(4,128)S(1)}, s32[4,16]{1,0:T(4,128)}, u32[]{:S(2)}) copy-start(s32[4,16]{1,0:T(4,128)} %param.12) | copy-start | bytes 772
  0.0 33.4 %copy-start.5 = (bf16[64,4096]{1,0:T(8,128)(2,1)S(1)}, bf16[64,4096]{1,0:T(8,128)(2,1)}, u32[]{:S(2)}) copy-start(bf16[64,4096]{1,0:T(8,128)(2,1)} %param.7) | copy-start | bytes 1572868
  0.9 32.5 %copy-start.10 = (bf16[64,1024]{1,0:T(8,128)(2,1)S(1)}, bf16[64,1024]{1,0:T(8,128)(2,1)}, u32[]{:S(2)}) copy-start(bf16[64,1024]{1,0:T(8,128)(2,1)} %param.9) | copy-start | bytes 393220
  20.7 25.2 %copy-start.2 = (bf16[8,128,256]{2,1,0:T(8,128)(2,1)}, bf16[8,128,256]{2,1,0:T(8,128)(2,1)S(1)}, u32[]{:S(2)}) copy-start(bf16[8,128,256]{2,1,0:T(8,128)(2,1)S(1)} %all_to_all.15) | copy-start | bytes 1572868
  20.7 16.8 %collective-permute-start.4 = (bf16[1024,256]{1,0:T(8,128)(2,1)S(1)}, bf16[1024,256]{1,0:T(8,128)(2,1)S(1)}, u32[]{:S(2)}, u32[]{:S(2)}) collective-permute-start(bf16[1024,256]{1,0:T(8,128)(2,1)S(1)} %bitcast.27), channel_id=1, source_target_pairs={{0,56},{1,449},{2,58},{3,451},{4,60},{5,453},{6,62},{7,455},{8,0},... | collective-permute-start | bytes 1572872 | tf_op jit(solution)/shard_map/ppermute | solution.py:135
  31.3 11.4 %collective-permute-start = (bf16[1024,256]{1,0:T(8,128)(2,1)S(1)}, bf16[1024,256]{1,0:T(8,128)(2,1)S(1)}, u32[]{:S(2)}, u32[]{:S(2)}) collective-permute-start(bf16[1024,256]{1,0:T(8,128)(2,1)S(1)} %bitcast.28), channel_id=1, source_target_pairs={{0,8},{1,65},{2,10},{3,67},{4,12},{5,69},{6,14},{7,71},{8,16},{9,7... | collective-permute-start | bytes 1572872 | tf_op jit(solution)/shard_map/ppermute | solution.py:135
  37.4 8.4 %copy-start.6 = (bf16[1024,256]{1,0:T(8,128)(2,1)}, bf16[1024,256]{1,0:T(8,128)(2,1)S(1)}, u32[]{:S(2)}) copy-start(bf16[1024,256]{1,0:T(8,128)(2,1)S(1)} %collective-permute-done.4.refs_8_) | copy-start | bytes 1572868
  37.4 13.6 %collective-permute-start.5 = (bf16[1024,256]{1,0:T(8,128)(2,1)S(1)}, bf16[1024,256]{1,0:T(8,128)(2,1)}, u32[]{:S(2)}, u32[]{:S(2)}) collective-permute-start(bf16[1024,256]{1,0:T(8,128)(2,1)S(1)} %collective-permute-done.4.refs_8_), channel_id=1, source_target_pairs={{0,56},{1,449},{2,58},{3,451},{4,60},{5,453},{6,62},{7,455},{8,0},... | collective-permute-start | bytes 1572872 | tf_op jit(solution)/shard_map/ppermute | solution.py:135
  42.8 3.1 %copy-start.7 = (bf16[1024,256]{1,0:T(8,128)(2,1)}, bf16[1024,256]{1,0:T(8,128)(2,1)S(1)}, u32[]{:S(2)}) copy-start(bf16[1024,256]{1,0:T(8,128)(2,1)S(1)} %collective-permute-done.refs_1_) | copy-start | bytes 1572868
  42.8 12.1 %collective-permute-start.1 = (bf16[1024,256]{1,0:T(8,128)(2,1)S(1)}, bf16[1024,256]{1,0:T(8,128)(2,1)}, u32[]{:S(2)}, u32[]{:S(2)}) collective-permute-start(bf16[1024,256]{1,0:T(8,128)(2,1)S(1)} %collective-permute-done.refs_1_), channel_id=1, source_target_pairs={{0,8},{1,65},{2,10},{3,67},{4,12},{5,69},{6,14},{7,71},{8,16},{9,7... | collective-permute-start | bytes 1572872 | tf_op jit(solution)/shard_map/ppermute | solution.py:135
  45.9 18.9 %all-to-all-start = ((bf16[8,64,896]{2,1,0:T(8,128)(2,1)}), bf16[8,64,896]{2,1,0:T(8,128)(2,1)S(1)}, u32[]{:S(2)}, u32[]{:S(2)}) async-start(bf16[8,64,896]{2,1,0:T(8,128)(2,1)} %maximum_bitcast_fusion), calls=%async_computation | async-start | bytes 1835008 | tf_op jit(solution)/shard_map/all_to_all | solution.py:193
  51.0 13.9 %collective-permute-start.6 = (bf16[1024,256]{1,0:T(8,128)(2,1)}, bf16[1024,256]{1,0:T(8,128)(2,1)S(1)}, u32[]{:S(2)}, u32[]{:S(2)}) collective-permute-start(bf16[1024,256]{1,0:T(8,128)(2,1)} %collective-permute-done.5.refs_7_), channel_id=1, source_target_pairs={{0,56},{1,449},{2,58},{3,451},{4,60},{5,453},{6,62},{7,455},{8,0},... | collective-permute-start | bytes 1572872 | tf_op jit(solution)/shard_map/ppermute | solution.py:135
  54.9 14.0 %collective-permute-start.2 = (bf16[1024,256]{1,0:T(8,128)(2,1)}, bf16[1024,256]{1,0:T(8,128)(2,1)S(1)}, u32[]{:S(2)}, u32[]{:S(2)}) collective-permute-start(bf16[1024,256]{1,0:T(8,128)(2,1)} %collective-permute-done.1.refs_2_), channel_id=1, source_target_pairs={{0,8},{1,65},{2,10},{3,67},{4,12},{5,69},{6,14},{7,71},{8,16},{9,7... | collective-permute-start | bytes 1572872 | tf_op jit(solution)/shard_map/ppermute | solution.py:135
  64.7 6.1 %copy-start.1 = (bf16[8,64,896]{2,1,0:T(8,128)(2,1)}, bf16[8,64,896]{2,1,0:T(8,128)(2,1)S(1)}, u32[]{:S(2)}) copy-start(bf16[8,64,896]{2,1,0:T(8,128)(2,1)S(1)} %all-to-all-done) | copy-start | bytes 2752516
  65.0 9.6 %copy-start.3 = (bf16[1024,256]{1,0:T(8,128)(2,1)}, bf16[1024,256]{1,0:T(8,128)(2,1)S(1)}, u32[]{:S(2)}) copy-start(bf16[1024,256]{1,0:T(8,128)(2,1)S(1)} %collective-permute-done.6.refs_6_) | copy-start | bytes 1572868
  65.0 10.2 %collective-permute-start.7 = (bf16[512,256]{1,0:T(8,128)(2,1)S(1)}, bf16[512,256]{1,0:T(8,128)(2,1)S(1)}, u32[]{:S(2)}, u32[]{:S(2)}) collective-permute-start(bf16[512,256]{1,0:T(8,128)(2,1)S(1)} %slice.14), channel_id=1, source_target_pairs={{0,56},{1,449},{2,58},{3,451},{4,60},{5,453},{6,62},{7,455},{8,0},... | collective-permute-start | bytes 786440 | tf_op jit(solution)/shard_map/ppermute | solution.py:135
  68.8 5.7 %copy-start.4 = (bf16[1024,256]{1,0:T(8,128)(2,1)}, bf16[1024,256]{1,0:T(8,128)(2,1)S(1)}, u32[]{:S(2)}) copy-start(bf16[1024,256]{1,0:T(8,128)(2,1)S(1)} %collective-permute-done.2.refs_3_) | copy-start | bytes 1572868
  68.9 8.6 %collective-permute-start.3 = (bf16[512,256]{1,0:T(8,128)(2,1)S(1)}, bf16[512,256]{1,0:T(8,128)(2,1)S(1)}, u32[]{:S(2)}, u32[]{:S(2)}) collective-permute-start(bf16[512,256]{1,0:T(8,128)(2,1)S(1)} %slice.13), channel_id=1, source_target_pairs={{0,8},{1,65},{2,10},{3,67},{4,12},{5,69},{6,14},{7,71},{8,16},{9,7... | collective-permute-start | bytes 786440 | tf_op jit(solution)/shard_map/ppermute | solution.py:135
  75.2 2.3 %copy-start.8 = (bf16[512,256]{1,0:T(8,128)(2,1)}, bf16[512,256]{1,0:T(8,128)(2,1)S(1)}, u32[]{:S(2)}) copy-start(bf16[512,256]{1,0:T(8,128)(2,1)S(1)} %collective-permute-done.7.refs_5_) | copy-start | bytes 786436
  77.5 0.7 copy-start.9

commit v3 on v2

--- a/solution.py
+++ b/solution.py
@@ -18,6 +18,7 @@
 EXP2_SCALE = HEAD_DIM ** (-0.5) * 1.4426950408889634
 NEG = -1e30
 TILE = 128
+TOGETHER = 8
 
 
 def product(left, right, contract_right):
@@ -36,6 +37,30 @@
     return jnp.concatenate(
         [rows[:, h * HEAD_DIM : (h + 1) * HEAD_DIM] for h in range(GROUPS)], axis=0
     )
+
+
+def pack_kernel(
+    ids_ref, queries_ref, keys_ref, values_ref, mem_keys_ref, mem_values_ref, out_ref, own_ref, id_ref
+):
+    for block in range(ids_ref.shape[0]):
+        for j in range(TOPB):
+            value = ids_ref[block, j].astype(jnp.float32)
+            id_ref[block * TOPB + j : block * TOPB + j + 1, :] = jnp.full(
+                (1, HEAD_DIM), value, jnp.float32
+            )
+    id_lanes = id_ref[...].astype(jnp.bfloat16)
+    for head in range(KV_HEADS):
+        here = slice(head * HEAD_DIM, (head + 1) * HEAD_DIM)
+        out_ref[head, :, :LANES] = queries_ref[:, head * LANES : (head + 1) * LANES]
+        out_ref[head, :, LANES : LANES + HEAD_DIM] = keys_ref[:, here]
+        out_ref[head, :, LANES + HEAD_DIM : LANES + 2 * HEAD_DIM] = values_ref[:, here]
+        out_ref[head, :, LANES + 2 * HEAD_DIM :] = id_lanes
+    start = pl.multiple_of(lax.axis_index("ctx") * HEAD_DIM, HEAD_DIM)
+    keys = mem_keys_ref[:, pl.ds(start, HEAD_DIM)]
+    values = mem_values_ref[:, pl.ds(start, HEAD_DIM)]
+    for place in range(own_ref.shape[0]):
+        own_ref[place, :, :HEAD_DIM] = keys
+        own_ref[place, :, HEAD_DIM:] = values
 
 
 def local_kernel(qkv_ref, out_ref):
@@ -55,6 +80,10 @@
             out_ref[lo:hi, h * HEAD_DIM : (h + 1) * HEAD_DIM] = summed[
                 h * TILE : (h + 1) * TILE
             ]
+
+
+def picked(store_ref, rows, lanes):
+    return jnp.concatenate([store_ref[pl.ds(row, BLOCK), lanes] for row in rows], axis=0)
 
 
 def memory_kernel(starts_ref, bias_ref, qkv_ref, local_ref, *refs):
@@ -76,26 +105,37 @@
     for copy in copies:
         copy.wait()
 
-    def one_block(index, carry):
-        lo = pl.multiple_of(index * QBLOCK, QBLOCK)
-        query = heads_to_rows(qkv_ref[pl.ds(lo, QBLOCK), :LANES])
-        starts = [pl.multiple_of(starts_ref[index, j], BLOCK) for j in range(TOPB)]
-        keys = jnp.concatenate(
-            [store_ref[pl.ds(s, BLOCK), :HEAD_DIM] for s in starts], axis=0
-        )
-        values = jnp.concatenate(
-            [store_ref[pl.ds(s, BLOCK), HEAD_DIM:] for s in starts], axis=0
-        )
-        weights, total = softmax_parts(product(query, keys, 1))
-        summed = product(weights.astype(jnp.bfloat16), values, 0) / total
-        for h in range(GROUPS):
-            lanes = slice(h * HEAD_DIM, (h + 1) * HEAD_DIM)
-            local_out = local_ref[pl.ds(lo, QBLOCK), lanes]
-            mixed = gates[h] * summed[h * QBLOCK : (h + 1) * QBLOCK] + (1.0 - gates[h]) * local_out
-            out_ref[pl.ds(lo, QBLOCK), lanes] = mixed.astype(jnp.bfloat16)
+    def some_blocks(step, carry):
+        indices = [step * TOGETHER + k for k in range(TOGETHER)]
+        places = [pl.multiple_of(index * QBLOCK, QBLOCK) for index in indices]
+        starts = [
+            [pl.multiple_of(starts_ref[index, j], BLOCK) for j in range(TOPB)] for index in indices
+        ]
+        scores = []
+        for lo, rows in zip(places, starts):
+            query = heads_to_rows(qkv_ref[pl.ds(lo, QBLOCK), :LANES])
+            scores.append(product(query, picked(store_ref, rows, slice(0, HEAD_DIM)), 1))
+        tops = [jnp.max(score, axis=-1, keepdims=True) for score in scores]
+        weights = [jnp.exp2((score - top) * EXP2_SCALE) for score, top in zip(scores, tops)]
+        totals = [jnp.sum(weight, axis=-1, keepdims=True) for weight in weights]
+        summed = [
+            product(
+                weight.astype(jnp.bfloat16),
+                picked(store_ref, rows, slice(HEAD_DIM, 2 * HEAD_DIM)),
+                0,
+            )
+            for weight, rows in zip(weights, starts)
+        ]
+        for lo, total, value in zip(places, totals, summed):
+            for h in range(GROUPS):
+                lanes = slice(h * HEAD_DIM, (h + 1) * HEAD_DIM)
+                rows = slice(h * QBLOCK, (h + 1) * QBLOCK)
+                memory_out = value[rows] * (gates[h] / total[rows])
+                mixed = memory_out + (1.0 - gates[h]) * local_ref[pl.ds(lo, QBLOCK), lanes]
+                out_ref[pl.ds(lo, QBLOCK), lanes] = mixed.astype(jnp.bfloat16)
         return carry
 
-    lax.fori_loop(0, query_blocks, one_block, 0, unroll=2)
+    lax.fori_loop(0, query_blocks // TOGETHER, some_blocks, 0)
 
 
 BOTH = ("mem", "ctx")
@@ -135,20 +175,13 @@
     return lax.ppermute(value, BOTH, pairs)
 
 
-def gathered(own):
-    rows = own.shape[0]
-    spread = jnp.broadcast_to(own[None], (SIDE,) + own.shape)
-    chunk = lax.all_to_all(
-        spread, BOTH, split_axis=0, concat_axis=0, tiled=True, axis_index_groups=first_groups()
-    ).reshape(SIDE * rows, own.shape[1])
-    ahead, behind = [chunk], [chunk]
-    for _ in range(SIDE // 2 - 1):
-        ahead.append(shifted(ahead[-1], 1))
-        behind.append(shifted(behind[-1], -1))
+def gathered(chunk):
     half = chunk.shape[0] // 2
-    last_ahead = shifted(ahead[-1][:half], 1)
-    last_behind = shifted(behind[-1][half:], -1)
-    return ahead + [last_ahead, last_behind] + behind[:0:-1]
+    ahead2, behind2 = shifted(chunk, 2), shifted(chunk, -2)
+    ahead1, behind1 = shifted(chunk, 1), shifted(chunk, -1)
+    ahead3, behind3 = shifted(ahead2, 1), shifted(behind2, -1)
+    ahead4, behind4 = shifted(ahead2[:half], 2), shifted(behind2[half:], -2)
+    return [chunk, ahead1, ahead2, ahead3, ahead4, behind4, behind3, behind2, behind1]
 
 
 def block_rows(ids, held, rows):
@@ -165,38 +198,30 @@
 def body(queries, local_keys, local_values, mem_keys, mem_values, block_ids, gate_bias):
     tokens = queries.shape[0]
     members = lax.axis_size("ctx")
-    head = lax.axis_index("ctx")
     span = tokens * members
     rows = mem_keys.shape[0]
-    start = head * HEAD_DIM
-    own = jnp.concatenate(
-        [
-            lax.dynamic_slice_in_dim(mem_keys, start, HEAD_DIM, 1),
-            lax.dynamic_slice_in_dim(mem_values, start, HEAD_DIM, 1),
-        ],
-        axis=1,
-    )
-    chunks = gathered(own)
-    id_lanes = jnp.broadcast_to(
-        block_ids.reshape(tokens, 1, 1).astype(jnp.bfloat16), (tokens, members, HEAD_DIM)
-    )
-    packed = jnp.concatenate(
-        [
-            queries.reshape(tokens, members, LANES),
-            local_keys.reshape(tokens, members, HEAD_DIM),
-            local_values.reshape(tokens, members, HEAD_DIM),
-            id_lanes,
-        ],
-        axis=2,
-    )
-    packed = jnp.transpose(packed, (1, 0, 2))
-    qkv = lax.all_to_all(packed, "ctx", split_axis=0, concat_axis=0, tiled=True)
-    qkv = qkv.reshape(span, LANES + 3 * HEAD_DIM)
-    ids = qkv[:, LANES + 2 * HEAD_DIM].astype(jnp.int32).reshape(span // QBLOCK, TOPB)
-    starts = block_rows(ids, rows // BLOCK, rows)
     vmem = pl.BlockSpec(memory_space=pltpu.VMEM)
     smem = pl.BlockSpec(memory_space=pltpu.SMEM)
     hbm = pl.BlockSpec(memory_space=pl.ANY)
+    packed, spread = pl.pallas_call(
+        pack_kernel,
+        out_shape=(
+            jax.ShapeDtypeStruct((members, tokens, LANES + 3 * HEAD_DIM), jnp.bfloat16),
+            jax.ShapeDtypeStruct((SIDE, rows, 2 * HEAD_DIM), jnp.bfloat16),
+        ),
+        in_specs=[smem] + [vmem] * 5,
+        out_specs=(vmem, vmem),
+        scratch_shapes=[pltpu.VMEM((tokens, HEAD_DIM), jnp.float32)],
+        cost_estimate=pl.CostEstimate(flops=0, bytes_accessed=4 << 20, transcendentals=0),
+    )(block_ids, queries, local_keys, local_values, mem_keys, mem_values)
+    qkv = lax.all_to_all(packed, "ctx", split_axis=0, concat_axis=0, tiled=True)
+    qkv = qkv.reshape(span, LANES + 3 * HEAD_DIM)
+    chunk = lax.all_to_all(
+        spread, BOTH, split_axis=0, concat_axis=0, tiled=True, axis_index_groups=first_groups()
+    ).reshape(SIDE * rows, 2 * HEAD_DIM)
+    chunks = gathered(chunk)
+    ids = qkv[:, LANES + 2 * HEAD_DIM].astype(jnp.int32).reshape(span // QBLOCK, TOPB)
+    starts = block_rows(ids, rows // BLOCK, rows)
     local_out = pl.pallas_call(
         local_kernel,
         out_shape=jax.ShapeDtypeStruct((span, LANES), jnp.float32),

time: 110 us -> 102 us (0.927)
  waiting for transfers between devices: 14.2 us -> 8.32 us
  Pallas kernels: 18.6 us -> 13.8 us
  starting transfers between devices: 36.4 us -> 38.2 us
    all_to_all x1, waiting for transfers between devices: 7.92 us -> 0.01 us  [body(): qkv = lax.all_to_all(packed, 'ctx', split_axis=0, concat_axis=0, tiled=True)]
    pallas_call x1, Pallas kernels: 14.9 us -> 7.55 us  [body(): pl.pallas_call(memory_kernel, out_shape=jax.ShapeDtypeStruct((span, LANES...]
    all_to_all x1, starting transfers between devices: 5.19 us -> 9.61 us  [body(): qkv = lax.all_to_all(packed, 'ctx', split_axis=0, concat_axis=0, tiled=True)]
    ppermute x8, starting transfers between devices: 31.2 us -> 28.6 us  [shifted(): return lax.ppermute(value, BOTH, pairs)]
    pallas_call x0 -> x1, Pallas kernels: none -> 2.52 us  [body(): pl.pallas_call(pack_kernel, out_shape=(jax.ShapeDtypeStruct((members, tok...]
    ppermute x8, waiting for transfers between devices: 6.23 us -> 8.32 us  [shifted(): return lax.ppermute(value, BOTH, pairs)]
    slice x2, local copies, waits for them, and re-layouts: 0.04 us -> 1.46 us  [gathered(): ahead4, behind4 = (shifted(ahead2[:half], 2), shifted(behind2[half:], -2))]
  transfers between devices with their start and end apart: 9 -> 9, of which waited for: 3 -> 3; matrix products, arithmetic and copies ran while one was open for 2% -> 4% of each run, Pallas kernels for 3% -> 4%
where the time goes in v3:
time: 102 us; the launch traced here: 101 us
  starting transfers between devices  38.2 us (37%)
  blocking collectives  35.8 us (35%)
  Pallas kernels  13.8 us (14%)
  waiting for transfers between devices  8.32 us (8%)
  local copies, waits for them, and re-layouts  3.07 us (3%)
  other arithmetic  1.5 us (1%)
    ppermute x8, starting transfers between devices, shifted(): return lax.ppermute(value, BOTH, pairs)  28.6 us
    all_to_all x1, blocking collectives, body(): lax.all_to_all(spread, BOTH, split_axis=0, concat_axis=0, tiled=True, axi...  19.8 us
    all_to_all x1, blocking collectives, body(): lax.all_to_all(mixed.reshape(members, tokens, LANES), 'ctx', split_axis=0...  16 us
    all_to_all x1, starting transfers between devices, body(): qkv = lax.all_to_all(packed, 'ctx', split_axis=0, concat_axis=0, tiled=True)  9.61 us
    ppermute x8, waiting for transfers between devices, shifted(): return lax.ppermute(value, BOTH, pairs)  8.32 us
    pallas_call x1, Pallas kernels, body(): pl.pallas_call(memory_kernel, out_shape=jax.ShapeDtypeStruct((span, LANES...  7.55 us
    pallas_call x1, Pallas kernels, body(): pl.pallas_call(local_kernel, out_shape=jax.ShapeDtypeStruct((span, LANES)...  3.74 us
    pallas_call x1, Pallas kernels, body(): pl.pallas_call(pack_kernel, out_shape=(jax.ShapeDtypeStruct((members, tok...  2.52 us
  transfers between devices with their start and end apart: 9, of which 3 were waited for; matrix products, arithmetic and copies ran while one was open for 4% of the time, Pallas kernels for 4%

profile of v3, /device:TPU:1, one launch (start us, length us, event | category | flops | bytes accessed | tf_op | source)
XLA Modules:
  0.0 100.8 jit_solution(18219547118292380737)
XLA Ops:
  0.0 2.5 %shard_map.73 = (bf16[8,64,896]{2,1,0:T(8,128)(2,1)}, bf16[8,128,256]{2,1,0:T(8,128)(2,1)}) custom-call(s32[4,16]{1,0:T(4,128)} %ids_ref.1, bf16[64,4096]{1,0:T(8,128)(2,1)} %queries_ref.1, bf16[64,1024]{1,0:T(8,128)(2,1)} %keys_ref.1, bf16[64,1024]{1,0:T(8,128)(2,1)} %values_ref.1, bf16[128,1024]{1,0:T(8,128)(2,1)} %mem_keys_ref.1, ...), custom_call_target="tpu_custom_call" | custom-call | bytes 4194304 | tf_op jit(solution)/shard_map/pallas_call | solution.py:206
  2.5 19.8 %all_to_all.15 = bf16[8,128,256]{2,1,0:T(8,128)(2,1)S(1)} all-to-all(bf16[8,128,256]{2,1,0:T(8,128)(2,1)} %get-tuple-element.8), channel_id=1, replica_groups={{0,64,128,192,256,320,384,448},{8,72,136,200,264,328,392,456},{16,80,14..., dimensions={0} | all-to-all | bytes 1048576 | tf_op jit(solution)/shard_map/all_to_all | solution.py:219
  22.3 9.6 %all-to-all-start = ((bf16[8,64,896]{2,1,0:T(8,128)(2,1)}), bf16[8,64,896]{2,1,0:T(8,128)(2,1)S(1)}, u32[]{:S(2)}, u32[]{:S(2)}) async-start(bf16[8,64,896]{2,1,0:T(8,128)(2,1)} %get-tuple-element.7), calls=%async_computation | async-start | bytes 1835008 | tf_op jit(solution)/shard_map/all_to_all | solution.py:217
  31.9 5.4 %collective-permute-start.4 = (bf16[1024,256]{1,0:T(8,128)(2,1)S(1)}, bf16[1024,256]{1,0:T(8,128)(2,1)S(1)}, u32[]{:S(2)}, u32[]{:S(2)}) collective-permute-start(bf16[1024,256]{1,0:T(8,128)(2,1)S(1)} %bitcast.10), channel_id=1, source_target_pairs={{0,48},{1,385},{2,50},{3,387},{4,52},{5,389},{6,54},{7,391},{8,56}... | collective-permute-start | bytes 1572872 | tf_op jit(solution)/shard_map/ppermute | solution.py:175
  37.4 1.9 %collective-permute-start.1 = (bf16[1024,256]{1,0:T(8,128)(2,1)S(1)}, bf16[1024,256]{1,0:T(8,128)(2,1)S(1)}, u32[]{:S(2)}, u32[]{:S(2)}) collective-permute-start(bf16[1024,256]{1,0:T(8,128)(2,1)S(1)} %bitcast.11), channel_id=1, source_target_pairs={{0,16},{1,129},{2,18},{3,131},{4,20},{5,133},{6,22},{7,135},{8,24}... | collective-permute-start | bytes 1572872 | tf_op jit(solution)/shard_map/ppermute | solution.py:175
  39.3 5.5 %collective-permute-start.7 = (bf16[1024,256]{1,0:T(8,128)(2,1)S(1)}, bf16[1024,256]{1,0:T(8,128)(2,1)S(1)}, u32[]{:S(2)}, u32[]{:S(2)}) collective-permute-start(bf16[1024,256]{1,0:T(8,128)(2,1)S(1)} %bitcast.12), channel_id=1, source_target_pairs={{0,56},{1,449},{2,58},{3,451},{4,60},{5,453},{6,62},{7,455},{8,0},... | collective-permute-start | bytes 1572872 | tf_op jit(solution)/shard_map/ppermute | solution.py:175
  44.8 1.9 %collective-permute-start = (bf16[1024,256]{1,0:T(8,128)(2,1)S(1)}, bf16[1024,256]{1,0:T(8,128)(2,1)S(1)}, u32[]{:S(2)}, u32[]{:S(2)}) collective-permute-start(bf16[1024,256]{1,0:T(8,128)(2,1)S(1)} %bitcast.13), channel_id=1, source_target_pairs={{0,8},{1,65},{2,10},{3,67},{4,12},{5,69},{6,14},{7,71},{8,16},{9,7... | collective-permute-start | bytes 1572872 | tf_op jit(solution)/shard_map/ppermute | solution.py:175
  46.7 2.0 %collective-permute-done.4.refs_7_ = bf16[1024,256]{1,0:T(8,128)(2,1)S(1)} collective-permute-done((bf16[1024,256]{1,0:T(8,128)(2,1)S(1)}, bf16[1024,256]{1,0:T(8,128)(2,1)S(1)}, u32[]{:S(2)}, u32[]{:S(2)}) %collective-permute-start.4) | collective-permute-done | bytes 524320 | tf_op jit(solution)/shard_map/ppermute | solution.py:175
  48.7 5.6 %collective-permute-start.6 = (bf16[1024,256]{1,0:T(8,128)(2,1)S(1)}, bf16[1024,256]{1,0:T(8,128)(2,1)}, u32[]{:S(2)}, u32[]{:S(2)}) collective-permute-start(bf16[1024,256]{1,0:T(8,128)(2,1)S(1)} %collective-permute-done.4.refs_7_), channel_id=1, source_target_pairs={{0,56},{1,449},{2,58},{3,451},{4,60},{5,453},{6,62},{7,455},{8,0},... | collective-permute-start | bytes 1572872 | tf_op jit(solution)/shard_map/ppermute | solution.py:175
  54.3 0.8 collective-permute-done.1.refs_2_
  55.1 2.1 %collective-permute-start.2 = (bf16[1024,256]{1,0:T(8,128)(2,1)S(1)}, bf16[1024,256]{1,0:T(8,128)(2,1)}, u32[]{:S(2)}, u32[]{:S(2)}) collective-permute-start(bf16[1024,256]{1,0:T(8,128)(2,1)S(1)} %collective-permute-done.1.refs_2_), channel_id=1, source_target_pairs={{0,8},{1,65},{2,10},{3,67},{4,12},{5,69},{6,14},{7,71},{8,16},{9,7... | collective-permute-start | bytes 1572872 | tf_op jit(solution)/shard_map/ppermute | solution.py:175
  57.2 0.0 all-to-all-done
  57.2 0.8 convert_reduce_fusion
  58.0 0.7 reshape.20
  58.8 0.7 slice.14
  59.5 3.5 %collective-permute-start.5 = (bf16[512,256]{1,0:T(8,128)(2,1)}, bf16[512,256]{1,0:T(8,128)(2,1)}, u32[]{:S(2)}, u32[]{:S(2)}) collective-permute-start(bf16[512,256]{1,0:T(8,128)(2,1)} %slice.14), channel_id=1, source_target_pairs={{0,48},{1,385},{2,50},{3,387},{4,52},{5,389},{6,54},{7,391},{8,56}... | collective-permute-start | bytes 786440 | tf_op jit(solution)/shard_map/ppermute | solution.py:175
  63.0 0.7 slice.13
  63.8 2.7 %collective-permute-start.3 = (bf16[512,256]{1,0:T(8,128)(2,1)}, bf16[512,256]{1,0:T(8,128)(2,1)}, u32[]{:S(2)}, u32[]{:S(2)}) collective-permute-start(bf16[512,256]{1,0:T(8,128)(2,1)} %slice.13), channel_id=1, source_target_pairs={{0,16},{1,129},{2,18},{3,131},{4,20},{5,133},{6,22},{7,135},{8,24}... | collective-permute-start | bytes 786440 | tf_op jit(solution)/shard_map/ppermute | solution.py:175
  66.4 3.7 %shard_map.74.local_ref = f32[512,512]{1,0:T(8,128)} custom-call(bf16[512,896]{1,0:T(8,128)(2,1)} %bitcast.7), custom_call_target="tpu_custom_call" | custom-call | flops 536870912 | bytes 2097152 | tf_op jit(solution)/shard_map/pallas_call | solution.py:225
  70.2 0.7 fusion.4.starts_ref
  70.9 5.6 %collective-permute-done.3.refs_4_ = bf16[512,256]{1,0:T(8,128)(2,1)} collective-permute-done((bf16[512,256]{1,0:T(8,128)(2,1)}, bf16[512,256]{1,0:T(8,128)(2,1)}, u32[]{:S(2)}, u32[]{:S(2)}) %collective-permute-start.3) | collective-permute-done | bytes 262176 | tf_op jit(solution)/shard_map/ppermute | solution.py:175
  76.5 7.5 %shard_map.75 = bf16[512,512]{1,0:T(8,128)(2,1)} custom-call(s32[32,16]{1,0:T(8,128)} %fusion.4.starts_ref, f32[32]{0:T(128)} %bias_ref.1, bf16[512,896]{1,0:T(8,128)(2,1)} %bitcast.8, f32[512,512]{1,0:T(8,128)} %shard_map.74.local_ref, bf16[1024,256]{1,0:T(8,128)(2,1)} %bitcast.14, bf16[1024,256]{1,0:T(8,128)(2,1)} %copy-done.5, ...), custom_call_target="tpu_custom_call" | custom-call | flops 536870912 | bytes 7340032 | tf_op jit(solution)/shard_map/pallas_call | solution.py:234
  84.0 16.0 %all_to_all.16 = bf16[8,64,512]{2,1,0:T(8,128)(2,1)S(1)} all-to-all(bf16[8,64,512]{2,1,0:T(8,128)(2,1)} %bitcast.15), channel_id=1, replica_groups=mesh['mem'=64,'ctx'=8] {'ctx'}, dimensions={0} | all-to-all | bytes 1048576 | tf_op jit(solution)/shard_map/all_to_all | solution.py:249
  100.0 0.8 copy.10
  (17 shorter events, 0.0 us)
Async XLA Ops:
  22.3 22.5 %copy-start.1 = (bf16[8,128,256]{2,1,0:T(8,128)(2,1)}, bf16[8,128,256]{2,1,0:T(8,128)(2,1)S(1)}, u32[]{:S(2)}) copy-start(bf16[8,128,256]{2,1,0:T(8,128)(2,1)S(1)} %all_to_all.15) | copy-start | bytes 1572868
  22.3 34.9 %all-to-all-start = ((bf16[8,64,896]{2,1,0:T(8,128)(2,1)}), bf16[8,64,896]{2,1,0:T(8,128)(2,1)S(1)}, u32[]{:S(2)}, u32[]{:S(2)}) async-start(bf16[8,64,896]{2,1,0:T(8,128)(2,1)} %get-tuple-element.7), calls=%async_computation | async-start | bytes 1835008 | tf_op jit(solution)/shard_map/all_to_all | solution.py:217
  31.9 16.8 %collective-permute-start.4 = (bf16[1024,256]{1,0:T(8,128)(2,1)S(1)}, bf16[1024,256]{1,0:T(8,128)(2,1)S(1)}, u32[]{:S(2)}, u32[]{:S(2)}) collective-permute-start(bf16[1024,256]{1,0:T(8,128)(2,1)S(1)} %bitcast.10), channel_id=1, source_target_pairs={{0,48},{1,385},{2,50},{3,387},{4,52},{5,389},{6,54},{7,391},{8,56}... | collective-permute-start | bytes 1572872 | tf_op jit(solution)/shard_map/ppermute | solution.py:175
  37.4 17.7 %collective-permute-start.1 = (bf16[1024,256]{1,0:T(8,128)(2,1)S(1)}, bf16[1024,256]{1,0:T(8,128)(2,1)S(1)}, u32[]{:S(2)}, u32[]{:S(2)}) collective-permute-start(bf16[1024,256]{1,0:T(8,128)(2,1)S(1)} %bitcast.11), channel_id=1, source_target_pairs={{0,16},{1,129},{2,18},{3,131},{4,20},{5,133},{6,22},{7,135},{8,24}... | collective-permute-start | bytes 1572872 | tf_op jit(solution)/shard_map/ppermute | solution.py:175
  39.3 24.5 %collective-permute-start.7 = (bf16[1024,256]{1,0:T(8,128)(2,1)S(1)}, bf16[1024,256]{1,0:T(8,128)(2,1)S(1)}, u32[]{:S(2)}, u32[]{:S(2)}) collective-permute-start(bf16[1024,256]{1,0:T(8,128)(2,1)S(1)} %bitcast.12), channel_id=1, source_target_pairs={{0,56},{1,449},{2,58},{3,451},{4,60},{5,453},{6,62},{7,455},{8,0},... | collective-permute-start | bytes 1572872 | tf_op jit(solution)/shard_map/ppermute | solution.py:175
  44.8 26.0 %collective-permute-start = (bf16[1024,256]{1,0:T(8,128)(2,1)S(1)}, bf16[1024,256]{1,0:T(8,128)(2,1)S(1)}, u32[]{:S(2)}, u32[]{:S(2)}) collective-permute-start(bf16[1024,256]{1,0:T(8,128)(2,1)S(1)} %bitcast.13), channel_id=1, source_target_pairs={{0,8},{1,65},{2,10},{3,67},{4,12},{5,69},{6,14},{7,71},{8,16},{9,7... | collective-permute-start | bytes 1572872 | tf_op jit(solution)/shard_map/ppermute | solution.py:175
  48.7 21.5 %copy-start.2 = (bf16[1024,256]{1,0:T(8,128)(2,1)}, bf16[1024,256]{1,0:T(8,128)(2,1)S(1)}, u32[]{:S(2)}) copy-start(bf16[1024,256]{1,0:T(8,128)(2,1)S(1)} %collective-permute-done.4.refs_7_) | copy-start | bytes 1572868
  48.7 27.7 %collective-permute-start.6 = (bf16[1024,256]{1,0:T(8,128)(2,1)S(1)}, bf16[1024,256]{1,0:T(8,128)(2,1)}, u32[]{:S(2)}, u32[]{:S(2)}) collective-permute-start(bf16[1024,256]{1,0:T(8,128)(2,1)S(1)} %collective-permute-done.4.refs_7_), channel_id=1, source_target_pairs={{0,56},{1,449},{2,58},{3,451},{4,60},{5,453},{6,62},{7,455},{8,0},... | collective-permute-start | bytes 1572872 | tf_op jit(solution)/shard_map/ppermute | solution.py:175
  55.1 15.1 %copy-start.3 = (bf16[1024,256]{1,0:T(8,128)(2,1)}, bf16[1024,256]{1,0:T(8,128)(2,1)S(1)}, u32[]{:S(2)}) copy-start(bf16[1024,256]{1,0:T(8,128)(2,1)S(1)} %collective-permute-done.1.refs_2_) | copy-start | bytes 1572868
  55.1 21.4 %collective-permute-start.2 = (bf16[1024,256]{1,0:T(8,128)(2,1)S(1)}, bf16[1024,256]{1,0:T(8,128)(2,1)}, u32[]{:S(2)}, u32[]{:S(2)}) collective-permute-start(bf16[1024,256]{1,0:T(8,128)(2,1)S(1)} %collective-permute-done.1.refs_2_), channel_id=1, source_target_pairs={{0,8},{1,65},{2,10},{3,67},{4,12},{5,69},{6,14},{7,71},{8,16},{9,7... | collective-permute-start | bytes 1572872 | tf_op jit(solution)/shard_map/ppermute | solution.py:175
  57.2 9.2 %copy-start = (bf16[8,64,896]{2,1,0:T(8,128)(2,1)}, bf16[8,64,896]{2,1,0:T(8,128)(2,1)S(1)}, u32[]{:S(2)}) copy-start(bf16[8,64,896]{2,1,0:T(8,128)(2,1)S(1)} %all-to-all-done) | copy-start | bytes 2752516
  59.5 11.3 %collective-permute-start.5 = (bf16[512,256]{1,0:T(8,128)(2,1)}, bf16[512,256]{1,0:T(8,128)(2,1)}, u32[]{:S(2)}, u32[]{:S(2)}) collective-permute-start(bf16[512,256]{1,0:T(8,128)(2,1)} %slice.14), channel_id=1, source_target_pairs={{0,48},{1,385},{2,50},{3,387},{4,52},{5,389},{6,54},{7,391},{8,56}... | collective-permute-start | bytes 786440 | tf_op jit(solution)/shard_map/ppermute | solution.py:175
  63.8 6.4 %copy-start.4 = (bf16[1024,256]{1,0:T(8,128)(2,1)}, bf16[1024,256]{1,0:T(8,128)(2,1)S(1)}, u32[]{:S(2)}) copy-start(bf16[1024,256]{1,0:T(8,128)(2,1)S(1)} %collective-permute-done.7.refs_8_) | copy-start | bytes 1572868
  63.8 12.7 %collective-permute-start.3 = (bf16[512,256]{1,0:T(8,128)(2,1)}, bf16[512,256]{1,0:T(8,128)(2,1)}, u32[]{:S(2)}, u32[]{:S(2)}) collective-permute-start(bf16[512,256]{1,0:T(8,128)(2,1)} %slice.13), channel_id=1, source_target_pairs={{0,16},{1,129},{2,18},{3,131},{4,20},{5,133},{6,22},{7,135},{8,24}... | collective-permute-start | bytes 786440 | tf_op jit(solution)/shard_map/ppermute | solution.py:175
  70.9 5.6 %copy-start.5 = (bf16[1024,256]{1,0:T(8,128)(2,1)}, bf16[1024,256]{1,0:T(8,128)(2,1)S(1)}, u32[]{:S(2)}) copy-start(bf16[1024,256]{1,0:T(8,128)(2,1)S(1)} %collective-permute-done.refs_1_) | copy-start | bytes 1572868

commit v4 on v3

--- a/solution.py
+++ b/solution.py
@@ -141,58 +141,59 @@
 BOTH = ("mem", "ctx")
 SIDE = 8
 CTX = 8
-
-
-def device(z, y, ctx):
+SLOPE = 3
+
+
+def device(along, across, ctx):
+    z, y = (across, along) if ctx % 2 == 0 else (along, across)
     return (z * SIDE + y) * CTX + ctx
 
 
-def ring_of(ctx):
-    return ctx % 2
-
-
-def first_groups():
-    groups = []
-    for ctx in range(CTX):
-        for other in range(SIDE):
-            if ring_of(ctx) == 0:
-                groups.append([device(z, other, ctx) for z in range(SIDE)])
-            else:
-                groups.append([device(other, y, ctx) for y in range(SIDE)])
-    return groups
-
-
-def shifted(value, step):
-    pairs = []
-    for z in range(SIDE):
-        for y in range(SIDE):
-            for ctx in range(CTX):
-                if ring_of(ctx) == 0:
-                    target = device(z, (y + step) % SIDE, ctx)
-                else:
-                    target = device((z + step) % SIDE, y, ctx)
-                pairs.append((device(z, y, ctx), target))
+def colour(along, across):
+    return (along + SLOPE * across) % SIDE
+
+
+def colour_groups():
+    return [
+        [device((wanted - SLOPE * across) % SIDE, across, ctx) for across in range(SIDE)]
+        for ctx in range(CTX)
+        for wanted in range(SIDE)
+    ]
+
+
+def shifted(value, along_step, across_step):
+    pairs = [
+        (
+            device(along, across, ctx),
+            device((along + along_step) % SIDE, (across + across_step) % SIDE, ctx),
+        )
+        for along in range(SIDE)
+        for across in range(SIDE)
+        for ctx in range(CTX)
+    ]
     return lax.ppermute(value, BOTH, pairs)
 
 
 def gathered(chunk):
-    half = chunk.shape[0] // 2
-    ahead2, behind2 = shifted(chunk, 2), shifted(chunk, -2)
-    ahead1, behind1 = shifted(chunk, 1), shifted(chunk, -1)
-    ahead3, behind3 = shifted(ahead2, 1), shifted(behind2, -1)
-    ahead4, behind4 = shifted(ahead2[:half], 2), shifted(behind2[half:], -2)
-    return [chunk, ahead1, ahead2, ahead3, ahead4, behind4, behind3, behind2, behind1]
+    back1, back7 = shifted(chunk, 1, 0), shifted(chunk, -1, 0)
+    back3, back5 = shifted(chunk, 0, 1), shifted(chunk, 0, -1)
+    back2, back6 = shifted(back1, 1, 0), shifted(back7, -1, 0)
+    back4 = shifted(back1, 0, 1)
+    return [chunk, back1, back2, back3, back4, back5, back6, back7]
 
 
 def block_rows(ids, held, rows):
     holder, slot = ids // held, ids % held
-    z, y = holder // SIDE, holder % SIDE
     mem = lax.axis_index("mem")
-    own_z, own_y = mem // SIDE, mem % SIDE
-    first = ring_of(lax.axis_index("ctx")) == 0
-    back = jnp.where(first, own_y - y, own_z - z) % SIDE
-    inner = jnp.where(first, z, y)
-    return (back * SIDE + inner) * rows + slot * BLOCK
+    first = lax.axis_index("ctx") % 2 == 0
+
+    def position(index):
+        z, y = index // SIDE, index % SIDE
+        return jnp.where(first, y, z), jnp.where(first, z, y)
+
+    along, across = position(holder)
+    back = (colour(*position(mem)) - colour(along, across)) % SIDE
+    return (back * SIDE + across) * rows + slot * BLOCK
 
 
 def body(queries, local_keys, local_values, mem_keys, mem_values, block_ids, gate_bias):
@@ -217,7 +218,7 @@
     qkv = lax.all_to_all(packed, "ctx", split_axis=0, concat_axis=0, tiled=True)
     qkv = qkv.reshape(span, LANES + 3 * HEAD_DIM)
     chunk = lax.all_to_all(
-        spread, BOTH, split_axis=0, concat_axis=0, tiled=True, axis_index_groups=first_groups()
+        spread, BOTH, split_axis=0, concat_axis=0, tiled=True, axis_index_groups=colour_groups()
     ).reshape(SIDE * rows, 2 * HEAD_DIM)
     chunks = gathered(chunk)
     ids = qkv[:, LANES + 2 * HEAD_DIM].astype(jnp.int32).reshape(span // QBLOCK, TOPB)

time: 102 us -> 101 us (level)
  blocking collectives: 35.8 us -> 51.5 us
  starting transfers between devices: 38.2 us -> 23.9 us
  local copies, waits for them, and re-layouts: 3.07 us -> 1.59 us
    all_to_all x1, blocking collectives: 19.8 us -> 36.4 us  [body(): lax.all_to_all(spread, BOTH, split_axis=0, concat_axis=0, tiled=True, axi...]
    ppermute x8 -> x7, starting transfers between devices: 28.6 us -> 18 us  [shifted(): return lax.ppermute(value, BOTH, pairs)]
    all_to_all x1, starting transfers between devices: 9.61 us -> 5.93 us  [body(): qkv = lax.all_to_all(packed, 'ctx', split_axis=0, concat_axis=0, tiled=True)]
    slice x2 -> x0, local copies, waits for them, and re-layouts: 1.46 us -> none  [gathered(): ahead4, behind4 = (shifted(ahead2[:half], 2), shifted(behind2[half:], -2))]
    ppermute x8 -> x7, waiting for transfers between devices: 8.32 us -> 8.07 us  [shifted(): return lax.ppermute(value, BOTH, pairs)]
  transfers between devices with their start and end apart: 9 -> 8, of which waited for: 3 -> 2; matrix products, arithmetic and copies ran while one was open for 4% -> 2% of each run, Pallas kernels for 4% -> 4%
where the time goes in v4:
time: 101 us
  blocking collectives  51.5 us (51%)
  starting transfers between devices  23.9 us (24%)
  Pallas kernels  13.8 us (14%)
  waiting for transfers between devices  8.07 us (8%)
  local copies, waits for them, and re-layouts  1.59 us (2%)
  other arithmetic  1.51 us (1%)
    all_to_all x1, blocking collectives, body(): lax.all_to_all(spread, BOTH, split_axis=0, concat_axis=0, tiled=True, axi...  36.4 us
    ppermute x7, starting transfers between devices, shifted(): return lax.ppermute(value, BOTH, pairs)  18 us
    all_to_all x1, blocking collectives, body(): lax.all_to_all(mixed.reshape(members, tokens, LANES), 'ctx', split_axis=0...  15.1 us
    ppermute x7, waiting for transfers between devices, shifted(): return lax.ppermute(value, BOTH, pairs)  8.07 us
    pallas_call x1, Pallas kernels, body(): pl.pallas_call(memory_kernel, out_shape=jax.ShapeDtypeStruct((span, LANES...  7.52 us
    all_to_all x1, starting transfers between devices, body(): qkv = lax.all_to_all(packed, 'ctx', split_axis=0, concat_axis=0, tiled=True)  5.93 us
    pallas_call x1, Pallas kernels, body(): pl.pallas_call(local_kernel, out_shape=jax.ShapeDtypeStruct((span, LANES)...  3.73 us
    pallas_call x1, Pallas kernels, body(): pl.pallas_call(pack_kernel, out_shape=(jax.ShapeDtypeStruct((members, tok...  2.52 us
  transfers between devices with their start and end apart: 8, of which 2 were waited for; matrix products, arithmetic and copies ran while one was open for 2% of the time, Pallas kernels for 4%

profile of v4, /device:TPU:1, one launch (start us, length us, event | category | flops | bytes accessed | tf_op | source)
XLA Modules:
  0.0 100.5 jit_solution(15750555751746969955)
XLA Ops:
  0.0 2.5 %shard_map.73 = (bf16[8,64,896]{2,1,0:T(8,128)(2,1)}, bf16[8,128,256]{2,1,0:T(8,128)(2,1)}) custom-call(s32[4,16]{1,0:T(4,128)} %ids_ref.1, bf16[64,4096]{1,0:T(8,128)(2,1)} %queries_ref.1, bf16[64,1024]{1,0:T(8,128)(2,1)} %keys_ref.1, bf16[64,1024]{1,0:T(8,128)(2,1)} %values_ref.1, bf16[128,1024]{1,0:T(8,128)(2,1)} %mem_keys_ref.1, ...), custom_call_target="tpu_custom_call" | custom-call | bytes 4194304 | tf_op jit(solution)/shard_map/pallas_call | solution.py:207
  2.5 36.4 %all_to_all.15 = bf16[8,128,256]{2,1,0:T(8,128)(2,1)S(1)} all-to-all(bf16[8,128,256]{2,1,0:T(8,128)(2,1)} %get-tuple-element.8), channel_id=1, replica_groups={{0,104,144,248,288,328,432,472},{8,112,152,192,296,336,440,480},{16,120..., dimensions={0} | all-to-all | bytes 1048576 | tf_op jit(solution)/shard_map/all_to_all | solution.py:220
  38.9 5.9 %all-to-all-start = ((bf16[8,64,896]{2,1,0:T(8,128)(2,1)}), bf16[8,64,896]{2,1,0:T(8,128)(2,1)S(1)}, u32[]{:S(2)}, u32[]{:S(2)}) async-start(bf16[8,64,896]{2,1,0:T(8,128)(2,1)} %get-tuple-element.7), calls=%async_computation | async-start | bytes 1835008 | tf_op jit(solution)/shard_map/all_to_all | solution.py:218
  44.8 1.9 %collective-permute-start.5 = (bf16[1024,256]{1,0:T(8,128)(2,1)S(1)}, bf16[1024,256]{1,0:T(8,128)(2,1)S(1)}, u32[]{:S(2)}, u32[]{:S(2)}) collective-permute-start(bf16[1024,256]{1,0:T(8,128)(2,1)S(1)} %bitcast.10), channel_id=1, source_target_pairs={{0,56},{1,449},{2,58},{3,451},{4,60},{5,453},{6,62},{7,455},{64,12... | collective-permute-start | bytes 1572872 | tf_op jit(solution)/shard_map/ppermute | solution.py:174
  46.8 3.4 %collective-permute-start = (bf16[1024,256]{1,0:T(8,128)(2,1)S(1)}, bf16[1024,256]{1,0:T(8,128)(2,1)S(1)}, u32[]{:S(2)}, u32[]{:S(2)}) collective-permute-start(bf16[1024,256]{1,0:T(8,128)(2,1)S(1)} %bitcast.11), channel_id=1, source_target_pairs={{0,8},{1,65},{2,10},{3,67},{4,12},{5,69},{6,14},{7,71},{64,72},{9,... | collective-permute-start | bytes 1572872 | tf_op jit(solution)/shard_map/ppermute | solution.py:174
  50.1 1.9 %collective-permute-start.4 = (bf16[1024,256]{1,0:T(8,128)(2,1)S(1)}, bf16[1024,256]{1,0:T(8,128)(2,1)S(1)}, u32[]{:S(2)}, u32[]{:S(2)}) collective-permute-start(bf16[1024,256]{1,0:T(8,128)(2,1)S(1)} %bitcast.12), channel_id=1, source_target_pairs={{0,448},{1,57},{2,450},{3,59},{4,452},{5,61},{6,454},{7,63},{64,0}... | collective-permute-start | bytes 1572872 | tf_op jit(solution)/shard_map/ppermute | solution.py:174
  52.1 3.4 %collective-permute-start.2 = (bf16[1024,256]{1,0:T(8,128)(2,1)S(1)}, bf16[1024,256]{1,0:T(8,128)(2,1)S(1)}, u32[]{:S(2)}, u32[]{:S(2)}) collective-permute-start(bf16[1024,256]{1,0:T(8,128)(2,1)S(1)} %bitcast.13), channel_id=1, source_target_pairs={{0,64},{1,9},{2,66},{3,11},{4,68},{5,13},{6,70},{7,15},{64,128},{9... | collective-permute-start | bytes 1572872 | tf_op jit(solution)/shard_map/ppermute | solution.py:174
  55.4 0.0 collective-permute-done.5.refs_7_
  55.5 3.1 %collective-permute-start.6 = (bf16[1024,256]{1,0:T(8,128)(2,1)S(1)}, bf16[1024,256]{1,0:T(8,128)(2,1)}, u32[]{:S(2)}, u32[]{:S(2)}) collective-permute-start(bf16[1024,256]{1,0:T(8,128)(2,1)S(1)} %collective-permute-done.5.refs_7_), channel_id=1, source_target_pairs={{0,56},{1,449},{2,58},{3,451},{4,60},{5,453},{6,62},{7,455},{64,12... | collective-permute-start | bytes 1572872 | tf_op jit(solution)/shard_map/ppermute | solution.py:174
  58.6 0.0 collective-permute-done.refs_1_
  58.6 2.1 %collective-permute-start.3 = (bf16[1024,256]{1,0:T(8,128)(2,1)S(1)}, bf16[1024,256]{1,0:T(8,128)(2,1)}, u32[]{:S(2)}, u32[]{:S(2)}) collective-permute-start(bf16[1024,256]{1,0:T(8,128)(2,1)S(1)} %collective-permute-done.refs_1_), channel_id=1, source_target_pairs={{0,64},{1,9},{2,66},{3,11},{4,68},{5,13},{6,70},{7,15},{64,128},{9... | collective-permute-start | bytes 1572872 | tf_op jit(solution)/shard_map/ppermute | solution.py:174
  60.8 2.2 %collective-permute-start.1 = (bf16[1024,256]{1,0:T(8,128)(2,1)S(1)}, bf16[1024,256]{1,0:T(8,128)(2,1)}, u32[]{:S(2)}, u32[]{:S(2)}) collective-permute-start(bf16[1024,256]{1,0:T(8,128)(2,1)S(1)} %collective-permute-done.refs_1_), channel_id=1, source_target_pairs={{0,8},{1,65},{2,10},{3,67},{4,12},{5,69},{6,14},{7,71},{64,72},{9,... | collective-permute-start | bytes 1572872 | tf_op jit(solution)/shard_map/ppermute | solution.py:174
  63.0 0.0 all-to-all-done
  63.0 0.8 convert_reduce_fusion
  63.9 0.7 reshape.20
  64.6 3.7 %shard_map.74.local_ref = f32[512,512]{1,0:T(8,128)} custom-call(bf16[512,896]{1,0:T(8,128)(2,1)} %bitcast.7), custom_call_target="tpu_custom_call" | custom-call | flops 536870912 | bytes 2097152 | tf_op jit(solution)/shard_map/pallas_call | solution.py:226
  68.3 0.7 fusion.6.starts_ref
  69.0 0.0 collective-permute-done.4.refs_5_
  69.0 0.0 collective-permute-done.2.refs_3_
  69.0 3.2 %collective-permute-done.3.refs_4_ = bf16[1024,256]{1,0:T(8,128)(2,1)} collective-permute-done((bf16[1024,256]{1,0:T(8,128)(2,1)S(1)}, bf16[1024,256]{1,0:T(8,128)(2,1)}, u32[]{:S(2)}, u32[]{:S(2)}) %collective-permute-start.3) | collective-permute-done | bytes 524320 | tf_op jit(solution)/shard_map/ppermute | solution.py:174
  72.2 4.9 %collective-permute-done.1.refs_2_ = bf16[1024,256]{1,0:T(8,128)(2,1)} collective-permute-done((bf16[1024,256]{1,0:T(8,128)(2,1)S(1)}, bf16[1024,256]{1,0:T(8,128)(2,1)}, u32[]{:S(2)}, u32[]{:S(2)}) %collective-permute-start.1) | collective-permute-done | bytes 524320 | tf_op jit(solution)/shard_map/ppermute | solution.py:174
  77.1 7.5 %shard_map.75 = bf16[512,512]{1,0:T(8,128)(2,1)} custom-call(s32[32,16]{1,0:T(8,128)} %fusion.6.starts_ref, f32[32]{0:T(128)} %bias_ref.1, bf16[512,896]{1,0:T(8,128)(2,1)} %bitcast.8, f32[512,512]{1,0:T(8,128)} %shard_map.74.local_ref, bf16[1024,256]{1,0:T(8,128)(2,1)} %bitcast.14, bf16[1024,256]{1,0:T(8,128)(2,1)} %copy-done.3, ...), custom_call_target="tpu_custom_call" | custom-call | flops 536870912 | bytes 7340032 | tf_op jit(solution)/shard_map/pallas_call | solution.py:235
  84.6 15.1 %all_to_all.16 = bf16[8,64,512]{2,1,0:T(8,128)(2,1)S(1)} all-to-all(bf16[8,64,512]{2,1,0:T(8,128)(2,1)} %bitcast.15), channel_id=1, replica_groups=mesh['mem'=64,'ctx'=8] {'ctx'}, dimensions={0} | all-to-all | bytes 1048576 | tf_op jit(solution)/shard_map/all_to_all | solution.py:250
  99.7 0.8 copy.10
  (13 shorter events, 0.0 us)
Async XLA Ops:
  38.9 13.2 %copy-start.1 = (bf16[8,128,256]{2,1,0:T(8,128)(2,1)}, bf16[8,128,256]{2,1,0:T(8,128)(2,1)S(1)}, u32[]{:S(2)}) copy-start(bf16[8,128,256]{2,1,0:T(8,128)(2,1)S(1)} %all_to_all.15) | copy-start | bytes 1572868
  38.9 24.1 %all-to-all-start = ((bf16[8,64,896]{2,1,0:T(8,128)(2,1)}), bf16[8,64,896]{2,1,0:T(8,128)(2,1)S(1)}, u32[]{:S(2)}, u32[]{:S(2)}) async-start(bf16[8,64,896]{2,1,0:T(8,128)(2,1)} %get-tuple-element.7), calls=%async_computation | async-start | bytes 1835008 | tf_op jit(solution)/shard_map/all_to_all | solution.py:218
  44.8 10.6 %collective-permute-start.5 = (bf16[1024,256]{1,0:T(8,128)(2,1)S(1)}, bf16[1024,256]{1,0:T(8,128)(2,1)S(1)}, u32[]{:S(2)}, u32[]{:S(2)}) collective-permute-start(bf16[1024,256]{1,0:T(8,128)(2,1)S(1)} %bitcast.10), channel_id=1, source_target_pairs={{0,56},{1,449},{2,58},{3,451},{4,60},{5,453},{6,62},{7,455},{64,12... | collective-permute-start | bytes 1572872 | tf_op jit(solution)/shard_map/ppermute | solution.py:174
  46.8 11.8 %collective-permute-start = (bf16[1024,256]{1,0:T(8,128)(2,1)S(1)}, bf16[1024,256]{1,0:T(8,128)(2,1)S(1)}, u32[]{:S(2)}, u32[]{:S(2)}) collective-permute-start(bf16[1024,256]{1,0:T(8,128)(2,1)S(1)} %bitcast.11), channel_id=1, source_target_pairs={{0,8},{1,65},{2,10},{3,67},{4,12},{5,69},{6,14},{7,71},{64,72},{9,... | collective-permute-start | bytes 1572872 | tf_op jit(solution)/shard_map/ppermute | solution.py:174
  50.1 18.9 %collective-permute-start.4 = (bf16[1024,256]{1,0:T(8,128)(2,1)S(1)}, bf16[1024,256]{1,0:T(8,128)(2,1)S(1)}, u32[]{:S(2)}, u32[]{:S(2)}) collective-permute-start(bf16[1024,256]{1,0:T(8,128)(2,1)S(1)} %bitcast.12), channel_id=1, source_target_pairs={{0,448},{1,57},{2,450},{3,59},{4,452},{5,61},{6,454},{7,63},{64,0}... | collective-permute-start | bytes 1572872 | tf_op jit(solution)/shard_map/ppermute | solution.py:174
  52.1 16.9 %collective-permute-start.2 = (bf16[1024,256]{1,0:T(8,128)(2,1)S(1)}, bf16[1024,256]{1,0:T(8,128)(2,1)S(1)}, u32[]{:S(2)}, u32[]{:S(2)}) collective-permute-start(bf16[1024,256]{1,0:T(8,128)(2,1)S(1)} %bitcast.13), channel_id=1, source_target_pairs={{0,64},{1,9},{2,66},{3,11},{4,68},{5,13},{6,70},{7,15},{64,128},{9... | collective-permute-start | bytes 1572872 | tf_op jit(solution)/shard_map/ppermute | solution.py:174
  55.4 21.6 %copy-start.2 = (bf16[1024,256]{1,0:T(8,128)(2,1)}, bf16[1024,256]{1,0:T(8,128)(2,1)S(1)}, u32[]{:S(2)}) copy-start(bf16[1024,256]{1,0:T(8,128)(2,1)S(1)} %collective-permute-done.5.refs_7_) | copy-start | bytes 1572868
  55.5 13.5 %collective-permute-start.6 = (bf16[1024,256]{1,0:T(8,128)(2,1)S(1)}, bf16[1024,256]{1,0:T(8,128)(2,1)}, u32[]{:S(2)}, u32[]{:S(2)}) collective-permute-start(bf16[1024,256]{1,0:T(8,128)(2,1)S(1)} %collective-permute-done.5.refs_7_), channel_id=1, source_target_pairs={{0,56},{1,449},{2,58},{3,451},{4,60},{5,453},{6,62},{7,455},{64,12... | collective-permute-start | bytes 1572872 | tf_op jit(solution)/shard_map/ppermute | solution.py:174
  58.6 18.5 %copy-start.3 = (bf16[1024,256]{1,0:T(8,128)(2,1)}, bf16[1024,256]{1,0:T(8,128)(2,1)S(1)}, u32[]{:S(2)}) copy-start(bf16[1024,256]{1,0:T(8,128)(2,1)S(1)} %collective-permute-done.refs_1_) | copy-start | bytes 1572868
  58.6 13.6 %collective-permute-start.3 = (bf16[1024,256]{1,0:T(8,128)(2,1)S(1)}, bf16[1024,256]{1,0:T(8,128)(2,1)}, u32[]{:S(2)}, u32[]{:S(2)}) collective-permute-start(bf16[1024,256]{1,0:T(8,128)(2,1)S(1)} %collective-permute-done.refs_1_), channel_id=1, source_target_pairs={{0,64},{1,9},{2,66},{3,11},{4,68},{5,13},{6,70},{7,15},{64,128},{9... | collective-permute-start | bytes 1572872 | tf_op jit(solution)/shard_map/ppermute | solution.py:174
  60.8 16.3 %collective-permute-start.1 = (bf16[1024,256]{1,0:T(8,128)(2,1)S(1)}, bf16[1024,256]{1,0:T(8,128)(2,1)}, u32[]{:S(2)}, u32[]{:S(2)}) collective-permute-start(bf16[1024,256]{1,0:T(8,128)(2,1)S(1)} %collective-permute-done.refs_1_), channel_id=1, source_target_pairs={{0,8},{1,65},{2,10},{3,67},{4,12},{5,69},{6,14},{7,71},{64,72},{9,... | collective-permute-start | bytes 1572872 | tf_op jit(solution)/shard_map/ppermute | solution.py:174
  63.0 1.6 %copy-start = (bf16[8,64,896]{2,1,0:T(8,128)(2,1)}, bf16[8,64,896]{2,1,0:T(8,128)(2,1)S(1)}, u32[]{:S(2)}) copy-start(bf16[8,64,896]{2,1,0:T(8,128)(2,1)S(1)} %all-to-all-done) | copy-start | bytes 2752516
  69.0 8.1 %copy-start.4 = (bf16[1024,256]{1,0:T(8,128)(2,1)}, bf16[1024,256]{1,0:T(8,128)(2,1)S(1)}, u32[]{:S(2)}) copy-start(bf16[1024,256]{1,0:T(8,128)(2,1)S(1)} %collective-permute-done.4.refs_5_) | copy-start | bytes 1572868
  69.0 8.1 %copy-start.5 = (bf16[1024,256]{1,0:T(8,128)(2,1)}, bf16[1024,256]{1,0:T(8,128)(2,1)S(1)}, u32[]{:S(2)}) copy-start(bf16[1024,256]{1,0:T(8,128)(2,1)S(1)} %collective-permute-done.2.refs_3_) | copy-start | bytes 1572868

commit v5 on v3

--- a/solution.py
+++ b/solution.py
@@ -18,7 +18,7 @@
 EXP2_SCALE = HEAD_DIM ** (-0.5) * 1.4426950408889634
 NEG = -1e30
 TILE = 128
-TOGETHER = 8
+TOGETHER = 32
 
 
 def product(left, right, contract_right):
@@ -63,8 +63,26 @@
         own_ref[place, :, HEAD_DIM:] = values
 
 
-def local_kernel(qkv_ref, out_ref):
+def block_rows(ids, held, rows):
+    holder, slot = ids // held, ids % held
+    z, y = holder // SIDE, holder % SIDE
+    mem = lax.axis_index("mem")
+    own_z, own_y = mem // SIDE, mem % SIDE
+    first = lax.axis_index("ctx") % 2 == 0
+    back = (jnp.where(first, own_y - y, own_z - z) + SIDE) % SIDE
+    inner = jnp.where(first, z, y)
+    return (back * SIDE + inner) * rows + slot * BLOCK
+
+
+def local_kernel(held, rows, qkv_ref, out_ref, starts_ref):
     span = qkv_ref.shape[0]
+    diagonal = lax.broadcasted_iota(jnp.int32, (TILE, HEAD_DIM), 0) == lax.broadcasted_iota(
+        jnp.int32, (TILE, HEAD_DIM), 1
+    )
+    for tile in range(span // TILE):
+        ids = qkv_ref[tile * TILE : (tile + 1) * TILE, LANES + 2 * HEAD_DIM :].astype(jnp.float32)
+        ids = jnp.sum(jnp.where(diagonal, ids, 0.0), axis=0, keepdims=True).astype(jnp.int32)
+        starts_ref[tile : tile + 1, :] = block_rows(ids, held, rows)
     for tile in range(span // TILE):
         lo, hi = tile * TILE, (tile + 1) * TILE
         query = heads_to_rows(qkv_ref[lo:hi, :LANES])
@@ -105,11 +123,11 @@
     for copy in copies:
         copy.wait()
 
-    def some_blocks(step, carry):
-        indices = [step * TOGETHER + k for k in range(TOGETHER)]
-        places = [pl.multiple_of(index * QBLOCK, QBLOCK) for index in indices]
+    for first in range(0, query_blocks, TOGETHER):
+        indices = range(first, first + TOGETHER)
+        places = [index * QBLOCK for index in indices]
         starts = [
-            [pl.multiple_of(starts_ref[index, j], BLOCK) for j in range(TOPB)] for index in indices
+            [pl.multiple_of(starts_ref[divmod(index * TOPB + j, TILE)], BLOCK) for j in range(TOPB)] for index in indices
         ]
         scores = []
         for lo, rows in zip(places, starts):
@@ -133,9 +151,6 @@
                 memory_out = value[rows] * (gates[h] / total[rows])
                 mixed = memory_out + (1.0 - gates[h]) * local_ref[pl.ds(lo, QBLOCK), lanes]
                 out_ref[pl.ds(lo, QBLOCK), lanes] = mixed.astype(jnp.bfloat16)
-        return carry
-
-    lax.fori_loop(0, query_blocks // TOGETHER, some_blocks, 0)
 
 
 BOTH = ("mem", "ctx")
@@ -176,23 +191,11 @@
 
 
 def gathered(chunk):
-    half = chunk.shape[0] // 2
     ahead2, behind2 = shifted(chunk, 2), shifted(chunk, -2)
     ahead1, behind1 = shifted(chunk, 1), shifted(chunk, -1)
+    ahead4 = shifted(ahead2, 2)
     ahead3, behind3 = shifted(ahead2, 1), shifted(behind2, -1)
-    ahead4, behind4 = shifted(ahead2[:half], 2), shifted(behind2[half:], -2)
-    return [chunk, ahead1, ahead2, ahead3, ahead4, behind4, behind3, behind2, behind1]
-
-
-def block_rows(ids, held, rows):
-    holder, slot = ids // held, ids % held
-    z, y = holder // SIDE, holder % SIDE
-    mem = lax.axis_index("mem")
-    own_z, own_y = mem // SIDE, mem % SIDE
-    first = ring_of(lax.axis_index("ctx")) == 0
-    back = jnp.where(first, own_y - y, own_z - z) % SIDE
-    inner = jnp.where(first, z, y)
-    return (back * SIDE + inner) * rows + slot * BLOCK
+    return [chunk, ahead1, ahead2, ahead3, ahead4, behind3, behind2, behind1]
 
 
 def body(queries, local_keys, local_values, mem_keys, mem_values, block_ids, gate_bias):
@@ -220,13 +223,14 @@
         spread, BOTH, split_axis=0, concat_axis=0, tiled=True, axis_index_groups=first_groups()
     ).reshape(SIDE * rows, 2 * HEAD_DIM)
     chunks = gathered(chunk)
-    ids = qkv[:, LANES + 2 * HEAD_DIM].astype(jnp.int32).reshape(span // QBLOCK, TOPB)
-    starts = block_rows(ids, rows // BLOCK, rows)
-    local_out = pl.pallas_call(
-        local_kernel,
-        out_shape=jax.ShapeDtypeStruct((span, LANES), jnp.float32),
+    local_out, starts = pl.pallas_call(
+        functools.partial(local_kernel, rows // BLOCK, rows),
+        out_shape=(
+            jax.ShapeDtypeStruct((span, LANES), jnp.float32),
+            jax.ShapeDtypeStruct((span // TILE, TILE), jnp.int32),
+        ),
         in_specs=[vmem],
-        out_specs=vmem,
+        out_specs=(vmem, vmem),
         cost_estimate=pl.CostEstimate(
             flops=4 * span * LANES * span, bytes_accessed=2 << 20, transcendentals=span * span * 4
         ),

time: 102 us -> 98.3 us (0.964)
  starting transfers between devices: 38.2 us -> 32.8 us
  waiting for transfers between devices: 8.32 us -> 13.6 us
  other arithmetic: 1.5 us -> 0 us
  local copies, waits for them, and re-layouts: 3.07 us -> 1.82 us
    ppermute x8 -> x7, waiting for transfers between devices: 8.32 us -> 13.5 us  [shifted(): return lax.ppermute(value, BOTH, pairs)]
    all_to_all x1, starting transfers between devices: 9.61 us -> 5.13 us  [body(): qkv = lax.all_to_all(packed, 'ctx', split_axis=0, concat_axis=0, tiled=True)]
    slice x2 -> x0, local copies, waits for them, and re-layouts: 1.46 us -> none  [gathered(): ahead4, behind4 = (shifted(ahead2[:half], 2), shifted(behind2[half:], -2))]
    ppermute x8 -> x7, starting transfers between devices: 28.6 us -> 27.7 us  [shifted(): return lax.ppermute(value, BOTH, pairs)]
  transfers between devices with their start and end apart: 9 -> 8, of which waited for: 3 -> 2; matrix products, arithmetic and copies ran while one was open for 4% -> 0% of each run, Pallas kernels for 4% -> 4%
where the time goes in v5:
time: 98.3 us; the launch traced here: 97.7 us
  blocking collectives  36.4 us (37%)
  starting transfers between devices  32.8 us (33%)
  waiting for transfers between devices  13.6 us (14%)
  Pallas kernels  13 us (13%)
  local copies, waits for them, and re-layouts  1.82 us (2%)
    ppermute x7, starting transfers between devices, shifted(): return lax.ppermute(value, BOTH, pairs)  27.7 us
    all_to_all x1, blocking collectives, body(): lax.all_to_all(spread, BOTH, split_axis=0, concat_axis=0, tiled=True, axi...  19.8 us
    all_to_all x1, blocking collectives, body(): lax.all_to_all(mixed.reshape(members, tokens, LANES), 'ctx', split_axis=0...  16.6 us
    ppermute x7, waiting for transfers between devices, shifted(): return lax.ppermute(value, BOTH, pairs)  13.5 us
    pallas_call x1, Pallas kernels, body(): pl.pallas_call(memory_kernel, out_shape=jax.ShapeDtypeStruct((span, LANES...  6.75 us
    all_to_all x1, starting transfers between devices, body(): qkv = lax.all_to_all(packed, 'ctx', split_axis=0, concat_axis=0, tiled=True)  5.13 us
    pallas_call x1, Pallas kernels, body(): pl.pallas_call(functools.partial(local_kernel, rows // BLOCK, rows), out_...  3.73 us
    pallas_call x1, Pallas kernels, body(): pl.pallas_call(pack_kernel, out_shape=(jax.ShapeDtypeStruct((members, tok...  2.52 us
  transfers between devices with their start and end apart: 8, of which 2 were waited for; matrix products, arithmetic and copies ran while one was open for 0% of the time, Pallas kernels for 4%

profile of v5, /device:TPU:1, one launch (start us, length us, event | category | flops | bytes accessed | tf_op | source)
XLA Modules:
  0.0 97.7 jit_solution(1537220861766970192)
XLA Ops:
  0.0 2.5 %shard_map.73 = (bf16[8,64,896]{2,1,0:T(8,128)(2,1)}, bf16[8,128,256]{2,1,0:T(8,128)(2,1)}) custom-call(s32[4,16]{1,0:T(4,128)} %ids_ref.1, bf16[64,4096]{1,0:T(8,128)(2,1)} %queries_ref.1, bf16[64,1024]{1,0:T(8,128)(2,1)} %keys_ref.1, bf16[64,1024]{1,0:T(8,128)(2,1)} %values_ref.1, bf16[128,1024]{1,0:T(8,128)(2,1)} %mem_keys_ref.1, ...), custom_call_target="tpu_custom_call" | custom-call | bytes 4194304 | tf_op jit(solution)/shard_map/pallas_call | solution.py:209
  2.5 19.8 %all_to_all.15 = bf16[8,128,256]{2,1,0:T(8,128)(2,1)S(1)} all-to-all(bf16[8,128,256]{2,1,0:T(8,128)(2,1)} %get-tuple-element.12), channel_id=1, replica_groups={{0,64,128,192,256,320,384,448},{8,72,136,200,264,328,392,456},{16,80,14..., dimensions={0} | all-to-all | bytes 1048576 | tf_op jit(solution)/shard_map/all_to_all | solution.py:222
  22.3 10.6 %collective-permute-start.4 = (bf16[1024,256]{1,0:T(8,128)(2,1)S(1)}, bf16[1024,256]{1,0:T(8,128)(2,1)S(1)}, u32[]{:S(2)}, u32[]{:S(2)}) collective-permute-start(bf16[1024,256]{1,0:T(8,128)(2,1)S(1)} %bitcast.8), channel_id=1, source_target_pairs={{0,48},{1,385},{2,50},{3,387},{4,52},{5,389},{6,54},{7,391},{8,56}... | collective-permute-start | bytes 1572872 | tf_op jit(solution)/shard_map/ppermute | solution.py:190
  33.0 1.9 %collective-permute-start.1 = (bf16[1024,256]{1,0:T(8,128)(2,1)S(1)}, bf16[1024,256]{1,0:T(8,128)(2,1)S(1)}, u32[]{:S(2)}, u32[]{:S(2)}) collective-permute-start(bf16[1024,256]{1,0:T(8,128)(2,1)S(1)} %bitcast.9), channel_id=1, source_target_pairs={{0,16},{1,129},{2,18},{3,131},{4,20},{5,133},{6,22},{7,135},{8,24}... | collective-permute-start | bytes 1572872 | tf_op jit(solution)/shard_map/ppermute | solution.py:190
  34.9 5.1 %all-to-all-start = ((bf16[8,64,896]{2,1,0:T(8,128)(2,1)}), bf16[8,64,896]{2,1,0:T(8,128)(2,1)S(1)}, u32[]{:S(2)}, u32[]{:S(2)}) async-start(bf16[8,64,896]{2,1,0:T(8,128)(2,1)} %get-tuple-element.9), calls=%async_computation | async-start | bytes 1835008 | tf_op jit(solution)/shard_map/all_to_all | solution.py:220
  40.0 4.8 %collective-permute-start.6 = (bf16[1024,256]{1,0:T(8,128)(2,1)S(1)}, bf16[1024,256]{1,0:T(8,128)(2,1)S(1)}, u32[]{:S(2)}, u32[]{:S(2)}) collective-permute-start(bf16[1024,256]{1,0:T(8,128)(2,1)S(1)} %bitcast.10), channel_id=1, source_target_pairs={{0,56},{1,449},{2,58},{3,451},{4,60},{5,453},{6,62},{7,455},{8,0},... | collective-permute-start | bytes 1572872 | tf_op jit(solution)/shard_map/ppermute | solution.py:190
  44.8 1.9 %collective-permute-start = (bf16[1024,256]{1,0:T(8,128)(2,1)S(1)}, bf16[1024,256]{1,0:T(8,128)(2,1)S(1)}, u32[]{:S(2)}, u32[]{:S(2)}) collective-permute-start(bf16[1024,256]{1,0:T(8,128)(2,1)S(1)} %bitcast.11), channel_id=1, source_target_pairs={{0,8},{1,65},{2,10},{3,67},{4,12},{5,69},{6,14},{7,71},{8,16},{9,7... | collective-permute-start | bytes 1572872 | tf_op jit(solution)/shard_map/ppermute | solution.py:190
  46.7 0.0 collective-permute-done.4.refs_6_
  46.8 4.6 %collective-permute-start.5 = (bf16[1024,256]{1,0:T(8,128)(2,1)S(1)}, bf16[1024,256]{1,0:T(8,128)(2,1)}, u32[]{:S(2)}, u32[]{:S(2)}) collective-permute-start(bf16[1024,256]{1,0:T(8,128)(2,1)S(1)} %collective-permute-done.4.refs_6_), channel_id=1, source_target_pairs={{0,56},{1,449},{2,58},{3,451},{4,60},{5,453},{6,62},{7,455},{8,0},... | collective-permute-start | bytes 1572872 | tf_op jit(solution)/shard_map/ppermute | solution.py:190
  51.3 0.0 collective-permute-done.1.refs_2_
  51.4 0.0 copy-start.3
  51.4 1.9 %collective-permute-start.3 = (bf16[1024,256]{1,0:T(8,128)(2,1)S(1)}, bf16[1024,256]{1,0:T(8,128)(2,1)}, u32[]{:S(2)}, u32[]{:S(2)}) collective-permute-start(bf16[1024,256]{1,0:T(8,128)(2,1)S(1)} %collective-permute-done.1.refs_2_), channel_id=1, source_target_pairs={{0,16},{1,129},{2,18},{3,131},{4,20},{5,133},{6,22},{7,135},{8,24}... | collective-permute-start | bytes 1572872 | tf_op jit(solution)/shard_map/ppermute | solution.py:190
  53.3 1.9 %collective-permute-start.2 = (bf16[1024,256]{1,0:T(8,128)(2,1)S(1)}, bf16[1024,256]{1,0:T(8,128)(2,1)}, u32[]{:S(2)}, u32[]{:S(2)}) collective-permute-start(bf16[1024,256]{1,0:T(8,128)(2,1)S(1)} %collective-permute-done.1.refs_2_), channel_id=1, source_target_pairs={{0,8},{1,65},{2,10},{3,67},{4,12},{5,69},{6,14},{7,71},{8,16},{9,7... | collective-permute-start | bytes 1572872 | tf_op jit(solution)/shard_map/ppermute | solution.py:190
  55.2 0.0 all-to-all-done
  55.2 1.0 copy-done
  56.2 3.7 %shard_map.74 = (f32[512,512]{1,0:T(8,128)}, s32[4,128]{1,0:T(4,128)}) custom-call(bf16[512,896]{1,0:T(8,128)(2,1)} %bitcast.6), custom_call_target="tpu_custom_call" | custom-call | flops 536870912 | bytes 2097152 | tf_op jit(solution)/shard_map/pallas_call | solution.py:226
  59.9 0.0 collective-permute-done.6.refs_7_
  59.9 0.0 collective-permute-done.refs_1_
  59.9 0.0 collective-permute-done.5.refs_5_
  60.0 8.7 %collective-permute-done.3.refs_4_ = bf16[1024,256]{1,0:T(8,128)(2,1)} collective-permute-done((bf16[1024,256]{1,0:T(8,128)(2,1)S(1)}, bf16[1024,256]{1,0:T(8,128)(2,1)}, u32[]{:S(2)}, u32[]{:S(2)}) %collective-permute-start.3) | collective-permute-done | bytes 524320 | tf_op jit(solution)/shard_map/ppermute | solution.py:190
  68.7 4.8 %collective-permute-done.2.refs_3_ = bf16[1024,256]{1,0:T(8,128)(2,1)} collective-permute-done((bf16[1024,256]{1,0:T(8,128)(2,1)S(1)}, bf16[1024,256]{1,0:T(8,128)(2,1)}, u32[]{:S(2)}, u32[]{:S(2)}) %collective-permute-start.2) | collective-permute-done | bytes 524320 | tf_op jit(solution)/shard_map/ppermute | solution.py:190
  73.5 6.8 %shard_map.75 = bf16[512,512]{1,0:T(8,128)(2,1)} custom-call(s32[4,128]{1,0:T(4,128)} %get-tuple-element.10.starts_ref, f32[32]{0:T(128)} %bias_ref.1, bf16[512,896]{1,0:T(8,128)(2,1)} %bitcast.7, f32[512,512]{1,0:T(8,128)} %get-tuple-element.11.local_ref, bf16[1024,256]{1,0:T(8,128)(2,1)} %bitcast.12, bf16[1024,256]{1,0:T(8,128)(2,1)} %copy-done.5, ...), custom_call_target="tpu_custom_call" | custom-call | flops 536870912 | bytes 7340032 | tf_op jit(solution)/shard_map/pallas_call | solution.py:238
  80.3 16.6 %all_to_all.16 = bf16[8,64,512]{2,1,0:T(8,128)(2,1)S(1)} all-to-all(bf16[8,64,512]{2,1,0:T(8,128)(2,1)} %bitcast.13), channel_id=1, replica_groups=mesh['mem'=64,'ctx'=8] {'ctx'}, dimensions={0} | all-to-all | bytes 1048576 | tf_op jit(solution)/shard_map/all_to_all | solution.py:253
  96.9 0.8 copy.9
  (10 shorter events, 0.0 us)
Async XLA Ops:
  22.3 22.5 %copy-start.1 = (bf16[8,128,256]{2,1,0:T(8,128)(2,1)}, bf16[8,128,256]{2,1,0:T(8,128)(2,1)S(1)}, u32[]{:S(2)}) copy-start(bf16[8,128,256]{2,1,0:T(8,128)(2,1)S(1)} %all_to_all.15) | copy-start | bytes 1572868
  22.3 24.4 %collective-permute-start.4 = (bf16[1024,256]{1,0:T(8,128)(2,1)S(1)}, bf16[1024,256]{1,0:T(8,128)(2,1)S(1)}, u32[]{:S(2)}, u32[]{:S(2)}) collective-permute-start(bf16[1024,256]{1,0:T(8,128)(2,1)S(1)} %bitcast.8), channel_id=1, source_target_pairs={{0,48},{1,385},{2,50},{3,387},{4,52},{5,389},{6,54},{7,391},{8,56}... | collective-permute-start | bytes 1572872 | tf_op jit(solution)/shard_map/ppermute | solution.py:190
  33.0 18.4 %collective-permute-start.1 = (bf16[1024,256]{1,0:T(8,128)(2,1)S(1)}, bf16[1024,256]{1,0:T(8,128)(2,1)S(1)}, u32[]{:S(2)}, u32[]{:S(2)}) collective-permute-start(bf16[1024,256]{1,0:T(8,128)(2,1)S(1)} %bitcast.9), channel_id=1, source_target_pairs={{0,16},{1,129},{2,18},{3,131},{4,20},{5,133},{6,22},{7,135},{8,24}... | collective-permute-start | bytes 1572872 | tf_op jit(solution)/shard_map/ppermute | solution.py:190
  34.9 20.3 %all-to-all-start = ((bf16[8,64,896]{2,1,0:T(8,128)(2,1)}), bf16[8,64,896]{2,1,0:T(8,128)(2,1)S(1)}, u32[]{:S(2)}, u32[]{:S(2)}) async-start(bf16[8,64,896]{2,1,0:T(8,128)(2,1)} %get-tuple-element.9), calls=%async_computation | async-start | bytes 1835008 | tf_op jit(solution)/shard_map/all_to_all | solution.py:220
  40.0 19.9 %collective-permute-start.6 = (bf16[1024,256]{1,0:T(8,128)(2,1)S(1)}, bf16[1024,256]{1,0:T(8,128)(2,1)S(1)}, u32[]{:S(2)}, u32[]{:S(2)}) collective-permute-start(bf16[1024,256]{1,0:T(8,128)(2,1)S(1)} %bitcast.10), channel_id=1, source_target_pairs={{0,56},{1,449},{2,58},{3,451},{4,60},{5,453},{6,62},{7,455},{8,0},... | collective-permute-start | bytes 1572872 | tf_op jit(solution)/shard_map/ppermute | solution.py:190
  44.8 15.1 %collective-permute-start = (bf16[1024,256]{1,0:T(8,128)(2,1)S(1)}, bf16[1024,256]{1,0:T(8,128)(2,1)S(1)}, u32[]{:S(2)}, u32[]{:S(2)}) collective-permute-start(bf16[1024,256]{1,0:T(8,128)(2,1)S(1)} %bitcast.11), channel_id=1, source_target_pairs={{0,8},{1,65},{2,10},{3,67},{4,12},{5,69},{6,14},{7,71},{8,16},{9,7... | collective-permute-start | bytes 1572872 | tf_op jit(solution)/shard_map/ppermute | solution.py:190
  46.7 26.7 %copy-start.2 = (bf16[1024,256]{1,0:T(8,128)(2,1)}, bf16[1024,256]{1,0:T(8,128)(2,1)S(1)}, u32[]{:S(2)}) copy-start(bf16[1024,256]{1,0:T(8,128)(2,1)S(1)} %collective-permute-done.4.refs_6_) | copy-start | bytes 1572868
  46.8 13.2 %collective-permute-start.5 = (bf16[1024,256]{1,0:T(8,128)(2,1)S(1)}, bf16[1024,256]{1,0:T(8,128)(2,1)}, u32[]{:S(2)}, u32[]{:S(2)}) collective-permute-start(bf16[1024,256]{1,0:T(8,128)(2,1)S(1)} %collective-permute-done.4.refs_6_), channel_id=1, source_target_pairs={{0,56},{1,449},{2,58},{3,451},{4,60},{5,453},{6,62},{7,455},{8,0},... | collective-permute-start | bytes 1572872 | tf_op jit(solution)/shard_map/ppermute | solution.py:190
  51.4 22.1 %copy-start.3 = (bf16[1024,256]{1,0:T(8,128)(2,1)}, bf16[1024,256]{1,0:T(8,128)(2,1)S(1)}, u32[]{:S(2)}) copy-start(bf16[1024,256]{1,0:T(8,128)(2,1)S(1)} %collective-permute-done.1.refs_2_) | copy-start | bytes 1572868
  51.4 17.3 %collective-permute-start.3 = (bf16[1024,256]{1,0:T(8,128)(2,1)S(1)}, bf16[1024,256]{1,0:T(8,128)(2,1)}, u32[]{:S(2)}, u32[]{:S(2)}) collective-permute-start(bf16[1024,256]{1,0:T(8,128)(2,1)S(1)} %collective-permute-done.1.refs_2_), channel_id=1, source_target_pairs={{0,16},{1,129},{2,18},{3,131},{4,20},{5,133},{6,22},{7,135},{8,24}... | collective-permute-start | bytes 1572872 | tf_op jit(solution)/shard_map/ppermute | solution.py:190
  53.3 20.2 %collective-permute-start.2 = (bf16[1024,256]{1,0:T(8,128)(2,1)S(1)}, bf16[1024,256]{1,0:T(8,128)(2,1)}, u32[]{:S(2)}, u32[]{:S(2)}) collective-permute-start(bf16[1024,256]{1,0:T(8,128)(2,1)S(1)} %collective-permute-done.1.refs_2_), channel_id=1, source_target_pairs={{0,8},{1,65},{2,10},{3,67},{4,12},{5,69},{6,14},{7,71},{8,16},{9,7... | collective-permute-start | bytes 1572872 | tf_op jit(solution)/shard_map/ppermute | solution.py:190
  55.2 1.0 copy-start
  59.9 13.6 %copy-start.4 = (bf16[1024,256]{1,0:T(8,128)(2,1)}, bf16[1024,256]{1,0:T(8,128)(2,1)S(1)}, u32[]{:S(2)}) copy-start(bf16[1024,256]{1,0:T(8,128)(2,1)S(1)} %collective-permute-done.6.refs_7_) | copy-start | bytes 1572868
  59.9 13.6 %copy-start.5 = (bf16[1024,256]{1,0:T(8,128)(2,1)}, bf16[1024,256]{1,0:T(8,128)(2,1)S(1)}, u32[]{:S(2)}) copy-start(bf16[1024,256]{1,0:T(8,128)(2,1)S(1)} %collective-permute-done.refs_1_) | copy-start | bytes 1572868

commit v6 on v5

--- a/solution.py
+++ b/solution.py
@@ -193,9 +193,10 @@
 def gathered(chunk):
     ahead2, behind2 = shifted(chunk, 2), shifted(chunk, -2)
     ahead1, behind1 = shifted(chunk, 1), shifted(chunk, -1)
-    ahead4 = shifted(ahead2, 2)
     ahead3, behind3 = shifted(ahead2, 1), shifted(behind2, -1)
-    return [chunk, ahead1, ahead2, ahead3, ahead4, behind3, behind2, behind1]
+    half = chunk.shape[0] // 2
+    ahead4, behind4 = shifted(ahead2[:half], 2), shifted(behind2[half:], -2)
+    return [chunk, ahead1, ahead2, ahead3, ahead4, behind4, behind3, behind2, behind1]
 
 
 def body(queries, local_keys, local_values, mem_keys, mem_values, block_ids, gate_bias):

time: 98.3 us -> 95.1 us (0.967)
  the two profiles are of different devices: /device:TPU:1 before, /device:TPU:8 now
where the time goes in v6:
time: 95.1 us; the launch traced here: 94.4 us
  blocking collectives  38.2 us (40%)
  starting transfers between devices  31.3 us (33%)
  Pallas kernels  13.1 us (14%)
  waiting for transfers between devices  8.39 us (9%)
  local copies, waits for them, and re-layouts  3.27 us (3%)
    ppermute x8, starting transfers between devices, shifted(): return lax.ppermute(value, BOTH, pairs)  27 us
    all_to_all x1, blocking collectives, body(): lax.all_to_all(spread, BOTH, split_axis=0, concat_axis=0, tiled=True, axi...  23.6 us
    all_to_all x1, blocking collectives, body(): lax.all_to_all(mixed.reshape(members, tokens, LANES), 'ctx', split_axis=0...  14.6 us
    ppermute x8, waiting for transfers between devices, shifted(): return lax.ppermute(value, BOTH, pairs)  8.39 us
    pallas_call x1, Pallas kernels, body(): pl.pallas_call(memory_kernel, out_shape=jax.ShapeDtypeStruct((span, LANES...  6.8 us
    all_to_all x1, starting transfers between devices, body(): qkv = lax.all_to_all(packed, 'ctx', split_axis=0, concat_axis=0, tiled=True)  4.31 us
    pallas_call x1, Pallas kernels, body(): pl.pallas_call(functools.partial(local_kernel, rows // BLOCK, rows), out_...  3.74 us
    pallas_call x1, Pallas kernels, body(): pl.pallas_call(pack_kernel, out_shape=(jax.ShapeDtypeStruct((members, tok...  2.52 us
  transfers between devices with their start and end apart: 9, of which 2 were waited for; matrix products, arithmetic and copies ran while one was open for 2% of the time, Pallas kernels for 4%

profile of v6, /device:TPU:8, one launch (start us, length us, event | category | flops | bytes accessed | tf_op | source)
XLA Modules:
  0.0 94.4 jit_solution(3900585972319819944)
XLA Ops:
  0.0 2.5 %shard_map.73 = (bf16[8,64,896]{2,1,0:T(8,128)(2,1)}, bf16[8,128,256]{2,1,0:T(8,128)(2,1)}) custom-call(s32[4,16]{1,0:T(4,128)} %ids_ref.1, bf16[64,4096]{1,0:T(8,128)(2,1)} %queries_ref.1, bf16[64,1024]{1,0:T(8,128)(2,1)} %keys_ref.1, bf16[64,1024]{1,0:T(8,128)(2,1)} %values_ref.1, bf16[128,1024]{1,0:T(8,128)(2,1)} %mem_keys_ref.1, ...), custom_call_target="tpu_custom_call" | custom-call | bytes 4194304 | tf_op jit(solution)/shard_map/pallas_call | solution.py:210
  2.5 23.6 %all_to_all.15 = bf16[8,128,256]{2,1,0:T(8,128)(2,1)S(1)} all-to-all(bf16[8,128,256]{2,1,0:T(8,128)(2,1)} %get-tuple-element.12), channel_id=1, replica_groups={{0,64,128,192,256,320,384,448},{8,72,136,200,264,328,392,456},{16,80,14..., dimensions={0} | all-to-all | bytes 1048576 | tf_op jit(solution)/shard_map/all_to_all | solution.py:223
  26.1 5.3 %collective-permute-start.4 = (bf16[1024,256]{1,0:T(8,128)(2,1)S(1)}, bf16[1024,256]{1,0:T(8,128)(2,1)S(1)}, u32[]{:S(2)}, u32[]{:S(2)}) collective-permute-start(bf16[1024,256]{1,0:T(8,128)(2,1)S(1)} %bitcast.8), channel_id=1, source_target_pairs={{0,48},{1,385},{2,50},{3,387},{4,52},{5,389},{6,54},{7,391},{8,56}... | collective-permute-start | bytes 1572872 | tf_op jit(solution)/shard_map/ppermute | solution.py:190
  31.4 1.9 %collective-permute-start.1 = (bf16[1024,256]{1,0:T(8,128)(2,1)S(1)}, bf16[1024,256]{1,0:T(8,128)(2,1)S(1)}, u32[]{:S(2)}, u32[]{:S(2)}) collective-permute-start(bf16[1024,256]{1,0:T(8,128)(2,1)S(1)} %bitcast.9), channel_id=1, source_target_pairs={{0,16},{1,129},{2,18},{3,131},{4,20},{5,133},{6,22},{7,135},{8,24}... | collective-permute-start | bytes 1572872 | tf_op jit(solution)/shard_map/ppermute | solution.py:190
  33.3 4.3 %all-to-all-start = ((bf16[8,64,896]{2,1,0:T(8,128)(2,1)}), bf16[8,64,896]{2,1,0:T(8,128)(2,1)S(1)}, u32[]{:S(2)}, u32[]{:S(2)}) async-start(bf16[8,64,896]{2,1,0:T(8,128)(2,1)} %get-tuple-element.9), calls=%async_computation | async-start | bytes 1835008 | tf_op jit(solution)/shard_map/all_to_all | solution.py:221
  37.6 3.2 %collective-permute-start.7 = (bf16[1024,256]{1,0:T(8,128)(2,1)S(1)}, bf16[1024,256]{1,0:T(8,128)(2,1)S(1)}, u32[]{:S(2)}, u32[]{:S(2)}) collective-permute-start(bf16[1024,256]{1,0:T(8,128)(2,1)S(1)} %bitcast.10), channel_id=1, source_target_pairs={{0,56},{1,449},{2,58},{3,451},{4,60},{5,453},{6,62},{7,455},{8,0},... | collective-permute-start | bytes 1572872 | tf_op jit(solution)/shard_map/ppermute | solution.py:190
  40.9 2.9 %collective-permute-start = (bf16[1024,256]{1,0:T(8,128)(2,1)S(1)}, bf16[1024,256]{1,0:T(8,128)(2,1)S(1)}, u32[]{:S(2)}, u32[]{:S(2)}) collective-permute-start(bf16[1024,256]{1,0:T(8,128)(2,1)S(1)} %bitcast.11), channel_id=1, source_target_pairs={{0,8},{1,65},{2,10},{3,67},{4,12},{5,69},{6,14},{7,71},{8,16},{9,7... | collective-permute-start | bytes 1572872 | tf_op jit(solution)/shard_map/ppermute | solution.py:190
  43.8 0.0 collective-permute-done.4.refs_7_
  43.8 4.3 %collective-permute-start.6 = (bf16[1024,256]{1,0:T(8,128)(2,1)S(1)}, bf16[1024,256]{1,0:T(8,128)(2,1)}, u32[]{:S(2)}, u32[]{:S(2)}) collective-permute-start(bf16[1024,256]{1,0:T(8,128)(2,1)S(1)} %collective-permute-done.4.refs_7_), channel_id=1, source_target_pairs={{0,56},{1,449},{2,58},{3,451},{4,60},{5,453},{6,62},{7,455},{8,0},... | collective-permute-start | bytes 1572872 | tf_op jit(solution)/shard_map/ppermute | solution.py:190
  48.1 2.2 %collective-permute-done.1.refs_2_ = bf16[1024,256]{1,0:T(8,128)(2,1)S(1)} collective-permute-done((bf16[1024,256]{1,0:T(8,128)(2,1)S(1)}, bf16[1024,256]{1,0:T(8,128)(2,1)S(1)}, u32[]{:S(2)}, u32[]{:S(2)}) %collective-permute-start.1) | collective-permute-done | bytes 524320 | tf_op jit(solution)/shard_map/ppermute | solution.py:190
  50.3 1.9 %collective-permute-start.2 = (bf16[1024,256]{1,0:T(8,128)(2,1)S(1)}, bf16[1024,256]{1,0:T(8,128)(2,1)}, u32[]{:S(2)}, u32[]{:S(2)}) collective-permute-start(bf16[1024,256]{1,0:T(8,128)(2,1)S(1)} %collective-permute-done.1.refs_2_), channel_id=1, source_target_pairs={{0,8},{1,65},{2,10},{3,67},{4,12},{5,69},{6,14},{7,71},{8,16},{9,7... | collective-permute-start | bytes 1572872 | tf_op jit(solution)/shard_map/ppermute | solution.py:190
  52.2 0.7 slice.9
  53.0 5.6 %collective-permute-start.5 = (bf16[512,256]{1,0:T(8,128)(2,1)}, bf16[512,256]{1,0:T(8,128)(2,1)}, u32[]{:S(2)}, u32[]{:S(2)}) collective-permute-start(bf16[512,256]{1,0:T(8,128)(2,1)} %slice.9), channel_id=1, source_target_pairs={{0,48},{1,385},{2,50},{3,387},{4,52},{5,389},{6,54},{7,391},{8,56}... | collective-permute-start | bytes 786440 | tf_op jit(solution)/shard_map/ppermute | solution.py:190
  58.6 0.7 slice.8
  59.3 1.9 %collective-permute-start.3 = (bf16[512,256]{1,0:T(8,128)(2,1)}, bf16[512,256]{1,0:T(8,128)(2,1)}, u32[]{:S(2)}, u32[]{:S(2)}) collective-permute-start(bf16[512,256]{1,0:T(8,128)(2,1)} %slice.8), channel_id=1, source_target_pairs={{0,16},{1,129},{2,18},{3,131},{4,20},{5,133},{6,22},{7,135},{8,24}... | collective-permute-start | bytes 786440 | tf_op jit(solution)/shard_map/ppermute | solution.py:190
  61.3 0.0 all-to-all-done
  61.3 1.0 %copy-done = bf16[8,64,896]{2,1,0:T(8,128)(2,1)} copy-done((bf16[8,64,896]{2,1,0:T(8,128)(2,1)}, bf16[8,64,896]{2,1,0:T(8,128)(2,1)S(1)}, u32[]{:S(2)}) %copy-start) | copy-done | bytes 917528
  62.2 3.7 %shard_map.74 = (f32[512,512]{1,0:T(8,128)}, s32[4,128]{1,0:T(4,128)}) custom-call(bf16[512,896]{1,0:T(8,128)(2,1)} %bitcast.6), custom_call_target="tpu_custom_call" | custom-call | flops 536870912 | bytes 2097152 | tf_op jit(solution)/shard_map/pallas_call | solution.py:227
  66.0 0.0 collective-permute-done.refs_1_
  66.0 6.2 %collective-permute-done.3.refs_4_ = bf16[512,256]{1,0:T(8,128)(2,1)} collective-permute-done((bf16[512,256]{1,0:T(8,128)(2,1)}, bf16[512,256]{1,0:T(8,128)(2,1)}, u32[]{:S(2)}, u32[]{:S(2)}) %collective-permute-start.3) | collective-permute-done | bytes 262176 | tf_op jit(solution)/shard_map/ppermute | solution.py:190
  72.2 0.0 collective-permute-done.6.refs_6_
  72.2 6.8 %shard_map.75 = bf16[512,512]{1,0:T(8,128)(2,1)} custom-call(s32[4,128]{1,0:T(4,128)} %get-tuple-element.10.starts_ref, f32[32]{0:T(128)} %bias_ref.1, bf16[512,896]{1,0:T(8,128)(2,1)} %bitcast.7, f32[512,512]{1,0:T(8,128)} %get-tuple-element.11.local_ref, bf16[1024,256]{1,0:T(8,128)(2,1)} %bitcast.12, bf16[1024,256]{1,0:T(8,128)(2,1)} %copy-done.5, ...), custom_call_target="tpu_custom_call" | custom-call | flops 536870912 | bytes 7340032 | tf_op jit(solution)/shard_map/pallas_call | solution.py:239
  79.0 14.6 %all_to_all.16 = bf16[8,64,512]{2,1,0:T(8,128)(2,1)S(1)} all-to-all(bf16[8,64,512]{2,1,0:T(8,128)(2,1)} %bitcast.13), channel_id=1, replica_groups=mesh['mem'=64,'ctx'=8] {'ctx'}, dimensions={0} | all-to-all | bytes 1048576 | tf_op jit(solution)/shard_map/all_to_all | solution.py:254
  93.6 0.8 copy.9
  (14 shorter events, 0.0 us)
Async XLA Ops:
  26.1 14.8 %copy-start.1 = (bf16[8,128,256]{2,1,0:T(8,128)(2,1)}, bf16[8,128,256]{2,1,0:T(8,128)(2,1)S(1)}, u32[]{:S(2)}) copy-start(bf16[8,128,256]{2,1,0:T(8,128)(2,1)S(1)} %all_to_all.15) | copy-start | bytes 1572868
  26.1 17.7 %collective-permute-start.4 = (bf16[1024,256]{1,0:T(8,128)(2,1)S(1)}, bf16[1024,256]{1,0:T(8,128)(2,1)S(1)}, u32[]{:S(2)}, u32[]{:S(2)}) collective-permute-start(bf16[1024,256]{1,0:T(8,128)(2,1)S(1)} %bitcast.8), channel_id=1, source_target_pairs={{0,48},{1,385},{2,50},{3,387},{4,52},{5,389},{6,54},{7,391},{8,56}... | collective-permute-start | bytes 1572872 | tf_op jit(solution)/shard_map/ppermute | solution.py:190
  31.4 18.9 %collective-permute-start.1 = (bf16[1024,256]{1,0:T(8,128)(2,1)S(1)}, bf16[1024,256]{1,0:T(8,128)(2,1)S(1)}, u32[]{:S(2)}, u32[]{:S(2)}) collective-permute-start(bf16[1024,256]{1,0:T(8,128)(2,1)S(1)} %bitcast.9), channel_id=1, source_target_pairs={{0,16},{1,129},{2,18},{3,131},{4,20},{5,133},{6,22},{7,135},{8,24}... | collective-permute-start | bytes 1572872 | tf_op jit(solution)/shard_map/ppermute | solution.py:190
  33.3 27.9 %all-to-all-start = ((bf16[8,64,896]{2,1,0:T(8,128)(2,1)}), bf16[8,64,896]{2,1,0:T(8,128)(2,1)S(1)}, u32[]{:S(2)}, u32[]{:S(2)}) async-start(bf16[8,64,896]{2,1,0:T(8,128)(2,1)} %get-tuple-element.9), calls=%async_computation | async-start | bytes 1835008 | tf_op jit(solution)/shard_map/all_to_all | solution.py:221
  37.6 21.7 %collective-permute-start.7 = (bf16[1024,256]{1,0:T(8,128)(2,1)S(1)}, bf16[1024,256]{1,0:T(8,128)(2,1)S(1)}, u32[]{:S(2)}, u32[]{:S(2)}) collective-permute-start(bf16[1024,256]{1,0:T(8,128)(2,1)S(1)} %bitcast.10), channel_id=1, source_target_pairs={{0,56},{1,449},{2,58},{3,451},{4,60},{5,453},{6,62},{7,455},{8,0},... | collective-permute-start | bytes 1572872 | tf_op jit(solution)/shard_map/ppermute | solution.py:190
  40.9 25.1 %collective-permute-start = (bf16[1024,256]{1,0:T(8,128)(2,1)S(1)}, bf16[1024,256]{1,0:T(8,128)(2,1)S(1)}, u32[]{:S(2)}, u32[]{:S(2)}) collective-permute-start(bf16[1024,256]{1,0:T(8,128)(2,1)S(1)} %bitcast.11), channel_id=1, source_target_pairs={{0,8},{1,65},{2,10},{3,67},{4,12},{5,69},{6,14},{7,71},{8,16},{9,7... | collective-permute-start | bytes 1572872 | tf_op jit(solution)/shard_map/ppermute | solution.py:190
  43.8 15.5 %copy-start.2 = (bf16[1024,256]{1,0:T(8,128)(2,1)}, bf16[1024,256]{1,0:T(8,128)(2,1)S(1)}, u32[]{:S(2)}) copy-start(bf16[1024,256]{1,0:T(8,128)(2,1)S(1)} %collective-permute-done.4.refs_7_) | copy-start | bytes 1572868
  43.8 28.3 %collective-permute-start.6 = (bf16[1024,256]{1,0:T(8,128)(2,1)S(1)}, bf16[1024,256]{1,0:T(8,128)(2,1)}, u32[]{:S(2)}, u32[]{:S(2)}) collective-permute-start(bf16[1024,256]{1,0:T(8,128)(2,1)S(1)} %collective-permute-done.4.refs_7_), channel_id=1, source_target_pairs={{0,56},{1,449},{2,58},{3,451},{4,60},{5,453},{6,62},{7,455},{8,0},... | collective-permute-start | bytes 1572872 | tf_op jit(solution)/shard_map/ppermute | solution.py:190
  50.3 9.0 %copy-start.3 = (bf16[1024,256]{1,0:T(8,128)(2,1)}, bf16[1024,256]{1,0:T(8,128)(2,1)S(1)}, u32[]{:S(2)}) copy-start(bf16[1024,256]{1,0:T(8,128)(2,1)S(1)} %collective-permute-done.1.refs_2_) | copy-start | bytes 1572868
  50.3 21.9 %collective-permute-start.2 = (bf16[1024,256]{1,0:T(8,128)(2,1)S(1)}, bf16[1024,256]{1,0:T(8,128)(2,1)}, u32[]{:S(2)}, u32[]{:S(2)}) collective-permute-start(bf16[1024,256]{1,0:T(8,128)(2,1)S(1)} %collective-permute-done.1.refs_2_), channel_id=1, source_target_pairs={{0,8},{1,65},{2,10},{3,67},{4,12},{5,69},{6,14},{7,71},{8,16},{9,7... | collective-permute-start | bytes 1572872 | tf_op jit(solution)/shard_map/ppermute | solution.py:190
  53.0 13.0 %collective-permute-start.5 = (bf16[512,256]{1,0:T(8,128)(2,1)}, bf16[512,256]{1,0:T(8,128)(2,1)}, u32[]{:S(2)}, u32[]{:S(2)}) collective-permute-start(bf16[512,256]{1,0:T(8,128)(2,1)} %slice.9), channel_id=1, source_target_pairs={{0,48},{1,385},{2,50},{3,387},{4,52},{5,389},{6,54},{7,391},{8,56}... | collective-permute-start | bytes 786440 | tf_op jit(solution)/shard_map/ppermute | solution.py:190
  59.3 12.9 %copy-start.4 = (bf16[1024,256]{1,0:T(8,128)(2,1)}, bf16[1024,256]{1,0:T(8,128)(2,1)S(1)}, u32[]{:S(2)}) copy-start(bf16[1024,256]{1,0:T(8,128)(2,1)S(1)} %collective-permute-done.7.refs_8_) | copy-start | bytes 1572868
  59.3 12.8 %collective-permute-start.3 = (bf16[512,256]{1,0:T(8,128)(2,1)}, bf16[512,256]{1,0:T(8,128)(2,1)}, u32[]{:S(2)}, u32[]{:S(2)}) collective-permute-start(bf16[512,256]{1,0:T(8,128)(2,1)} %slice.8), channel_id=1, source_target_pairs={{0,16},{1,129},{2,18},{3,131},{4,20},{5,133},{6,22},{7,135},{8,24}... | collective-permute-start | bytes 786440 | tf_op jit(solution)/shard_map/ppermute | solution.py:190
  61.3 1.0 %copy-start = (bf16[8,64,896]{2,1,0:T(8,128)(2,1)}, bf16[8,64,896]{2,1,0:T(8,128)(2,1)S(1)}, u32[]{:S(2)}) copy-start(bf16[8,64,896]{2,1,0:T(8,128)(2,1)S(1)} %all-to-all-done) | copy-start | bytes 2752516
  66.0 6.2 %copy-start.5 = (bf16[1024,256]{1,0:T(8,128)(2,1)}, bf16[1024,256]{1,0:T(8,128)(2,1)S(1)}, u32[]{:S(2)}) copy-start(bf16[1024,256]{1,0:T(8,128)(2,1)S(1)} %collective-permute-done.refs_1_) | copy-start | bytes 1572868

commit v7 on v5

--- a/solution.py
+++ b/solution.py
@@ -74,7 +74,11 @@
     return (back * SIDE + inner) * rows + slot * BLOCK
 
 
-def local_kernel(held, rows, qkv_ref, out_ref, starts_ref):
+def local_kernel(held, rows, bias_ref, qkv_ref, out_ref, starts_ref, gates_ref):
+    head = lax.axis_index("ctx")
+    for h in range(GROUPS):
+        bias = jnp.full((1, HEAD_DIM), bias_ref[head * GROUPS + h], jnp.float32)
+        gates_ref[h : h + 1, :] = jax.nn.sigmoid(bias)
     span = qkv_ref.shape[0]
     diagonal = lax.broadcasted_iota(jnp.int32, (TILE, HEAD_DIM), 0) == lax.broadcasted_iota(
         jnp.int32, (TILE, HEAD_DIM), 1
@@ -104,21 +108,22 @@
     return jnp.concatenate([store_ref[pl.ds(row, BLOCK), lanes] for row in rows], axis=0)
 
 
-def memory_kernel(starts_ref, bias_ref, qkv_ref, local_ref, *refs):
+def memory_kernel(places, starts_ref, gates_ref, qkv_ref, local_ref, *refs):
     chunks, (out_ref, store_ref, sems) = refs[:-3], refs[-3:]
-    copies, row = [], 0
-    for i, chunk in enumerate(chunks):
-        rows = chunk.shape[0]
-        copies.append(
-            pltpu.make_async_copy(chunk, store_ref.at[pl.ds(row, rows)], sems.at[i])
-        )
-        copies[-1].start()
-        row += rows
-    head = lax.axis_index("ctx")
-    gates = [
-        jax.nn.sigmoid(jnp.full((1, HEAD_DIM), bias_ref[head * GROUPS + h], jnp.float32))
-        for h in range(GROUPS)
-    ]
+    whole = store_ref.shape[0] // SIDE
+    copies = []
+    for chunk, backs in zip(chunks, places):
+        rows = chunk.shape[0] // len(backs)
+        for k, back in enumerate(backs):
+            copies.append(
+                pltpu.make_async_copy(
+                    chunk.at[pl.ds(k * rows, rows)],
+                    store_ref.at[pl.ds(int(back * whole), rows)],
+                    sems.at[len(copies)],
+                )
+            )
+            copies[-1].start()
+    gates = [gates_ref[h : h + 1, :] for h in range(GROUPS)]
     query_blocks = qkv_ref.shape[0] // QBLOCK
     for copy in copies:
         copy.wait()
@@ -190,12 +195,56 @@
     return lax.ppermute(value, BOTH, pairs)
 
 
-def gathered(chunk):
+def join_kernel(chunk_ref, ahead_ref, behind_ref, *refs):
+    (ahead_pair, behind_pair, ahead_half, behind_half), sems = refs[:4], refs[4]
+    rows = chunk_ref.shape[0]
+    half = rows // 2
+    moves = [
+        (chunk_ref, ahead_pair.at[pl.ds(0, rows)]),
+        (ahead_ref, ahead_pair.at[pl.ds(rows, rows)]),
+        (chunk_ref, behind_pair.at[pl.ds(0, rows)]),
+        (behind_ref, behind_pair.at[pl.ds(rows, rows)]),
+        (ahead_ref.at[pl.ds(0, half)], ahead_half),
+        (behind_ref.at[pl.ds(half, half)], behind_half),
+    ]
+    copies = [
+        pltpu.make_async_copy(source, target, sems.at[i])
+        for i, (source, target) in enumerate(moves)
+    ]
+    for copy in copies:
+        copy.start()
+    for copy in copies:
+        copy.wait()
+
+
+def gathered(chunk, qkv):
+    rows, width = chunk.shape
     ahead2, behind2 = shifted(chunk, 2), shifted(chunk, -2)
-    ahead1, behind1 = shifted(chunk, 1), shifted(chunk, -1)
-    ahead4 = shifted(ahead2, 2)
-    ahead3, behind3 = shifted(ahead2, 1), shifted(behind2, -1)
-    return [chunk, ahead1, ahead2, ahead3, ahead4, behind3, behind2, behind1]
+    hbm = pl.BlockSpec(memory_space=pl.ANY)
+    joined = pl.pallas_call(
+        join_kernel,
+        out_shape=[
+            jax.ShapeDtypeStruct((count, width), chunk.dtype)
+            for count in (2 * rows, 2 * rows, rows // 2, rows // 2)
+        ],
+        in_specs=[hbm] * 3,
+        out_specs=[pl.BlockSpec(memory_space=pltpu.HBM)] * 4,
+        scratch_shapes=[pltpu.SemaphoreType.DMA((6,))],
+        compiler_params=pltpu.CompilerParams(vmem_limit_bytes=1 << 20),
+        cost_estimate=pl.CostEstimate(flops=0, bytes_accessed=5 << 20, transcendentals=0),
+    )(chunk, ahead2, behind2)
+    ahead13, behind13 = shifted(joined[0], 1), shifted(joined[1], -1)
+    ahead_half, behind_half, qkv = lax.optimization_barrier((joined[2], joined[3], qkv))
+    ahead4, behind4 = shifted(ahead_half, 2), shifted(behind_half, -2)
+    return qkv, [
+        (chunk, (0,)),
+        (ahead13, (1, 3)),
+        (ahead2, (2,)),
+        (ahead4, (4,)),
+        (behind4, (4.5,)),
+        (behind13, (7, 5)),
+        (behind2, (6,)),
+    ]
 
 
 def body(queries, local_keys, local_values, mem_keys, mem_values, block_ids, gate_bias):
@@ -222,34 +271,38 @@
     chunk = lax.all_to_all(
         spread, BOTH, split_axis=0, concat_axis=0, tiled=True, axis_index_groups=first_groups()
     ).reshape(SIDE * rows, 2 * HEAD_DIM)
-    chunks = gathered(chunk)
-    local_out, starts = pl.pallas_call(
+    qkv, pieces = gathered(chunk, qkv)
+    chunks, places = [piece for piece, _ in pieces], [backs for _, backs in pieces]
+    local_out, starts, gates = pl.pallas_call(
         functools.partial(local_kernel, rows // BLOCK, rows),
         out_shape=(
             jax.ShapeDtypeStruct((span, LANES), jnp.float32),
             jax.ShapeDtypeStruct((span // TILE, TILE), jnp.int32),
-        ),
-        in_specs=[vmem],
-        out_specs=(vmem, vmem),
+            jax.ShapeDtypeStruct((GROUPS, HEAD_DIM), jnp.float32),
+        ),
+        in_specs=[smem, vmem],
+        out_specs=(vmem, vmem, vmem),
+        compiler_params=pltpu.CompilerParams(vmem_limit_bytes=12 << 20),
         cost_estimate=pl.CostEstimate(
             flops=4 * span * LANES * span, bytes_accessed=2 << 20, transcendentals=span * span * 4
         ),
-    )(qkv)
+    )(gate_bias, qkv)
     mixed = pl.pallas_call(
-        memory_kernel,
+        functools.partial(memory_kernel, places),
         out_shape=jax.ShapeDtypeStruct((span, LANES), jnp.bfloat16),
-        in_specs=[smem, smem, vmem, vmem] + [hbm] * len(chunks),
+        in_specs=[smem, vmem, vmem, vmem] + [hbm] * len(chunks),
         out_specs=vmem,
         scratch_shapes=[
             pltpu.VMEM((SIDE * SIDE * rows, 2 * HEAD_DIM), jnp.bfloat16),
-            pltpu.SemaphoreType.DMA((len(chunks),)),
+            pltpu.SemaphoreType.DMA((sum(map(len, places)),)),
         ],
+        compiler_params=pltpu.CompilerParams(vmem_limit_bytes=32 << 20),
         cost_estimate=pl.CostEstimate(
             flops=4 * span * LANES * TOPB * BLOCK,
             bytes_accessed=7 << 20,
             transcendentals=span * GROUPS * TOPB * BLOCK,
         ),
-    )(starts, gate_bias, qkv, local_out, *chunks)
+    )(starts, gates, qkv, local_out, *chunks)
     back = lax.all_to_all(
         mixed.reshape(members, tokens, LANES), "ctx", split_axis=0, concat_axis=0, tiled=True
     )

time: 98.3 us -> 99.1 us (level)
  waiting for transfers between devices: 13.6 us -> 18.7 us
  Pallas kernels: 13 us -> 10.4 us
  starting transfers between devices: 32.8 us -> 31.6 us
    ppermute x7 -> x6, waiting for transfers between devices: 13.5 us -> 18.7 us  [shifted(): return lax.ppermute(value, BOTH, pairs)]
    pallas_call x1, Pallas kernels: 3.73 us -> 2.11 us  [body(): pl.pallas_call(functools.partial(local_kernel, rows // BLOCK, rows), out_...]
    ppermute x7 -> x6, starting transfers between devices: 27.7 us -> 26.4 us  [shifted(): return lax.ppermute(value, BOTH, pairs)]
    pallas_call x1 -> x2, Pallas kernels: 6.75 us -> 5.76 us  [the longest x1 4.37 us: body(): pl.pallas_call(functools.partial(memory_kernel, places), out_shape=jax.Sh...]
  transfers between devices with their start and end apart: 8 -> 7, of which waited for: 2 -> 4; matrix products, arithmetic and copies ran while one was open for 0% -> 0% of each run, Pallas kernels for 4% -> 4%
where the time goes in v7:
time: 99.1 us; the launch traced here: 98.7 us
  blocking collectives  35.7 us (36%)
  starting transfers between devices  31.6 us (32%)
  waiting for transfers between devices  18.7 us (19%)
  Pallas kernels  10.4 us (10%)
  local copies, waits for them, and re-layouts  2.23 us (2%)
    ppermute x6, starting transfers between devices, shifted(): return lax.ppermute(value, BOTH, pairs)  26.4 us
    all_to_all x1, blocking collectives, body(): lax.all_to_all(spread, BOTH, split_axis=0, concat_axis=0, tiled=True, axi...  19.8 us
    ppermute x6, waiting for transfers between devices, shifted(): return lax.ppermute(value, BOTH, pairs)  18.7 us
    all_to_all x1, blocking collectives, body(): lax.all_to_all(mixed.reshape(members, tokens, LANES), 'ctx', split_axis=0...  15.9 us
    all_to_all x1, starting transfers between devices, body(): qkv = lax.all_to_all(packed, 'ctx', split_axis=0, concat_axis=0, tiled=True)  5.13 us
    pallas_call x1, Pallas kernels, body(): pl.pallas_call(functools.partial(memory_kernel, places), out_shape=jax.Sh...  4.37 us
    pallas_call x1, Pallas kernels, body(): pl.pallas_call(pack_kernel, out_shape=(jax.ShapeDtypeStruct((members, tok...  2.52 us
    pallas_call x1, Pallas kernels, body(): pl.pallas_call(functools.partial(local_kernel, rows // BLOCK, rows), out_...  2.11 us
  transfers between devices with their start and end apart: 7, of which 4 were waited for; matrix products, arithmetic and copies ran while one was open for 0% of the time, Pallas kernels for 4%

profile of v7, /device:TPU:1, one launch (start us, length us, event | category | flops | bytes accessed | tf_op | source)
XLA Modules:
  0.0 98.7 jit_solution(851321374428689718)
XLA Ops:
  0.0 2.5 %shard_map.73 = (bf16[8,64,896]{2,1,0:T(8,128)(2,1)}, bf16[8,128,256]{2,1,0:T(8,128)(2,1)}) custom-call(s32[4,16]{1,0:T(4,128)} %ids_ref.1, bf16[64,4096]{1,0:T(8,128)(2,1)} %queries_ref.1, bf16[64,1024]{1,0:T(8,128)(2,1)} %keys_ref.1, bf16[64,1024]{1,0:T(8,128)(2,1)} %values_ref.1, bf16[128,1024]{1,0:T(8,128)(2,1)} %mem_keys_ref.1, ...), custom_call_target="tpu_custom_call" | custom-call | bytes 4194304 | tf_op jit(solution)/shard_map/pallas_call | solution.py:258
  2.5 19.8 %all_to_all.15 = bf16[8,128,256]{2,1,0:T(8,128)(2,1)S(1)} all-to-all(bf16[8,128,256]{2,1,0:T(8,128)(2,1)} %get-tuple-element.17), channel_id=1, replica_groups={{0,64,128,192,256,320,384,448},{8,72,136,200,264,328,392,456},{16,80,14..., dimensions={0} | all-to-all | bytes 1048576 | tf_op jit(solution)/shard_map/all_to_all | solution.py:271
  22.3 10.6 %collective-permute-start.1 = (bf16[1024,256]{1,0:T(8,128)(2,1)S(1)}, bf16[1024,256]{1,0:T(8,128)(2,1)S(1)}, u32[]{:S(2)}, u32[]{:S(2)}) collective-permute-start(bf16[1024,256]{1,0:T(8,128)(2,1)S(1)} %bitcast.6), channel_id=1, source_target_pairs={{0,48},{1,385},{2,50},{3,387},{4,52},{5,389},{6,54},{7,391},{8,56}... | collective-permute-start | bytes 1572872 | tf_op jit(solution)/shard_map/ppermute | solution.py:195
  33.0 1.9 %collective-permute-start = (bf16[1024,256]{1,0:T(8,128)(2,1)S(1)}, bf16[1024,256]{1,0:T(8,128)(2,1)S(1)}, u32[]{:S(2)}, u32[]{:S(2)}) collective-permute-start(bf16[1024,256]{1,0:T(8,128)(2,1)S(1)} %bitcast.7), channel_id=1, source_target_pairs={{0,16},{1,129},{2,18},{3,131},{4,20},{5,133},{6,22},{7,135},{8,24}... | collective-permute-start | bytes 1572872 | tf_op jit(solution)/shard_map/ppermute | solution.py:195
  34.9 5.1 %all-to-all-start.1 = ((bf16[8,64,896]{2,1,0:T(8,128)(2,1)}), bf16[8,64,896]{2,1,0:T(8,128)(2,1)S(1)}, u32[]{:S(2)}, u32[]{:S(2)}) async-start(bf16[8,64,896]{2,1,0:T(8,128)(2,1)} %get-tuple-element.20), calls=%async_computation.1 | async-start | bytes 1835008 | tf_op jit(solution)/shard_map/all_to_all | solution.py:269
  40.0 4.7 %collective-permute-done.1.behind_ref.refs_6_ = bf16[1024,256]{1,0:T(8,128)(2,1)S(1)} collective-permute-done((bf16[1024,256]{1,0:T(8,128)(2,1)S(1)}, bf16[1024,256]{1,0:T(8,128)(2,1)S(1)}, u32[]{:S(2)}, u32[]{:S(2)}) %collective-permute-start.1) | collective-permute-done | bytes 524320 | tf_op jit(solution)/shard_map/ppermute | solution.py:195
  44.7 5.9 %collective-permute-done.ahead_ref.refs_2_ = bf16[1024,256]{1,0:T(8,128)(2,1)S(1)} collective-permute-done((bf16[1024,256]{1,0:T(8,128)(2,1)S(1)}, bf16[1024,256]{1,0:T(8,128)(2,1)S(1)}, u32[]{:S(2)}, u32[]{:S(2)}) %collective-permute-start) | collective-permute-done | bytes 524320 | tf_op jit(solution)/shard_map/ppermute | solution.py:195
  50.6 1.4 %shard_map.74 = (bf16[2048,256]{1,0:T(8,128)(2,1)}, bf16[2048,256]{1,0:T(8,128)(2,1)}, bf16[512,256]{1,0:T(8,128)(2,1)S(1)}, bf16[512,256]{1,0:T(8,128)(2,1)S(1)}) custom-call(bf16[1024,256]{1,0:T(8,128)(2,1)S(1)} %bitcast.8, bf16[1024,256]{1,0:T(8,128)(2,1)S(1)} %collective-permute-done.ahead_ref.refs_2_, ...), custom_call_target="tpu_custom_call" | custom-call | bytes 5242880 | tf_op jit(solution)/shard_map/pallas_call | solution.py:224
  52.0 0.7 copy-done
  52.7 0.7 copy-done.1
  53.4 2.0 %collective-permute-start.2 = (bf16[2048,256]{1,0:T(8,128)(2,1)}, bf16[2048,256]{1,0:T(8,128)(2,1)S(1)}, u32[]{:S(2)}, u32[]{:S(2)}) collective-permute-start(bf16[2048,256]{1,0:T(8,128)(2,1)} %get-tuple-element.25), channel_id=1, source_target_pairs={{0,8},{1,65},{2,10},{3,67},{4,12},{5,69},{6,14},{7,71},{8,16},{9,7... | collective-permute-start | bytes 3145736 | tf_op jit(solution)/shard_map/ppermute | solution.py:195
  55.4 4.5 %collective-permute-start.5 = (bf16[2048,256]{1,0:T(8,128)(2,1)}, bf16[2048,256]{1,0:T(8,128)(2,1)}, u32[]{:S(2)}, u32[]{:S(2)}) collective-permute-start(bf16[2048,256]{1,0:T(8,128)(2,1)} %get-tuple-element.28), channel_id=1, source_target_pairs={{0,56},{1,449},{2,58},{3,451},{4,60},{5,453},{6,62},{7,455},{8,0},... | collective-permute-start | bytes 3145736 | tf_op jit(solution)/shard_map/ppermute | solution.py:195
  59.9 0.0 all-to-all-done.1
  59.9 0.0 copy-start.2
  59.9 1.9 %collective-permute-start.3 = (bf16[512,256]{1,0:T(8,128)(2,1)}, bf16[512,256]{1,0:T(8,128)(2,1)S(1)}, u32[]{:S(2)}, u32[]{:S(2)}) collective-permute-start(bf16[512,256]{1,0:T(8,128)(2,1)} %copy-done.1), channel_id=1, source_target_pairs={{0,16},{1,129},{2,18},{3,131},{4,20},{5,133},{6,22},{7,135},{8,24}... | collective-permute-start | bytes 786440 | tf_op jit(solution)/shard_map/ppermute | solution.py:195
  61.9 5.5 %collective-permute-start.4 = (bf16[512,256]{1,0:T(8,128)(2,1)}, bf16[512,256]{1,0:T(8,128)(2,1)S(1)}, u32[]{:S(2)}, u32[]{:S(2)}) collective-permute-start(bf16[512,256]{1,0:T(8,128)(2,1)} %copy-done), channel_id=1, source_target_pairs={{0,48},{1,385},{2,50},{3,387},{4,52},{5,389},{6,54},{7,391},{8,56}... | collective-permute-start | bytes 786440 | tf_op jit(solution)/shard_map/ppermute | solution.py:195
  67.3 2.1 %shard_map.75 = (f32[512,512]{1,0:T(8,128)S(1)}, s32[4,128]{1,0:T(4,128)S(1)}, f32[4,128]{1,0:T(4,128)S(1)}) custom-call(f32[32]{0:T(128)S(1)} %copy-done.2, bf16[512,896]{1,0:T(8,128)(2,1)S(1)} %bitcast.10), custom_call_target="tpu_custom_call" | custom-call | flops 536870912 | bytes 2097152 | tf_op jit(solution)/shard_map/pallas_call | solution.py:276
  69.5 4.5 %collective-permute-done.3.refs_3_ = bf16[512,256]{1,0:T(8,128)(2,1)S(1)} collective-permute-done((bf16[512,256]{1,0:T(8,128)(2,1)}, bf16[512,256]{1,0:T(8,128)(2,1)S(1)}, u32[]{:S(2)}, u32[]{:S(2)}) %collective-permute-start.3) | collective-permute-done | bytes 262176 | tf_op jit(solution)/shard_map/ppermute | solution.py:195
  73.9 3.6 %collective-permute-done.4.refs_4_ = bf16[512,256]{1,0:T(8,128)(2,1)S(1)} collective-permute-done((bf16[512,256]{1,0:T(8,128)(2,1)}, bf16[512,256]{1,0:T(8,128)(2,1)S(1)}, u32[]{:S(2)}, u32[]{:S(2)}) %collective-permute-start.4) | collective-permute-done | bytes 262176 | tf_op jit(solution)/shard_map/ppermute | solution.py:195
  77.6 0.0 collective-permute-done.2.refs_1_
  77.6 0.0 collective-permute-done.5.refs_5_
  77.6 4.4 %shard_map.76 = bf16[512,512]{1,0:T(8,128)(2,1)S(1)} custom-call(s32[4,128]{1,0:T(4,128)S(1)} %get-tuple-element.22.starts_ref, f32[4,128]{1,0:T(4,128)S(1)} %get-tuple-element.23.gates_ref, bf16[512,896]{1,0:T(8,128)(2,1)S(1)} %bitcast.11, f32[512,512]{1,0:T(8,128)S(1)} %get-tuple-element.24.local_ref, bf16[1024,256]{1,0:T(8,128)(2,1)S(1)} %bitcast.9, ...), custom_call_target="tpu_custom_call" | custom-call | flops 536870912 | bytes 7340032 | tf_op jit(solution)/shard_map/pallas_call | solution.py:290
  82.0 15.9 %all_to_all.16 = bf16[8,64,512]{2,1,0:T(8,128)(2,1)S(1)} all-to-all(bf16[8,64,512]{2,1,0:T(8,128)(2,1)S(1)} %bitcast.12), channel_id=1, replica_groups=mesh['mem'=64,'ctx'=8] {'ctx'}, dimensions={0} | all-to-all | bytes 1048576 | tf_op jit(solution)/shard_map/all_to_all | solution.py:306
  97.8 0.8 copy.9
  (3 shorter events, 0.0 us)
Async XLA Ops:
  22.3 22.4 %collective-permute-start.1 = (bf16[1024,256]{1,0:T(8,128)(2,1)S(1)}, bf16[1024,256]{1,0:T(8,128)(2,1)S(1)}, u32[]{:S(2)}, u32[]{:S(2)}) collective-permute-start(bf16[1024,256]{1,0:T(8,128)(2,1)S(1)} %bitcast.6), channel_id=1, source_target_pairs={{0,48},{1,385},{2,50},{3,387},{4,52},{5,389},{6,54},{7,391},{8,56}... | collective-permute-start | bytes 1572872 | tf_op jit(solution)/shard_map/ppermute | solution.py:195
  33.0 17.7 %collective-permute-start = (bf16[1024,256]{1,0:T(8,128)(2,1)S(1)}, bf16[1024,256]{1,0:T(8,128)(2,1)S(1)}, u32[]{:S(2)}, u32[]{:S(2)}) collective-permute-start(bf16[1024,256]{1,0:T(8,128)(2,1)S(1)} %bitcast.7), channel_id=1, source_target_pairs={{0,16},{1,129},{2,18},{3,131},{4,20},{5,133},{6,22},{7,135},{8,24}... | collective-permute-start | bytes 1572872 | tf_op jit(solution)/shard_map/ppermute | solution.py:195
  34.9 25.0 %all-to-all-start.1 = ((bf16[8,64,896]{2,1,0:T(8,128)(2,1)}), bf16[8,64,896]{2,1,0:T(8,128)(2,1)S(1)}, u32[]{:S(2)}, u32[]{:S(2)}) async-start(bf16[8,64,896]{2,1,0:T(8,128)(2,1)} %get-tuple-element.20), calls=%async_computation.1 | async-start | bytes 1835008 | tf_op jit(solution)/shard_map/all_to_all | solution.py:269
  52.0 0.7 copy-start
  52.7 0.7 copy-start.1
  53.4 24.2 %collective-permute-start.2 = (bf16[2048,256]{1,0:T(8,128)(2,1)}, bf16[2048,256]{1,0:T(8,128)(2,1)S(1)}, u32[]{:S(2)}, u32[]{:S(2)}) collective-permute-start(bf16[2048,256]{1,0:T(8,128)(2,1)} %get-tuple-element.25), channel_id=1, source_target_pairs={{0,8},{1,65},{2,10},{3,67},{4,12},{5,69},{6,14},{7,71},{8,16},{9,7... | collective-permute-start | bytes 3145736 | tf_op jit(solution)/shard_map/ppermute | solution.py:195
  55.4 22.1 %collective-permute-start.5 = (bf16[2048,256]{1,0:T(8,128)(2,1)}, bf16[2048,256]{1,0:T(8,128)(2,1)}, u32[]{:S(2)}, u32[]{:S(2)}) collective-permute-start(bf16[2048,256]{1,0:T(8,128)(2,1)} %get-tuple-element.28), channel_id=1, source_target_pairs={{0,56},{1,449},{2,58},{3,451},{4,60},{5,453},{6,62},{7,455},{8,0},... | collective-permute-start | bytes 3145736 | tf_op jit(solution)/shard_map/ppermute | solution.py:195
  59.9 7.4 %copy-start.2 = (f32[32]{0:T(128)S(1)}, f32[32]{0:T(128)}, u32[]{:S(2)}) copy-start(f32[32]{0:T(128)} %bias_ref.1) | copy-start | bytes 388
  59.9 14.0 %collective-permute-start.3 = (bf16[512,256]{1,0:T(8,128)(2,1)}, bf16[512,256]{1,0:T(8,128)(2,1)S(1)}, u32[]{:S(2)}, u32[]{:S(2)}) collective-permute-start(bf16[512,256]{1,0:T(8,128)(2,1)} %copy-done.1), channel_id=1, source_target_pairs={{0,16},{1,129},{2,18},{3,131},{4,20},{5,133},{6,22},{7,135},{8,24}... | collective-permute-start | bytes 786440 | tf_op jit(solution)/shard_map/ppermute | solution.py:195
  61.9 15.7 %collective-permute-start.4 = (bf16[512,256]{1,0:T(8,128)(2,1)}, bf16[512,256]{1,0:T(8,128)(2,1)S(1)}, u32[]{:S(2)}, u32[]{:S(2)}) collective-permute-start(bf16[512,256]{1,0:T(8,128)(2,1)} %copy-done), channel_id=1, source_target_pairs={{0,48},{1,385},{2,50},{3,387},{4,52},{5,389},{6,54},{7,391},{8,56}... | collective-permute-start | bytes 786440 | tf_op jit(solution)/shard_map/ppermute | solution.py:195

commit v8 on v6

--- a/solution.py
+++ b/solution.py
@@ -74,7 +74,11 @@
     return (back * SIDE + inner) * rows + slot * BLOCK
 
 
-def local_kernel(held, rows, qkv_ref, out_ref, starts_ref):
+def local_kernel(held, rows, bias_ref, qkv_ref, out_ref, starts_ref, gates_ref):
+    head = lax.axis_index("ctx")
+    for h in range(GROUPS):
+        bias = jnp.full((1, HEAD_DIM), bias_ref[head * GROUPS + h], jnp.float32)
+        gates_ref[h : h + 1, :] = jax.nn.sigmoid(bias)
     span = qkv_ref.shape[0]
     diagonal = lax.broadcasted_iota(jnp.int32, (TILE, HEAD_DIM), 0) == lax.broadcasted_iota(
         jnp.int32, (TILE, HEAD_DIM), 1
@@ -104,7 +108,7 @@
     return jnp.concatenate([store_ref[pl.ds(row, BLOCK), lanes] for row in rows], axis=0)
 
 
-def memory_kernel(starts_ref, bias_ref, qkv_ref, local_ref, *refs):
+def memory_kernel(starts_ref, gates_ref, qkv_ref, local_ref, *refs):
     chunks, (out_ref, store_ref, sems) = refs[:-3], refs[-3:]
     copies, row = [], 0
     for i, chunk in enumerate(chunks):
@@ -114,11 +118,7 @@
         )
         copies[-1].start()
         row += rows
-    head = lax.axis_index("ctx")
-    gates = [
-        jax.nn.sigmoid(jnp.full((1, HEAD_DIM), bias_ref[head * GROUPS + h], jnp.float32))
-        for h in range(GROUPS)
-    ]
+    gates = [gates_ref[h : h + 1, :] for h in range(GROUPS)]
     query_blocks = qkv_ref.shape[0] // QBLOCK
     for copy in copies:
         copy.wait()
@@ -224,33 +224,36 @@
         spread, BOTH, split_axis=0, concat_axis=0, tiled=True, axis_index_groups=first_groups()
     ).reshape(SIDE * rows, 2 * HEAD_DIM)
     chunks = gathered(chunk)
-    local_out, starts = pl.pallas_call(
+    local_out, starts, gates = pl.pallas_call(
         functools.partial(local_kernel, rows // BLOCK, rows),
         out_shape=(
             jax.ShapeDtypeStruct((span, LANES), jnp.float32),
             jax.ShapeDtypeStruct((span // TILE, TILE), jnp.int32),
-        ),
-        in_specs=[vmem],
-        out_specs=(vmem, vmem),
+            jax.ShapeDtypeStruct((GROUPS, HEAD_DIM), jnp.float32),
+        ),
+        in_specs=[smem, vmem],
+        out_specs=(vmem, vmem, vmem),
+        compiler_params=pltpu.CompilerParams(vmem_limit_bytes=12 << 20),
         cost_estimate=pl.CostEstimate(
             flops=4 * span * LANES * span, bytes_accessed=2 << 20, transcendentals=span * span * 4
         ),
-    )(qkv)
+    )(gate_bias, qkv)
     mixed = pl.pallas_call(
         memory_kernel,
         out_shape=jax.ShapeDtypeStruct((span, LANES), jnp.bfloat16),
-        in_specs=[smem, smem, vmem, vmem] + [hbm] * len(chunks),
+        in_specs=[smem, vmem, vmem, vmem] + [hbm] * len(chunks),
         out_specs=vmem,
         scratch_shapes=[
             pltpu.VMEM((SIDE * SIDE * rows, 2 * HEAD_DIM), jnp.bfloat16),
             pltpu.SemaphoreType.DMA((len(chunks),)),
         ],
+        compiler_params=pltpu.CompilerParams(vmem_limit_bytes=32 << 20),
         cost_estimate=pl.CostEstimate(
             flops=4 * span * LANES * TOPB * BLOCK,
             bytes_accessed=7 << 20,
             transcendentals=span * GROUPS * TOPB * BLOCK,
         ),
-    )(starts, gate_bias, qkv, local_out, *chunks)
+    )(starts, gates, qkv, local_out, *chunks)
     back = lax.all_to_all(
         mixed.reshape(members, tokens, LANES), "ctx", split_axis=0, concat_axis=0, tiled=True
     )

time: 95.1 us -> 92.5 us (0.973)
  Pallas kernels: 13.1 us -> 9.09 us
  waiting for transfers between devices: 8.39 us -> 11 us
  local copies, waits for them, and re-layouts: 3.27 us -> 2.27 us
    ppermute x8, waiting for transfers between devices: 8.39 us -> 11 us  [shifted(): return lax.ppermute(value, BOTH, pairs)]
    pallas_call x1, Pallas kernels: 6.8 us -> 4.46 us  [body(): pl.pallas_call(memory_kernel, out_shape=jax.ShapeDtypeStruct((span, LANES...]
    pallas_call x1, Pallas kernels: 3.74 us -> 2.11 us  [body(): pl.pallas_call(functools.partial(local_kernel, rows // BLOCK, rows), out_...]
    unnamed x12 -> x2, local copies, waits for them, and re-layouts: 0.98 us -> 0.01 us
  transfers between devices with their start and end apart: 9 -> 9, of which waited for: 2 -> 3; matrix products, arithmetic and copies ran while one was open for 2% -> 2% of each run, Pallas kernels for 4% -> 2%
where the time goes in v8:
time: 92.5 us; the launch traced here: 91.9 us
  blocking collectives  38 us (41%)
  starting transfers between devices  31.4 us (34%)
  waiting for transfers between devices  11 us (12%)
  Pallas kernels  9.09 us (10%)
  local copies, waits for them, and re-layouts  2.27 us (2%)
    ppermute x8, starting transfers between devices, shifted(): return lax.ppermute(value, BOTH, pairs)  27.1 us
    all_to_all x1, blocking collectives, body(): lax.all_to_all(spread, BOTH, split_axis=0, concat_axis=0, tiled=True, axi...  23.6 us
    all_to_all x1, blocking collectives, body(): lax.all_to_all(mixed.reshape(members, tokens, LANES), 'ctx', split_axis=0...  14.4 us
    ppermute x8, waiting for transfers between devices, shifted(): return lax.ppermute(value, BOTH, pairs)  11 us
    pallas_call x1, Pallas kernels, body(): pl.pallas_call(memory_kernel, out_shape=jax.ShapeDtypeStruct((span, LANES...  4.46 us
    all_to_all x1, starting transfers between devices, body(): qkv = lax.all_to_all(packed, 'ctx', split_axis=0, concat_axis=0, tiled=True)  4.31 us
    pallas_call x1, Pallas kernels, body(): pl.pallas_call(pack_kernel, out_shape=(jax.ShapeDtypeStruct((members, tok...  2.52 us
    pallas_call x1, Pallas kernels, body(): pl.pallas_call(functools.partial(local_kernel, rows // BLOCK, rows), out_...  2.11 us
  transfers between devices with their start and end apart: 9, of which 3 were waited for; matrix products, arithmetic and copies ran while one was open for 2% of the time, Pallas kernels for 2%

profile of v8, /device:TPU:8, one launch (start us, length us, event | category | flops | bytes accessed | tf_op | source)
XLA Modules:
  0.0 91.9 jit_solution(17105413776521126235)
XLA Ops:
  0.0 2.5 %shard_map.73 = (bf16[8,64,896]{2,1,0:T(8,128)(2,1)}, bf16[8,128,256]{2,1,0:T(8,128)(2,1)}) custom-call(s32[4,16]{1,0:T(4,128)} %ids_ref.1, bf16[64,4096]{1,0:T(8,128)(2,1)} %queries_ref.1, bf16[64,1024]{1,0:T(8,128)(2,1)} %keys_ref.1, bf16[64,1024]{1,0:T(8,128)(2,1)} %values_ref.1, bf16[128,1024]{1,0:T(8,128)(2,1)} %mem_keys_ref.1, ...), custom_call_target="tpu_custom_call" | custom-call | bytes 4194304 | tf_op jit(solution)/shard_map/pallas_call | solution.py:210
  2.5 23.6 %all_to_all.15 = bf16[8,128,256]{2,1,0:T(8,128)(2,1)S(1)} all-to-all(bf16[8,128,256]{2,1,0:T(8,128)(2,1)} %get-tuple-element.14), channel_id=1, replica_groups={{0,64,128,192,256,320,384,448},{8,72,136,200,264,328,392,456},{16,80,14..., dimensions={0} | all-to-all | bytes 1048576 | tf_op jit(solution)/shard_map/all_to_all | solution.py:223
  26.1 5.3 %collective-permute-start.4 = (bf16[1024,256]{1,0:T(8,128)(2,1)S(1)}, bf16[1024,256]{1,0:T(8,128)(2,1)S(1)}, u32[]{:S(2)}, u32[]{:S(2)}) collective-permute-start(bf16[1024,256]{1,0:T(8,128)(2,1)S(1)} %bitcast.8), channel_id=1, source_target_pairs={{0,48},{1,385},{2,50},{3,387},{4,52},{5,389},{6,54},{7,391},{8,56}... | collective-permute-start | bytes 1572872 | tf_op jit(solution)/shard_map/ppermute | solution.py:190
  31.4 1.9 %collective-permute-start.1 = (bf16[1024,256]{1,0:T(8,128)(2,1)S(1)}, bf16[1024,256]{1,0:T(8,128)(2,1)S(1)}, u32[]{:S(2)}, u32[]{:S(2)}) collective-permute-start(bf16[1024,256]{1,0:T(8,128)(2,1)S(1)} %bitcast.9), channel_id=1, source_target_pairs={{0,16},{1,129},{2,18},{3,131},{4,20},{5,133},{6,22},{7,135},{8,24}... | collective-permute-start | bytes 1572872 | tf_op jit(solution)/shard_map/ppermute | solution.py:190
  33.3 4.3 %all-to-all-start = ((bf16[8,64,896]{2,1,0:T(8,128)(2,1)}), bf16[8,64,896]{2,1,0:T(8,128)(2,1)S(1)}, u32[]{:S(2)}, u32[]{:S(2)}) async-start(bf16[8,64,896]{2,1,0:T(8,128)(2,1)} %get-tuple-element.10), calls=%async_computation | async-start | bytes 1835008 | tf_op jit(solution)/shard_map/all_to_all | solution.py:221
  37.6 3.2 %collective-permute-start.7 = (bf16[1024,256]{1,0:T(8,128)(2,1)S(1)}, bf16[1024,256]{1,0:T(8,128)(2,1)S(1)}, u32[]{:S(2)}, u32[]{:S(2)}) collective-permute-start(bf16[1024,256]{1,0:T(8,128)(2,1)S(1)} %bitcast.10), channel_id=1, source_target_pairs={{0,56},{1,449},{2,58},{3,451},{4,60},{5,453},{6,62},{7,455},{8,0},... | collective-permute-start | bytes 1572872 | tf_op jit(solution)/shard_map/ppermute | solution.py:190
  40.9 2.9 %collective-permute-start = (bf16[1024,256]{1,0:T(8,128)(2,1)S(1)}, bf16[1024,256]{1,0:T(8,128)(2,1)S(1)}, u32[]{:S(2)}, u32[]{:S(2)}) collective-permute-start(bf16[1024,256]{1,0:T(8,128)(2,1)S(1)} %bitcast.11), channel_id=1, source_target_pairs={{0,8},{1,65},{2,10},{3,67},{4,12},{5,69},{6,14},{7,71},{8,16},{9,7... | collective-permute-start | bytes 1572872 | tf_op jit(solution)/shard_map/ppermute | solution.py:190
  43.8 0.0 collective-permute-done.4.refs_7_
  43.8 4.3 %collective-permute-start.6 = (bf16[1024,256]{1,0:T(8,128)(2,1)S(1)}, bf16[1024,256]{1,0:T(8,128)(2,1)}, u32[]{:S(2)}, u32[]{:S(2)}) collective-permute-start(bf16[1024,256]{1,0:T(8,128)(2,1)S(1)} %collective-permute-done.4.refs_7_), channel_id=1, source_target_pairs={{0,56},{1,449},{2,58},{3,451},{4,60},{5,453},{6,62},{7,455},{8,0},... | collective-permute-start | bytes 1572872 | tf_op jit(solution)/shard_map/ppermute | solution.py:190
  48.1 2.2 %collective-permute-done.1.refs_2_ = bf16[1024,256]{1,0:T(8,128)(2,1)S(1)} collective-permute-done((bf16[1024,256]{1,0:T(8,128)(2,1)S(1)}, bf16[1024,256]{1,0:T(8,128)(2,1)S(1)}, u32[]{:S(2)}, u32[]{:S(2)}) %collective-permute-start.1) | collective-permute-done | bytes 524320 | tf_op jit(solution)/shard_map/ppermute | solution.py:190
  50.3 1.9 %collective-permute-start.2 = (bf16[1024,256]{1,0:T(8,128)(2,1)S(1)}, bf16[1024,256]{1,0:T(8,128)(2,1)}, u32[]{:S(2)}, u32[]{:S(2)}) collective-permute-start(bf16[1024,256]{1,0:T(8,128)(2,1)S(1)} %collective-permute-done.1.refs_2_), channel_id=1, source_target_pairs={{0,8},{1,65},{2,10},{3,67},{4,12},{5,69},{6,14},{7,71},{8,16},{9,7... | collective-permute-start | bytes 1572872 | tf_op jit(solution)/shard_map/ppermute | solution.py:190
  52.2 0.7 slice.9
  52.9 5.6 %collective-permute-start.5 = (bf16[512,256]{1,0:T(8,128)(2,1)}, bf16[512,256]{1,0:T(8,128)(2,1)}, u32[]{:S(2)}, u32[]{:S(2)}) collective-permute-start(bf16[512,256]{1,0:T(8,128)(2,1)} %slice.9), channel_id=1, source_target_pairs={{0,48},{1,385},{2,50},{3,387},{4,52},{5,389},{6,54},{7,391},{8,56}... | collective-permute-start | bytes 786440 | tf_op jit(solution)/shard_map/ppermute | solution.py:190
  58.5 0.7 slice.8
  59.2 0.0 collective-permute-done.7.refs_8_
  59.2 2.0 %collective-permute-start.3 = (bf16[512,256]{1,0:T(8,128)(2,1)}, bf16[512,256]{1,0:T(8,128)(2,1)}, u32[]{:S(2)}, u32[]{:S(2)}) collective-permute-start(bf16[512,256]{1,0:T(8,128)(2,1)} %slice.8), channel_id=1, source_target_pairs={{0,16},{1,129},{2,18},{3,131},{4,20},{5,133},{6,22},{7,135},{8,24}... | collective-permute-start | bytes 786440 | tf_op jit(solution)/shard_map/ppermute | solution.py:190
  61.3 0.0 all-to-all-done
  61.3 2.1 %shard_map.74 = (f32[512,512]{1,0:T(8,128)S(1)}, s32[4,128]{1,0:T(4,128)S(1)}, f32[4,128]{1,0:T(4,128)S(1)}) custom-call(f32[32]{0:T(128)S(1)} %copy-done, bf16[512,896]{1,0:T(8,128)(2,1)S(1)} %bitcast.6), custom_call_target="tpu_custom_call" | custom-call | flops 536870912 | bytes 2097152 | tf_op jit(solution)/shard_map/pallas_call | solution.py:227
  63.4 0.0 collective-permute-done.refs_1_
  63.4 1.8 %collective-permute-done.5.refs_5_ = bf16[512,256]{1,0:T(8,128)(2,1)} collective-permute-done((bf16[512,256]{1,0:T(8,128)(2,1)}, bf16[512,256]{1,0:T(8,128)(2,1)}, u32[]{:S(2)}, u32[]{:S(2)}) %collective-permute-start.5) | collective-permute-done | bytes 262176 | tf_op jit(solution)/shard_map/ppermute | solution.py:190
  65.3 7.0 %collective-permute-done.3.refs_4_ = bf16[512,256]{1,0:T(8,128)(2,1)} collective-permute-done((bf16[512,256]{1,0:T(8,128)(2,1)}, bf16[512,256]{1,0:T(8,128)(2,1)}, u32[]{:S(2)}, u32[]{:S(2)}) %collective-permute-start.3) | collective-permute-done | bytes 262176 | tf_op jit(solution)/shard_map/ppermute | solution.py:190
  72.2 4.5 %shard_map.75 = bf16[512,512]{1,0:T(8,128)(2,1)S(1)} custom-call(s32[4,128]{1,0:T(4,128)S(1)} %get-tuple-element.11.starts_ref, f32[4,128]{1,0:T(4,128)S(1)} %get-tuple-element.12.gates_ref, bf16[512,896]{1,0:T(8,128)(2,1)S(1)} %bitcast.7, f32[512,512]{1,0:T(8,128)S(1)} %get-tuple-element.13.local_ref, bf16[1024,256]{1,0:T(8,128)(2,1)S(1)} %bitcast.12, ...), custom_call_target="tpu_custom_call" | custom-call | flops 536870912 | bytes 7340032 | tf_op jit(solution)/shard_map/pallas_call | solution.py:241
  76.7 14.4 %all_to_all.16 = bf16[8,64,512]{2,1,0:T(8,128)(2,1)S(1)} all-to-all(bf16[8,64,512]{2,1,0:T(8,128)(2,1)S(1)} %bitcast.13), channel_id=1, replica_groups=mesh['mem'=64,'ctx'=8] {'ctx'}, dimensions={0} | all-to-all | bytes 1048576 | tf_op jit(solution)/shard_map/all_to_all | solution.py:257
  91.1 0.8 copy.9
  (4 shorter events, 0.0 us)
Async XLA Ops:
  26.1 17.7 %collective-permute-start.4 = (bf16[1024,256]{1,0:T(8,128)(2,1)S(1)}, bf16[1024,256]{1,0:T(8,128)(2,1)S(1)}, u32[]{:S(2)}, u32[]{:S(2)}) collective-permute-start(bf16[1024,256]{1,0:T(8,128)(2,1)S(1)} %bitcast.8), channel_id=1, source_target_pairs={{0,48},{1,385},{2,50},{3,387},{4,52},{5,389},{6,54},{7,391},{8,56}... | collective-permute-start | bytes 1572872 | tf_op jit(solution)/shard_map/ppermute | solution.py:190
  31.4 18.9 %collective-permute-start.1 = (bf16[1024,256]{1,0:T(8,128)(2,1)S(1)}, bf16[1024,256]{1,0:T(8,128)(2,1)S(1)}, u32[]{:S(2)}, u32[]{:S(2)}) collective-permute-start(bf16[1024,256]{1,0:T(8,128)(2,1)S(1)} %bitcast.9), channel_id=1, source_target_pairs={{0,16},{1,129},{2,18},{3,131},{4,20},{5,133},{6,22},{7,135},{8,24}... | collective-permute-start | bytes 1572872 | tf_op jit(solution)/shard_map/ppermute | solution.py:190
  33.3 28.0 %all-to-all-start = ((bf16[8,64,896]{2,1,0:T(8,128)(2,1)}), bf16[8,64,896]{2,1,0:T(8,128)(2,1)S(1)}, u32[]{:S(2)}, u32[]{:S(2)}) async-start(bf16[8,64,896]{2,1,0:T(8,128)(2,1)} %get-tuple-element.10), calls=%async_computation | async-start | bytes 1835008 | tf_op jit(solution)/shard_map/all_to_all | solution.py:221
  37.6 21.6 %collective-permute-start.7 = (bf16[1024,256]{1,0:T(8,128)(2,1)S(1)}, bf16[1024,256]{1,0:T(8,128)(2,1)S(1)}, u32[]{:S(2)}, u32[]{:S(2)}) collective-permute-start(bf16[1024,256]{1,0:T(8,128)(2,1)S(1)} %bitcast.10), channel_id=1, source_target_pairs={{0,56},{1,449},{2,58},{3,451},{4,60},{5,453},{6,62},{7,455},{8,0},... | collective-permute-start | bytes 1572872 | tf_op jit(solution)/shard_map/ppermute | solution.py:190
  40.9 22.6 %collective-permute-start = (bf16[1024,256]{1,0:T(8,128)(2,1)S(1)}, bf16[1024,256]{1,0:T(8,128)(2,1)S(1)}, u32[]{:S(2)}, u32[]{:S(2)}) collective-permute-start(bf16[1024,256]{1,0:T(8,128)(2,1)S(1)} %bitcast.11), channel_id=1, source_target_pairs={{0,8},{1,65},{2,10},{3,67},{4,12},{5,69},{6,14},{7,71},{8,16},{9,7... | collective-permute-start | bytes 1572872 | tf_op jit(solution)/shard_map/ppermute | solution.py:190
  43.8 28.4 %collective-permute-start.6 = (bf16[1024,256]{1,0:T(8,128)(2,1)S(1)}, bf16[1024,256]{1,0:T(8,128)(2,1)}, u32[]{:S(2)}, u32[]{:S(2)}) collective-permute-start(bf16[1024,256]{1,0:T(8,128)(2,1)S(1)} %collective-permute-done.4.refs_7_), channel_id=1, source_target_pairs={{0,56},{1,449},{2,58},{3,451},{4,60},{5,453},{6,62},{7,455},{8,0},... | collective-permute-start | bytes 1572872 | tf_op jit(solution)/shard_map/ppermute | solution.py:190
  50.3 21.9 %collective-permute-start.2 = (bf16[1024,256]{1,0:T(8,128)(2,1)S(1)}, bf16[1024,256]{1,0:T(8,128)(2,1)}, u32[]{:S(2)}, u32[]{:S(2)}) collective-permute-start(bf16[1024,256]{1,0:T(8,128)(2,1)S(1)} %collective-permute-done.1.refs_2_), channel_id=1, source_target_pairs={{0,8},{1,65},{2,10},{3,67},{4,12},{5,69},{6,14},{7,71},{8,16},{9,7... | collective-permute-start | bytes 1572872 | tf_op jit(solution)/shard_map/ppermute | solution.py:190
  52.9 12.3 %collective-permute-start.5 = (bf16[512,256]{1,0:T(8,128)(2,1)}, bf16[512,256]{1,0:T(8,128)(2,1)}, u32[]{:S(2)}, u32[]{:S(2)}) collective-permute-start(bf16[512,256]{1,0:T(8,128)(2,1)} %slice.9), channel_id=1, source_target_pairs={{0,48},{1,385},{2,50},{3,387},{4,52},{5,389},{6,54},{7,391},{8,56}... | collective-permute-start | bytes 786440 | tf_op jit(solution)/shard_map/ppermute | solution.py:190
  59.2 2.1 %copy-start = (f32[32]{0:T(128)S(1)}, f32[32]{0:T(128)}, u32[]{:S(2)}) copy-start(f32[32]{0:T(128)} %bias_ref.1) | copy-start | bytes 388
  59.2 13.0 %collective-permute-start.3 = (bf16[512,256]{1,0:T(8,128)(2,1)}, bf16[512,256]{1,0:T(8,128)(2,1)}, u32[]{:S(2)}, u32[]{:S(2)}) collective-permute-start(bf16[512,256]{1,0:T(8,128)(2,1)} %slice.8), channel_id=1, source_target_pairs={{0,16},{1,129},{2,18},{3,131},{4,20},{5,133},{6,22},{7,135},{8,24}... | collective-permute-start | bytes 786440 | tf_op jit(solution)/shard_map/ppermute | solution.py:190

commit v9 on v8

--- a/solution.py
+++ b/solution.py
@@ -177,26 +177,35 @@
     return groups
 
 
-def shifted(value, step):
+def moved(value, target):
     pairs = []
     for z in range(SIDE):
         for y in range(SIDE):
             for ctx in range(CTX):
                 if ring_of(ctx) == 0:
-                    target = device(z, (y + step) % SIDE, ctx)
+                    to = device(z, target(y) % SIDE, ctx)
                 else:
-                    target = device((z + step) % SIDE, y, ctx)
-                pairs.append((device(z, y, ctx), target))
+                    to = device(target(z) % SIDE, y, ctx)
+                pairs.append((device(z, y, ctx), to))
     return lax.ppermute(value, BOTH, pairs)
+
+
+def shifted(value, step):
+    return moved(value, lambda place: place + step)
+
+
+def ring_place():
+    mem = lax.axis_index("mem")
+    return jnp.where(lax.axis_index("ctx") % 2 == 0, mem % SIDE, mem // SIDE)
 
 
 def gathered(chunk):
     ahead2, behind2 = shifted(chunk, 2), shifted(chunk, -2)
     ahead1, behind1 = shifted(chunk, 1), shifted(chunk, -1)
     ahead3, behind3 = shifted(ahead2, 1), shifted(behind2, -1)
-    half = chunk.shape[0] // 2
-    ahead4, behind4 = shifted(ahead2[:half], 2), shifted(behind2[half:], -2)
-    return [chunk, ahead1, ahead2, ahead3, ahead4, behind4, behind3, behind2, behind1]
+    onward = jnp.where(ring_place() % 2 == 0, ahead2, behind2)
+    far = moved(onward, lambda place: place + 2 if place % 2 == 0 else place - 2)
+    return [chunk, ahead1, ahead2, ahead3, far, behind3, behind2, behind1]
 
 
 def body(queries, local_keys, local_values, mem_keys, mem_values, block_ids, gate_bias):

time: 92.5 us -> 92.2 us (level)
  the two profiles are of different devices: /device:TPU:8 before, /device:TPU:1 now
where the time goes in v9:
time: 92.2 us; the launch traced here: 91.7 us
  blocking collectives  35.6 us (39%)
  starting transfers between devices  34.1 us (37%)
  waiting for transfers between devices  11.1 us (12%)
  Pallas kernels  9.09 us (10%)
    ppermute x7, starting transfers between devices, moved(): return lax.ppermute(value, BOTH, pairs)  29 us
    all_to_all x1, blocking collectives, body(): lax.all_to_all(spread, BOTH, split_axis=0, concat_axis=0, tiled=True, axi...  19.8 us
    all_to_all x1, blocking collectives, body(): lax.all_to_all(mixed.reshape(members, tokens, LANES), 'ctx', split_axis=0...  15.8 us
    ppermute x7, waiting for transfers between devices, moved(): return lax.ppermute(value, BOTH, pairs)  11.1 us
    all_to_all x1, starting transfers between devices, body(): qkv = lax.all_to_all(packed, 'ctx', split_axis=0, concat_axis=0, tiled=True)  5.13 us
    pallas_call x1, Pallas kernels, body(): pl.pallas_call(memory_kernel, out_shape=jax.ShapeDtypeStruct((span, LANES...  4.46 us
    pallas_call x1, Pallas kernels, body(): pl.pallas_call(pack_kernel, out_shape=(jax.ShapeDtypeStruct((members, tok...  2.52 us
    pallas_call x1, Pallas kernels, body(): pl.pallas_call(functools.partial(local_kernel, rows // BLOCK, rows), out_...  2.11 us
  transfers between devices with their start and end apart: 8, of which 3 were waited for; matrix products, arithmetic and copies ran while one was open for 1% of the time, Pallas kernels for 2%

profile of v9, /device:TPU:1, one launch (start us, length us, event | category | flops | bytes accessed | tf_op | source)
XLA Modules:
  0.0 91.7 jit_solution(5482380425159011989)
XLA Ops:
  0.0 2.5 %shard_map.73 = (bf16[8,64,896]{2,1,0:T(8,128)(2,1)}, bf16[8,128,256]{2,1,0:T(8,128)(2,1)}) custom-call(s32[4,16]{1,0:T(4,128)} %ids_ref.1, bf16[64,4096]{1,0:T(8,128)(2,1)} %queries_ref.1, bf16[64,1024]{1,0:T(8,128)(2,1)} %keys_ref.1, bf16[64,1024]{1,0:T(8,128)(2,1)} %values_ref.1, bf16[128,1024]{1,0:T(8,128)(2,1)} %mem_keys_ref.1, ...), custom_call_target="tpu_custom_call" | custom-call | bytes 4194304 | tf_op jit(solution)/shard_map/pallas_call | solution.py:219
  2.5 19.8 %all_to_all.15 = bf16[8,128,256]{2,1,0:T(8,128)(2,1)S(1)} all-to-all(bf16[8,128,256]{2,1,0:T(8,128)(2,1)} %get-tuple-element.14), channel_id=1, replica_groups={{0,64,128,192,256,320,384,448},{8,72,136,200,264,328,392,456},{16,80,14..., dimensions={0} | all-to-all | bytes 1048576 | tf_op jit(solution)/shard_map/all_to_all | solution.py:232
  22.3 10.6 %collective-permute-start.3 = (bf16[1024,256]{1,0:T(8,128)(2,1)S(1)}, bf16[1024,256]{1,0:T(8,128)(2,1)S(1)}, u32[]{:S(2)}, u32[]{:S(2)}) collective-permute-start(bf16[1024,256]{1,0:T(8,128)(2,1)S(1)} %bitcast.8), channel_id=1, source_target_pairs={{0,48},{1,385},{2,50},{3,387},{4,52},{5,389},{6,54},{7,391},{8,56}... | collective-permute-start | bytes 1572872 | tf_op jit(solution)/shard_map/ppermute | solution.py:190
  33.0 1.9 %collective-permute-start.1 = (bf16[1024,256]{1,0:T(8,128)(2,1)S(1)}, bf16[1024,256]{1,0:T(8,128)(2,1)S(1)}, u32[]{:S(2)}, u32[]{:S(2)}) collective-permute-start(bf16[1024,256]{1,0:T(8,128)(2,1)S(1)} %bitcast.9), channel_id=1, source_target_pairs={{0,16},{1,129},{2,18},{3,131},{4,20},{5,133},{6,22},{7,135},{8,24}... | collective-permute-start | bytes 1572872 | tf_op jit(solution)/shard_map/ppermute | solution.py:190
  34.9 5.1 %all-to-all-start = ((bf16[8,64,896]{2,1,0:T(8,128)(2,1)}), bf16[8,64,896]{2,1,0:T(8,128)(2,1)S(1)}, u32[]{:S(2)}, u32[]{:S(2)}) async-start(bf16[8,64,896]{2,1,0:T(8,128)(2,1)} %get-tuple-element.10), calls=%async_computation | async-start | bytes 1835008 | tf_op jit(solution)/shard_map/all_to_all | solution.py:230
  40.0 4.8 %collective-permute-start.6 = (bf16[1024,256]{1,0:T(8,128)(2,1)S(1)}, bf16[1024,256]{1,0:T(8,128)(2,1)S(1)}, u32[]{:S(2)}, u32[]{:S(2)}) collective-permute-start(bf16[1024,256]{1,0:T(8,128)(2,1)S(1)} %bitcast.10), channel_id=1, source_target_pairs={{0,56},{1,449},{2,58},{3,451},{4,60},{5,453},{6,62},{7,455},{8,0},... | collective-permute-start | bytes 1572872 | tf_op jit(solution)/shard_map/ppermute | solution.py:190
  44.8 1.9 %collective-permute-start = (bf16[1024,256]{1,0:T(8,128)(2,1)S(1)}, bf16[1024,256]{1,0:T(8,128)(2,1)S(1)}, u32[]{:S(2)}, u32[]{:S(2)}) collective-permute-start(bf16[1024,256]{1,0:T(8,128)(2,1)S(1)} %bitcast.11), channel_id=1, source_target_pairs={{0,8},{1,65},{2,10},{3,67},{4,12},{5,69},{6,14},{7,71},{8,16},{9,7... | collective-permute-start | bytes 1572872 | tf_op jit(solution)/shard_map/ppermute | solution.py:190
  46.7 0.0 collective-permute-done.3.refs_6_
  46.7 4.6 %collective-permute-start.5 = (bf16[1024,256]{1,0:T(8,128)(2,1)S(1)}, bf16[1024,256]{1,0:T(8,128)(2,1)}, u32[]{:S(2)}, u32[]{:S(2)}) collective-permute-start(bf16[1024,256]{1,0:T(8,128)(2,1)S(1)} %collective-permute-done.3.refs_6_), channel_id=1, source_target_pairs={{0,56},{1,449},{2,58},{3,451},{4,60},{5,453},{6,62},{7,455},{8,0},... | collective-permute-start | bytes 1572872 | tf_op jit(solution)/shard_map/ppermute | solution.py:190
  51.3 0.0 collective-permute-done.1.refs_2_
  51.3 0.9 broadcast_select_fusion
  52.2 2.0 %collective-permute-start.4 = (bf16[1024,256]{1,0:T(8,128)(2,1)}, bf16[1024,256]{1,0:T(8,128)(2,1)}, u32[]{:S(2)}, u32[]{:S(2)}) collective-permute-start(bf16[1024,256]{1,0:T(8,128)(2,1)} %broadcast_select_fusion), channel_id=1, source_target_pairs={{0,16},{1,129},{2,18},{3,131},{4,20},{5,133},{6,22},{7,135},{8,56}... | collective-permute-start | bytes 1572872 | tf_op jit(solution)/shard_map/ppermute | solution.py:190
  54.2 3.1 %collective-permute-start.2 = (bf16[1024,256]{1,0:T(8,128)(2,1)S(1)}, bf16[1024,256]{1,0:T(8,128)(2,1)}, u32[]{:S(2)}, u32[]{:S(2)}) collective-permute-start(bf16[1024,256]{1,0:T(8,128)(2,1)S(1)} %collective-permute-done.1.refs_2_), channel_id=1, source_target_pairs={{0,8},{1,65},{2,10},{3,67},{4,12},{5,69},{6,14},{7,71},{8,16},{9,7... | collective-permute-start | bytes 1572872 | tf_op jit(solution)/shard_map/ppermute | solution.py:190
  57.3 0.0 all-to-all-done
  57.3 0.0 copy-done
  57.4 2.1 %shard_map.74 = (f32[512,512]{1,0:T(8,128)S(1)}, s32[4,128]{1,0:T(4,128)S(1)}, f32[4,128]{1,0:T(4,128)S(1)}) custom-call(f32[32]{0:T(128)S(1)} %copy-done, bf16[512,896]{1,0:T(8,128)(2,1)S(1)} %bitcast.6), custom_call_target="tpu_custom_call" | custom-call | flops 536870912 | bytes 2097152 | tf_op jit(solution)/shard_map/pallas_call | solution.py:236
  59.5 0.0 collective-permute-done.6.refs_7_
  59.5 0.0 collective-permute-done.refs_1_
  59.5 3.6 %collective-permute-done.5.refs_5_ = bf16[1024,256]{1,0:T(8,128)(2,1)} collective-permute-done((bf16[1024,256]{1,0:T(8,128)(2,1)S(1)}, bf16[1024,256]{1,0:T(8,128)(2,1)}, u32[]{:S(2)}, u32[]{:S(2)}) %collective-permute-start.5) | collective-permute-done | bytes 524320 | tf_op jit(solution)/shard_map/ppermute | solution.py:190
  63.0 2.0 %collective-permute-done.4.refs_4_ = bf16[1024,256]{1,0:T(8,128)(2,1)} collective-permute-done((bf16[1024,256]{1,0:T(8,128)(2,1)}, bf16[1024,256]{1,0:T(8,128)(2,1)}, u32[]{:S(2)}, u32[]{:S(2)}) %collective-permute-start.4) | collective-permute-done | bytes 524320 | tf_op jit(solution)/shard_map/ppermute | solution.py:190
  65.0 5.6 %collective-permute-done.2.refs_3_ = bf16[1024,256]{1,0:T(8,128)(2,1)} collective-permute-done((bf16[1024,256]{1,0:T(8,128)(2,1)S(1)}, bf16[1024,256]{1,0:T(8,128)(2,1)}, u32[]{:S(2)}, u32[]{:S(2)}) %collective-permute-start.2) | collective-permute-done | bytes 524320 | tf_op jit(solution)/shard_map/ppermute | solution.py:190
  70.6 4.5 %shard_map.75 = bf16[512,512]{1,0:T(8,128)(2,1)S(1)} custom-call(s32[4,128]{1,0:T(4,128)S(1)} %get-tuple-element.11.starts_ref, f32[4,128]{1,0:T(4,128)S(1)} %get-tuple-element.12.gates_ref, bf16[512,896]{1,0:T(8,128)(2,1)S(1)} %bitcast.7, f32[512,512]{1,0:T(8,128)S(1)} %get-tuple-element.13.local_ref, bf16[1024,256]{1,0:T(8,128)(2,1)S(1)} %bitcast.12, ...), custom_call_target="tpu_custom_call" | custom-call | flops 536870912 | bytes 7340032 | tf_op jit(solution)/shard_map/pallas_call | solution.py:250
  75.0 15.8 %all_to_all.16 = bf16[8,64,512]{2,1,0:T(8,128)(2,1)S(1)} all-to-all(bf16[8,64,512]{2,1,0:T(8,128)(2,1)S(1)} %bitcast.13), channel_id=1, replica_groups=mesh['mem'=64,'ctx'=8] {'ctx'}, dimensions={0} | all-to-all | bytes 1048576 | tf_op jit(solution)/shard_map/all_to_all | solution.py:266
  90.9 0.8 copy.9
  (1 shorter events, 0.0 us)
Async XLA Ops:
  22.3 24.4 %collective-permute-start.3 = (bf16[1024,256]{1,0:T(8,128)(2,1)S(1)}, bf16[1024,256]{1,0:T(8,128)(2,1)S(1)}, u32[]{:S(2)}, u32[]{:S(2)}) collective-permute-start(bf16[1024,256]{1,0:T(8,128)(2,1)S(1)} %bitcast.8), channel_id=1, source_target_pairs={{0,48},{1,385},{2,50},{3,387},{4,52},{5,389},{6,54},{7,391},{8,56}... | collective-permute-start | bytes 1572872 | tf_op jit(solution)/shard_map/ppermute | solution.py:190
  33.0 18.4 %collective-permute-start.1 = (bf16[1024,256]{1,0:T(8,128)(2,1)S(1)}, bf16[1024,256]{1,0:T(8,128)(2,1)S(1)}, u32[]{:S(2)}, u32[]{:S(2)}) collective-permute-start(bf16[1024,256]{1,0:T(8,128)(2,1)S(1)} %bitcast.9), channel_id=1, source_target_pairs={{0,16},{1,129},{2,18},{3,131},{4,20},{5,133},{6,22},{7,135},{8,24}... | collective-permute-start | bytes 1572872 | tf_op jit(solution)/shard_map/ppermute | solution.py:190
  34.9 22.4 %all-to-all-start = ((bf16[8,64,896]{2,1,0:T(8,128)(2,1)}), bf16[8,64,896]{2,1,0:T(8,128)(2,1)S(1)}, u32[]{:S(2)}, u32[]{:S(2)}) async-start(bf16[8,64,896]{2,1,0:T(8,128)(2,1)} %get-tuple-element.10), calls=%async_computation | async-start | bytes 1835008 | tf_op jit(solution)/shard_map/all_to_all | solution.py:230
  40.0 19.4 %collective-permute-start.6 = (bf16[1024,256]{1,0:T(8,128)(2,1)S(1)}, bf16[1024,256]{1,0:T(8,128)(2,1)S(1)}, u32[]{:S(2)}, u32[]{:S(2)}) collective-permute-start(bf16[1024,256]{1,0:T(8,128)(2,1)S(1)} %bitcast.10), channel_id=1, source_target_pairs={{0,56},{1,449},{2,58},{3,451},{4,60},{5,453},{6,62},{7,455},{8,0},... | collective-permute-start | bytes 1572872 | tf_op jit(solution)/shard_map/ppermute | solution.py:190
  44.8 14.7 %collective-permute-start = (bf16[1024,256]{1,0:T(8,128)(2,1)S(1)}, bf16[1024,256]{1,0:T(8,128)(2,1)S(1)}, u32[]{:S(2)}, u32[]{:S(2)}) collective-permute-start(bf16[1024,256]{1,0:T(8,128)(2,1)S(1)} %bitcast.11), channel_id=1, source_target_pairs={{0,8},{1,65},{2,10},{3,67},{4,12},{5,69},{6,14},{7,71},{8,16},{9,7... | collective-permute-start | bytes 1572872 | tf_op jit(solution)/shard_map/ppermute | solution.py:190
  46.7 16.3 %collective-permute-start.5 = (bf16[1024,256]{1,0:T(8,128)(2,1)S(1)}, bf16[1024,256]{1,0:T(8,128)(2,1)}, u32[]{:S(2)}, u32[]{:S(2)}) collective-permute-start(bf16[1024,256]{1,0:T(8,128)(2,1)S(1)} %collective-permute-done.3.refs_6_), channel_id=1, source_target_pairs={{0,56},{1,449},{2,58},{3,451},{4,60},{5,453},{6,62},{7,455},{8,0},... | collective-permute-start | bytes 1572872 | tf_op jit(solution)/shard_map/ppermute | solution.py:190
  52.2 5.2 %copy-start = (f32[32]{0:T(128)S(1)}, f32[32]{0:T(128)}, u32[]{:S(2)}) copy-start(f32[32]{0:T(128)} %bias_ref.1) | copy-start | bytes 388
  52.2 12.8 %collective-permute-start.4 = (bf16[1024,256]{1,0:T(8,128)(2,1)}, bf16[1024,256]{1,0:T(8,128)(2,1)}, u32[]{:S(2)}, u32[]{:S(2)}) collective-permute-start(bf16[1024,256]{1,0:T(8,128)(2,1)} %broadcast_select_fusion), channel_id=1, source_target_pairs={{0,16},{1,129},{2,18},{3,131},{4,20},{5,133},{6,22},{7,135},{8,56}... | collective-permute-start | bytes 1572872 | tf_op jit(solution)/shard_map/ppermute | solution.py:190
  54.2 16.3 %collective-permute-start.2 = (bf16[1024,256]{1,0:T(8,128)(2,1)S(1)}, bf16[1024,256]{1,0:T(8,128)(2,1)}, u32[]{:S(2)}, u32[]{:S(2)}) collective-permute-start(bf16[1024,256]{1,0:T(8,128)(2,1)S(1)} %collective-permute-done.1.refs_2_), channel_id=1, source_target_pairs={{0,8},{1,65},{2,10},{3,67},{4,12},{5,69},{6,14},{7,71},{8,16},{9,7... | collective-permute-start | bytes 1572872 | tf_op jit(solution)/shard_map/ppermute | solution.py:190

commit v10 on v9

--- a/solution.py
+++ b/solution.py
@@ -200,8 +200,8 @@
 
 
 def gathered(chunk):
-    ahead2, behind2 = shifted(chunk, 2), shifted(chunk, -2)
     ahead1, behind1 = shifted(chunk, 1), shifted(chunk, -1)
+    ahead2, behind2 = shifted(ahead1, 1), shifted(behind1, -1)
     ahead3, behind3 = shifted(ahead2, 1), shifted(behind2, -1)
     onward = jnp.where(ring_place() % 2 == 0, ahead2, behind2)
     far = moved(onward, lambda place: place + 2 if place % 2 == 0 else place - 2)

time: 92.2 us -> 96.9 us (1.051)
  waiting for transfers between devices: 11.1 us -> 15.3 us
    all_to_all x1, waiting for transfers between devices: 0.01 us -> 3.39 us  [body(): qkv = lax.all_to_all(packed, 'ctx', split_axis=0, concat_axis=0, tiled=True)]
  transfers between devices with their start and end apart: 8 -> 8, of which waited for: 3 -> 5; matrix products, arithmetic and copies ran while one was open for 1% -> 1% of each run, Pallas kernels for 2% -> 2%
where the time goes in v10:
time: 96.9 us; the launch traced here: 96.4 us
  blocking collectives  35.8 us (37%)
  starting transfers between devices  34.4 us (36%)
  waiting for transfers between devices  15.3 us (16%)
  Pallas kernels  9.08 us (9%)
    ppermute x7, starting transfers between devices, moved(): return lax.ppermute(value, BOTH, pairs)  29.2 us
    all_to_all x1, blocking collectives, body(): lax.all_to_all(spread, BOTH, split_axis=0, concat_axis=0, tiled=True, axi...  19.8 us
    all_to_all x1, blocking collectives, body(): lax.all_to_all(mixed.reshape(members, tokens, LANES), 'ctx', split_axis=0...  16.1 us
    ppermute x7, waiting for transfers between devices, moved(): return lax.ppermute(value, BOTH, pairs)  11.9 us
    all_to_all x1, starting transfers between devices, body(): qkv = lax.all_to_all(packed, 'ctx', split_axis=0, concat_axis=0, tiled=True)  5.19 us
    pallas_call x1, Pallas kernels, body(): pl.pallas_call(memory_kernel, out_shape=jax.ShapeDtypeStruct((span, LANES...  4.45 us
    all_to_all x1, waiting for transfers between devices, body(): qkv = lax.all_to_all(packed, 'ctx', split_axis=0, concat_axis=0, tiled=True)  3.39 us
    pallas_call x1, Pallas kernels, body(): pl.pallas_call(pack_kernel, out_shape=(jax.ShapeDtypeStruct((members, tok...  2.52 us
  transfers between devices with their start and end apart: 8, of which 5 were waited for; matrix products, arithmetic and copies ran while one was open for 1% of the time, Pallas kernels for 2%

profile of v10, /device:TPU:1, one launch (start us, length us, event | category | flops | bytes accessed | tf_op | source)
XLA Modules:
  0.0 96.4 jit_solution(15316377192487964077)
XLA Ops:
  0.0 2.5 %shard_map.73 = (bf16[8,64,896]{2,1,0:T(8,128)(2,1)}, bf16[8,128,256]{2,1,0:T(8,128)(2,1)}) custom-call(s32[4,16]{1,0:T(4,128)} %ids_ref.1, bf16[64,4096]{1,0:T(8,128)(2,1)} %queries_ref.1, bf16[64,1024]{1,0:T(8,128)(2,1)} %keys_ref.1, bf16[64,1024]{1,0:T(8,128)(2,1)} %values_ref.1, bf16[128,1024]{1,0:T(8,128)(2,1)} %mem_keys_ref.1, ...), custom_call_target="tpu_custom_call" | custom-call | bytes 4194304 | tf_op jit(solution)/shard_map/pallas_call | solution.py:219
  2.5 19.8 %all_to_all.15 = bf16[8,128,256]{2,1,0:T(8,128)(2,1)S(1)} all-to-all(bf16[8,128,256]{2,1,0:T(8,128)(2,1)} %get-tuple-element.14), channel_id=1, replica_groups={{0,64,128,192,256,320,384,448},{8,72,136,200,264,328,392,456},{16,80,14..., dimensions={0} | all-to-all | bytes 1048576 | tf_op jit(solution)/shard_map/all_to_all | solution.py:232
  22.3 10.7 %collective-permute-start.3 = (bf16[1024,256]{1,0:T(8,128)(2,1)S(1)}, bf16[1024,256]{1,0:T(8,128)(2,1)S(1)}, u32[]{:S(2)}, u32[]{:S(2)}) collective-permute-start(bf16[1024,256]{1,0:T(8,128)(2,1)S(1)} %bitcast.8), channel_id=1, source_target_pairs={{0,56},{1,449},{2,58},{3,451},{4,60},{5,453},{6,62},{7,455},{8,0},... | collective-permute-start | bytes 1572872 | tf_op jit(solution)/shard_map/ppermute | solution.py:190
  33.0 1.9 %collective-permute-start = (bf16[1024,256]{1,0:T(8,128)(2,1)S(1)}, bf16[1024,256]{1,0:T(8,128)(2,1)S(1)}, u32[]{:S(2)}, u32[]{:S(2)}) collective-permute-start(bf16[1024,256]{1,0:T(8,128)(2,1)S(1)} %bitcast.9), channel_id=1, source_target_pairs={{0,8},{1,65},{2,10},{3,67},{4,12},{5,69},{6,14},{7,71},{8,16},{9,7... | collective-permute-start | bytes 1572872 | tf_op jit(solution)/shard_map/ppermute | solution.py:190
  34.9 4.2 %collective-permute-done.3.refs_7_ = bf16[1024,256]{1,0:T(8,128)(2,1)S(1)} collective-permute-done((bf16[1024,256]{1,0:T(8,128)(2,1)S(1)}, bf16[1024,256]{1,0:T(8,128)(2,1)S(1)}, u32[]{:S(2)}, u32[]{:S(2)}) %collective-permute-start.3) | collective-permute-done | bytes 524320 | tf_op jit(solution)/shard_map/ppermute | solution.py:190
  39.1 5.3 %collective-permute-start.4 = (bf16[1024,256]{1,0:T(8,128)(2,1)S(1)}, bf16[1024,256]{1,0:T(8,128)(2,1)S(1)}, u32[]{:S(2)}, u32[]{:S(2)}) collective-permute-start(bf16[1024,256]{1,0:T(8,128)(2,1)S(1)} %collective-permute-done.3.refs_7_), channel_id=1, source_target_pairs={{0,56},{1,449},{2,58},{3,451},{4,60},{5,453},{6,62},{7,455},{8,0},... | collective-permute-start | bytes 1572872 | tf_op jit(solution)/shard_map/ppermute | solution.py:190
  44.4 0.0 collective-permute-done.refs_1_
  44.4 1.9 %collective-permute-start.1 = (bf16[1024,256]{1,0:T(8,128)(2,1)S(1)}, bf16[1024,256]{1,0:T(8,128)(2,1)S(1)}, u32[]{:S(2)}, u32[]{:S(2)}) collective-permute-start(bf16[1024,256]{1,0:T(8,128)(2,1)S(1)} %collective-permute-done.refs_1_), channel_id=1, source_target_pairs={{0,8},{1,65},{2,10},{3,67},{4,12},{5,69},{6,14},{7,71},{8,16},{9,7... | collective-permute-start | bytes 1572872 | tf_op jit(solution)/shard_map/ppermute | solution.py:190
  46.3 5.2 %all-to-all-start = ((bf16[8,64,896]{2,1,0:T(8,128)(2,1)}), bf16[8,64,896]{2,1,0:T(8,128)(2,1)S(1)}, u32[]{:S(2)}, u32[]{:S(2)}) async-start(bf16[8,64,896]{2,1,0:T(8,128)(2,1)} %get-tuple-element.10), calls=%async_computation | async-start | bytes 1835008 | tf_op jit(solution)/shard_map/all_to_all | solution.py:230
  51.5 0.0 collective-permute-done.4.refs_6_
  51.5 4.3 %collective-permute-start.6 = (bf16[1024,256]{1,0:T(8,128)(2,1)S(1)}, bf16[1024,256]{1,0:T(8,128)(2,1)}, u32[]{:S(2)}, u32[]{:S(2)}) collective-permute-start(bf16[1024,256]{1,0:T(8,128)(2,1)S(1)} %collective-permute-done.4.refs_6_), channel_id=1, source_target_pairs={{0,56},{1,449},{2,58},{3,451},{4,60},{5,453},{6,62},{7,455},{8,0},... | collective-permute-start | bytes 1572872 | tf_op jit(solution)/shard_map/ppermute | solution.py:190
  55.8 0.0 collective-permute-done.1.refs_2_
  55.8 0.8 broadcast_select_fusion
  56.7 2.0 %collective-permute-start.5 = (bf16[1024,256]{1,0:T(8,128)(2,1)}, bf16[1024,256]{1,0:T(8,128)(2,1)}, u32[]{:S(2)}, u32[]{:S(2)}) collective-permute-start(bf16[1024,256]{1,0:T(8,128)(2,1)} %broadcast_select_fusion), channel_id=1, source_target_pairs={{0,16},{1,129},{2,18},{3,131},{4,20},{5,133},{6,22},{7,135},{8,56}... | collective-permute-start | bytes 1572872 | tf_op jit(solution)/shard_map/ppermute | solution.py:190
  58.7 3.1 %collective-permute-start.2 = (bf16[1024,256]{1,0:T(8,128)(2,1)S(1)}, bf16[1024,256]{1,0:T(8,128)(2,1)}, u32[]{:S(2)}, u32[]{:S(2)}) collective-permute-start(bf16[1024,256]{1,0:T(8,128)(2,1)S(1)} %collective-permute-done.1.refs_2_), channel_id=1, source_target_pairs={{0,8},{1,65},{2,10},{3,67},{4,12},{5,69},{6,14},{7,71},{8,16},{9,7... | collective-permute-start | bytes 1572872 | tf_op jit(solution)/shard_map/ppermute | solution.py:190
  61.8 3.4 %all-to-all-done = bf16[8,64,896]{2,1,0:T(8,128)(2,1)S(1)} async-done(((bf16[8,64,896]{2,1,0:T(8,128)(2,1)}), bf16[8,64,896]{2,1,0:T(8,128)(2,1)S(1)}, u32[]{:S(2)}, u32[]{:S(2)}) %all-to-all-start) | async-done | bytes 917536 | tf_op jit(solution)/shard_map/all_to_all | solution.py:230
  65.2 0.0 copy-done
  65.2 2.1 %shard_map.74 = (f32[512,512]{1,0:T(8,128)S(1)}, s32[4,128]{1,0:T(4,128)S(1)}, f32[4,128]{1,0:T(4,128)S(1)}) custom-call(f32[32]{0:T(128)S(1)} %copy-done, bf16[512,896]{1,0:T(8,128)(2,1)S(1)} %bitcast.6), custom_call_target="tpu_custom_call" | custom-call | flops 536870912 | bytes 2097152 | tf_op jit(solution)/shard_map/pallas_call | solution.py:236
  67.3 0.2 collective-permute-done.6.refs_5_
  67.5 2.0 %collective-permute-done.5.refs_4_ = bf16[1024,256]{1,0:T(8,128)(2,1)} collective-permute-done((bf16[1024,256]{1,0:T(8,128)(2,1)}, bf16[1024,256]{1,0:T(8,128)(2,1)}, u32[]{:S(2)}, u32[]{:S(2)}) %collective-permute-start.5) | collective-permute-done | bytes 524320 | tf_op jit(solution)/shard_map/ppermute | solution.py:190
  69.5 5.6 %collective-permute-done.2.refs_3_ = bf16[1024,256]{1,0:T(8,128)(2,1)} collective-permute-done((bf16[1024,256]{1,0:T(8,128)(2,1)S(1)}, bf16[1024,256]{1,0:T(8,128)(2,1)}, u32[]{:S(2)}, u32[]{:S(2)}) %collective-permute-start.2) | collective-permute-done | bytes 524320 | tf_op jit(solution)/shard_map/ppermute | solution.py:190
  75.1 4.4 %shard_map.75 = bf16[512,512]{1,0:T(8,128)(2,1)S(1)} custom-call(s32[4,128]{1,0:T(4,128)S(1)} %get-tuple-element.11.starts_ref, f32[4,128]{1,0:T(4,128)S(1)} %get-tuple-element.12.gates_ref, bf16[512,896]{1,0:T(8,128)(2,1)S(1)} %bitcast.7, f32[512,512]{1,0:T(8,128)S(1)} %get-tuple-element.13.local_ref, bf16[1024,256]{1,0:T(8,128)(2,1)S(1)} %bitcast.10, ...), custom_call_target="tpu_custom_call" | custom-call | flops 536870912 | bytes 7340032 | tf_op jit(solution)/shard_map/pallas_call | solution.py:250
  79.5 16.1 %all_to_all.16 = bf16[8,64,512]{2,1,0:T(8,128)(2,1)S(1)} all-to-all(bf16[8,64,512]{2,1,0:T(8,128)(2,1)S(1)} %bitcast.11), channel_id=1, replica_groups=mesh['mem'=64,'ctx'=8] {'ctx'}, dimensions={0} | all-to-all | bytes 1048576 | tf_op jit(solution)/shard_map/all_to_all | solution.py:266
  95.6 0.8 copy.9
  (1 shorter events, 0.0 us)
Async XLA Ops:
  22.3 16.8 %collective-permute-start.3 = (bf16[1024,256]{1,0:T(8,128)(2,1)S(1)}, bf16[1024,256]{1,0:T(8,128)(2,1)S(1)}, u32[]{:S(2)}, u32[]{:S(2)}) collective-permute-start(bf16[1024,256]{1,0:T(8,128)(2,1)S(1)} %bitcast.8), channel_id=1, source_target_pairs={{0,56},{1,449},{2,58},{3,451},{4,60},{5,453},{6,62},{7,455},{8,0},... | collective-permute-start | bytes 1572872 | tf_op jit(solution)/shard_map/ppermute | solution.py:190
  33.0 11.4 %collective-permute-start = (bf16[1024,256]{1,0:T(8,128)(2,1)S(1)}, bf16[1024,256]{1,0:T(8,128)(2,1)S(1)}, u32[]{:S(2)}, u32[]{:S(2)}) collective-permute-start(bf16[1024,256]{1,0:T(8,128)(2,1)S(1)} %bitcast.9), channel_id=1, source_target_pairs={{0,8},{1,65},{2,10},{3,67},{4,12},{5,69},{6,14},{7,71},{8,16},{9,7... | collective-permute-start | bytes 1572872 | tf_op jit(solution)/shard_map/ppermute | solution.py:190
  39.1 12.4 %collective-permute-start.4 = (bf16[1024,256]{1,0:T(8,128)(2,1)S(1)}, bf16[1024,256]{1,0:T(8,128)(2,1)S(1)}, u32[]{:S(2)}, u32[]{:S(2)}) collective-permute-start(bf16[1024,256]{1,0:T(8,128)(2,1)S(1)} %collective-permute-done.3.refs_7_), channel_id=1, source_target_pairs={{0,56},{1,449},{2,58},{3,451},{4,60},{5,453},{6,62},{7,455},{8,0},... | collective-permute-start | bytes 1572872 | tf_op jit(solution)/shard_map/ppermute | solution.py:190
  44.4 11.4 %collective-permute-start.1 = (bf16[1024,256]{1,0:T(8,128)(2,1)S(1)}, bf16[1024,256]{1,0:T(8,128)(2,1)S(1)}, u32[]{:S(2)}, u32[]{:S(2)}) collective-permute-start(bf16[1024,256]{1,0:T(8,128)(2,1)S(1)} %collective-permute-done.refs_1_), channel_id=1, source_target_pairs={{0,8},{1,65},{2,10},{3,67},{4,12},{5,69},{6,14},{7,71},{8,16},{9,7... | collective-permute-start | bytes 1572872 | tf_op jit(solution)/shard_map/ppermute | solution.py:190
  46.3 18.9 %all-to-all-start = ((bf16[8,64,896]{2,1,0:T(8,128)(2,1)}), bf16[8,64,896]{2,1,0:T(8,128)(2,1)S(1)}, u32[]{:S(2)}, u32[]{:S(2)}) async-start(bf16[8,64,896]{2,1,0:T(8,128)(2,1)} %get-tuple-element.10), calls=%async_computation | async-start | bytes 1835008 | tf_op jit(solution)/shard_map/all_to_all | solution.py:230
  51.5 16.0 %collective-permute-start.6 = (bf16[1024,256]{1,0:T(8,128)(2,1)S(1)}, bf16[1024,256]{1,0:T(8,128)(2,1)}, u32[]{:S(2)}, u32[]{:S(2)}) collective-permute-start(bf16[1024,256]{1,0:T(8,128)(2,1)S(1)} %collective-permute-done.4.refs_6_), channel_id=1, source_target_pairs={{0,56},{1,449},{2,58},{3,451},{4,60},{5,453},{6,62},{7,455},{8,0},... | collective-permute-start | bytes 1572872 | tf_op jit(solution)/shard_map/ppermute | solution.py:190
  56.7 8.5 %copy-start = (f32[32]{0:T(128)S(1)}, f32[32]{0:T(128)}, u32[]{:S(2)}) copy-start(f32[32]{0:T(128)} %bias_ref.1) | copy-start | bytes 388
  56.7 12.8 %collective-permute-start.5 = (bf16[1024,256]{1,0:T(8,128)(2,1)}, bf16[1024,256]{1,0:T(8,128)(2,1)}, u32[]{:S(2)}, u32[]{:S(2)}) collective-permute-start(bf16[1024,256]{1,0:T(8,128)(2,1)} %broadcast_select_fusion), channel_id=1, source_target_pairs={{0,16},{1,129},{2,18},{3,131},{4,20},{5,133},{6,22},{7,135},{8,56}... | collective-permute-start | bytes 1572872 | tf_op jit(solution)/shard_map/ppermute | solution.py:190
  58.7 16.3 %collective-permute-start.2 = (bf16[1024,256]{1,0:T(8,128)(2,1)S(1)}, bf16[1024,256]{1,0:T(8,128)(2,1)}, u32[]{:S(2)}, u32[]{:S(2)}) collective-permute-start(bf16[1024,256]{1,0:T(8,128)(2,1)S(1)} %collective-permute-done.1.refs_2_), channel_id=1, source_target_pairs={{0,8},{1,65},{2,10},{3,67},{4,12},{5,69},{6,14},{7,71},{8,16},{9,7... | collective-permute-start | bytes 1572872 | tf_op jit(solution)/shard_map/ppermute | solution.py:190

commit v11 on v9

--- a/solution.py
+++ b/solution.py
@@ -39,9 +39,7 @@
     )
 
 
-def pack_kernel(
-    ids_ref, queries_ref, keys_ref, values_ref, mem_keys_ref, mem_values_ref, out_ref, own_ref, id_ref
-):
+def pack_kernel(ids_ref, queries_ref, keys_ref, values_ref, out_ref, id_ref):
     for block in range(ids_ref.shape[0]):
         for j in range(TOPB):
             value = ids_ref[block, j].astype(jnp.float32)
@@ -55,12 +53,6 @@
         out_ref[head, :, LANES : LANES + HEAD_DIM] = keys_ref[:, here]
         out_ref[head, :, LANES + HEAD_DIM : LANES + 2 * HEAD_DIM] = values_ref[:, here]
         out_ref[head, :, LANES + 2 * HEAD_DIM :] = id_lanes
-    start = pl.multiple_of(lax.axis_index("ctx") * HEAD_DIM, HEAD_DIM)
-    keys = mem_keys_ref[:, pl.ds(start, HEAD_DIM)]
-    values = mem_values_ref[:, pl.ds(start, HEAD_DIM)]
-    for place in range(own_ref.shape[0]):
-        own_ref[place, :, :HEAD_DIM] = keys
-        own_ref[place, :, HEAD_DIM:] = values
 
 
 def block_rows(ids, held, rows):
@@ -216,17 +208,24 @@
     vmem = pl.BlockSpec(memory_space=pltpu.VMEM)
     smem = pl.BlockSpec(memory_space=pltpu.SMEM)
     hbm = pl.BlockSpec(memory_space=pl.ANY)
-    packed, spread = pl.pallas_call(
+    start = lax.axis_index("ctx") * HEAD_DIM
+    own = jnp.concatenate(
+        [
+            lax.dynamic_slice_in_dim(mem_keys, start, HEAD_DIM, 1),
+            lax.dynamic_slice_in_dim(mem_values, start, HEAD_DIM, 1),
+        ],
+        axis=1,
+    )
+    spread = jnp.broadcast_to(own[None], (SIDE,) + own.shape)
+    packed = pl.pallas_call(
         pack_kernel,
-        out_shape=(
-            jax.ShapeDtypeStruct((members, tokens, LANES + 3 * HEAD_DIM), jnp.bfloat16),
-            jax.ShapeDtypeStruct((SIDE, rows, 2 * HEAD_DIM), jnp.bfloat16),
-        ),
-        in_specs=[smem] + [vmem] * 5,
-        out_specs=(vmem, vmem),
+        out_shape=jax.ShapeDtypeStruct((members, tokens, LANES + 3 * HEAD_DIM), jnp.bfloat16),
+        in_specs=[smem] + [vmem] * 3,
+        out_specs=vmem,
         scratch_shapes=[pltpu.VMEM((tokens, HEAD_DIM), jnp.float32)],
-        cost_estimate=pl.CostEstimate(flops=0, bytes_accessed=4 << 20, transcendentals=0),
-    )(block_ids, queries, local_keys, local_values, mem_keys, mem_values)
+        compiler_params=pltpu.CompilerParams(vmem_limit_bytes=8 << 20),
+        cost_estimate=pl.CostEstimate(flops=0, bytes_accessed=2 << 20, transcendentals=0),
+    )(block_ids, queries, local_keys, local_values)
     qkv = lax.all_to_all(packed, "ctx", split_axis=0, concat_axis=0, tiled=True)
     qkv = qkv.reshape(span, LANES + 3 * HEAD_DIM)
     chunk = lax.all_to_all(

time: 92.2 us -> 92.2 us (level)
  transfers between devices with their start and end apart: 8 -> 8, of which waited for: 3 -> 3; matrix products, arithmetic and copies ran while one was open for 1% -> 1% of each run, Pallas kernels for 2% -> 4%
where the time goes in v11:
time: 92.2 us; the launch traced here: 91.6 us
  blocking collectives  35.6 us (39%)
  starting transfers between devices  34.1 us (37%)
  waiting for transfers between devices  11.1 us (12%)
  Pallas kernels  8.18 us (9%)
  local copies, waits for them, and re-layouts  1.68 us (2%)
    ppermute x7, starting transfers between devices, moved(): return lax.ppermute(value, BOTH, pairs)  29 us
    all_to_all x1, blocking collectives, body(): lax.all_to_all(spread, BOTH, split_axis=0, concat_axis=0, tiled=True, axi...  19.7 us
    all_to_all x1, blocking collectives, body(): lax.all_to_all(mixed.reshape(members, tokens, LANES), 'ctx', split_axis=0...  15.8 us
    ppermute x7, waiting for transfers between devices, moved(): return lax.ppermute(value, BOTH, pairs)  11.1 us
    all_to_all x1, starting transfers between devices, body(): qkv = lax.all_to_all(packed, 'ctx', split_axis=0, concat_axis=0, tiled=True)  5.12 us
    pallas_call x1, Pallas kernels, body(): pl.pallas_call(memory_kernel, out_shape=jax.ShapeDtypeStruct((span, LANES...  4.46 us
    pallas_call x1, Pallas kernels, body(): pl.pallas_call(functools.partial(local_kernel, rows // BLOCK, rows), out_...  2.11 us
  transfers between devices with their start and end apart: 8, of which 3 were waited for; matrix products, arithmetic and copies ran while one was open for 1% of the time, Pallas kernels for 4%

profile of v11, /device:TPU:1, one launch (start us, length us, event | category | flops | bytes accessed | tf_op | source)
XLA Modules:
  0.0 91.6 jit_solution(2413058677791746998)
XLA Ops:
  0.0 0.8 constant_dynamic-slice_fusion
  0.8 0.0 copy-start
  0.8 0.0 copy-start.1
  0.9 0.0 copy-start.2
  0.9 0.0 copy-start.3
  0.9 19.7 %all_to_all.15 = bf16[8,128,256]{2,1,0:T(8,128)(2,1)S(1)} all-to-all(bf16[8,128,256]{2,1,0:T(8,128)(2,1)S(1)} %broadcast_in_dim.2), channel_id=1, replica_groups={{0,64,128,192,256,320,384,448},{8,72,136,200,264,328,392,456},{16,80,14..., dimensions={0} | all-to-all | bytes 1048576 | tf_op jit(solution)/shard_map/all_to_all | solution.py:231
  20.6 10.6 %collective-permute-start.3 = (bf16[1024,256]{1,0:T(8,128)(2,1)S(1)}, bf16[1024,256]{1,0:T(8,128)(2,1)S(1)}, u32[]{:S(2)}, u32[]{:S(2)}) collective-permute-start(bf16[1024,256]{1,0:T(8,128)(2,1)S(1)} %bitcast.8), channel_id=1, source_target_pairs={{0,48},{1,385},{2,50},{3,387},{4,52},{5,389},{6,54},{7,391},{8,56}... | collective-permute-start | bytes 1572872 | tf_op jit(solution)/shard_map/ppermute | solution.py:182
  31.3 1.9 %collective-permute-start.1 = (bf16[1024,256]{1,0:T(8,128)(2,1)S(1)}, bf16[1024,256]{1,0:T(8,128)(2,1)S(1)}, u32[]{:S(2)}, u32[]{:S(2)}) collective-permute-start(bf16[1024,256]{1,0:T(8,128)(2,1)S(1)} %bitcast.9), channel_id=1, source_target_pairs={{0,16},{1,129},{2,18},{3,131},{4,20},{5,133},{6,22},{7,135},{8,24}... | collective-permute-start | bytes 1572872 | tf_op jit(solution)/shard_map/ppermute | solution.py:182
  33.2 1.6 %shard_map.73 = bf16[8,64,896]{2,1,0:T(8,128)(2,1)} custom-call(s32[4,16]{1,0:T(4,128)S(1)} %copy-done.3, bf16[64,4096]{1,0:T(8,128)(2,1)S(1)} %copy-done, bf16[64,1024]{1,0:T(8,128)(2,1)S(1)} %copy-done.1, bf16[64,1024]{1,0:T(8,128)(2,1)S(1)} %copy-done.2), custom_call_target="tpu_custom_call" | custom-call | bytes 2097152 | tf_op jit(solution)/shard_map/pallas_call | solution.py:220
  34.8 5.1 %all-to-all-start = ((bf16[8,64,896]{2,1,0:T(8,128)(2,1)}), bf16[8,64,896]{2,1,0:T(8,128)(2,1)S(1)}, u32[]{:S(2)}, u32[]{:S(2)}) async-start(bf16[8,64,896]{2,1,0:T(8,128)(2,1)} %shard_map.73), calls=%async_computation | async-start | bytes 1835008 | tf_op jit(solution)/shard_map/all_to_all | solution.py:229
  40.0 4.8 %collective-permute-start.6 = (bf16[1024,256]{1,0:T(8,128)(2,1)S(1)}, bf16[1024,256]{1,0:T(8,128)(2,1)S(1)}, u32[]{:S(2)}, u32[]{:S(2)}) collective-permute-start(bf16[1024,256]{1,0:T(8,128)(2,1)S(1)} %bitcast.10), channel_id=1, source_target_pairs={{0,56},{1,449},{2,58},{3,451},{4,60},{5,453},{6,62},{7,455},{8,0},... | collective-permute-start | bytes 1572872 | tf_op jit(solution)/shard_map/ppermute | solution.py:182
  44.7 1.9 %collective-permute-start = (bf16[1024,256]{1,0:T(8,128)(2,1)S(1)}, bf16[1024,256]{1,0:T(8,128)(2,1)S(1)}, u32[]{:S(2)}, u32[]{:S(2)}) collective-permute-start(bf16[1024,256]{1,0:T(8,128)(2,1)S(1)} %bitcast.11), channel_id=1, source_target_pairs={{0,8},{1,65},{2,10},{3,67},{4,12},{5,69},{6,14},{7,71},{8,16},{9,7... | collective-permute-start | bytes 1572872 | tf_op jit(solution)/shard_map/ppermute | solution.py:182
  46.7 0.0 collective-permute-done.3.refs_6_
  46.7 4.6 %collective-permute-start.5 = (bf16[1024,256]{1,0:T(8,128)(2,1)S(1)}, bf16[1024,256]{1,0:T(8,128)(2,1)}, u32[]{:S(2)}, u32[]{:S(2)}) collective-permute-start(bf16[1024,256]{1,0:T(8,128)(2,1)S(1)} %collective-permute-done.3.refs_6_), channel_id=1, source_target_pairs={{0,56},{1,449},{2,58},{3,451},{4,60},{5,453},{6,62},{7,455},{8,0},... | collective-permute-start | bytes 1572872 | tf_op jit(solution)/shard_map/ppermute | solution.py:182
  51.3 0.9 broadcast_select_fusion
  52.1 2.0 %collective-permute-start.4 = (bf16[1024,256]{1,0:T(8,128)(2,1)}, bf16[1024,256]{1,0:T(8,128)(2,1)}, u32[]{:S(2)}, u32[]{:S(2)}) collective-permute-start(bf16[1024,256]{1,0:T(8,128)(2,1)} %broadcast_select_fusion), channel_id=1, source_target_pairs={{0,16},{1,129},{2,18},{3,131},{4,20},{5,133},{6,22},{7,135},{8,56}... | collective-permute-start | bytes 1572872 | tf_op jit(solution)/shard_map/ppermute | solution.py:182
  54.2 3.1 %collective-permute-start.2 = (bf16[1024,256]{1,0:T(8,128)(2,1)S(1)}, bf16[1024,256]{1,0:T(8,128)(2,1)}, u32[]{:S(2)}, u32[]{:S(2)}) collective-permute-start(bf16[1024,256]{1,0:T(8,128)(2,1)S(1)} %collective-permute-done.1.refs_2_), channel_id=1, source_target_pairs={{0,8},{1,65},{2,10},{3,67},{4,12},{5,69},{6,14},{7,71},{8,16},{9,7... | collective-permute-start | bytes 1572872 | tf_op jit(solution)/shard_map/ppermute | solution.py:182
  57.3 2.1 %shard_map.74 = (f32[512,512]{1,0:T(8,128)S(1)}, s32[4,128]{1,0:T(4,128)S(1)}, f32[4,128]{1,0:T(4,128)S(1)}) custom-call(f32[32]{0:T(128)S(1)} %copy-done.4, bf16[512,896]{1,0:T(8,128)(2,1)S(1)} %bitcast.6), custom_call_target="tpu_custom_call" | custom-call | flops 536870912 | bytes 2097152 | tf_op jit(solution)/shard_map/pallas_call | solution.py:235
  59.4 3.6 %collective-permute-done.5.refs_5_ = bf16[1024,256]{1,0:T(8,128)(2,1)} collective-permute-done((bf16[1024,256]{1,0:T(8,128)(2,1)S(1)}, bf16[1024,256]{1,0:T(8,128)(2,1)}, u32[]{:S(2)}, u32[]{:S(2)}) %collective-permute-start.5) | collective-permute-done | bytes 524320 | tf_op jit(solution)/shard_map/ppermute | solution.py:182
  63.0 2.0 %collective-permute-done.4.refs_4_ = bf16[1024,256]{1,0:T(8,128)(2,1)} collective-permute-done((bf16[1024,256]{1,0:T(8,128)(2,1)}, bf16[1024,256]{1,0:T(8,128)(2,1)}, u32[]{:S(2)}, u32[]{:S(2)}) %collective-permute-start.4) | collective-permute-done | bytes 524320 | tf_op jit(solution)/shard_map/ppermute | solution.py:182
  64.9 5.6 %collective-permute-done.2.refs_3_ = bf16[1024,256]{1,0:T(8,128)(2,1)} collective-permute-done((bf16[1024,256]{1,0:T(8,128)(2,1)S(1)}, bf16[1024,256]{1,0:T(8,128)(2,1)}, u32[]{:S(2)}, u32[]{:S(2)}) %collective-permute-start.2) | collective-permute-done | bytes 524320 | tf_op jit(solution)/shard_map/ppermute | solution.py:182
  70.5 4.5 %shard_map.75 = bf16[512,512]{1,0:T(8,128)(2,1)S(1)} custom-call(s32[4,128]{1,0:T(4,128)S(1)} %get-tuple-element.8.starts_ref, f32[4,128]{1,0:T(4,128)S(1)} %get-tuple-element.9.gates_ref, bf16[512,896]{1,0:T(8,128)(2,1)S(1)} %bitcast.7, f32[512,512]{1,0:T(8,128)S(1)} %get-tuple-element.10.local_ref, bf16[1024,256]{1,0:T(8,128)(2,1)S(1)} %bitcast.12, ...), custom_call_target="tpu_custom_call" | custom-call | flops 536870912 | bytes 7340032 | tf_op jit(solution)/shard_map/pallas_call | solution.py:249
  75.0 15.8 %all_to_all.16 = bf16[8,64,512]{2,1,0:T(8,128)(2,1)S(1)} all-to-all(bf16[8,64,512]{2,1,0:T(8,128)(2,1)S(1)} %bitcast.13), channel_id=1, replica_groups=mesh['mem'=64,'ctx'=8] {'ctx'}, dimensions={0} | all-to-all | bytes 1048576 | tf_op jit(solution)/shard_map/all_to_all | solution.py:265
  90.8 0.8 copy.9
  (12 shorter events, 0.1 us)
Async XLA Ops:
  0.8 32.4 %copy-start = (bf16[64,4096]{1,0:T(8,128)(2,1)S(1)}, bf16[64,4096]{1,0:T(8,128)(2,1)}, u32[]{:S(2)}) copy-start(bf16[64,4096]{1,0:T(8,128)(2,1)} %queries_ref.1) | copy-start | bytes 1572868
  0.8 32.4 %copy-start.1 = (bf16[64,1024]{1,0:T(8,128)(2,1)S(1)}, bf16[64,1024]{1,0:T(8,128)(2,1)}, u32[]{:S(2)}) copy-start(bf16[64,1024]{1,0:T(8,128)(2,1)} %keys_ref.1) | copy-start | bytes 393220
  0.9 32.4 %copy-start.2 = (bf16[64,1024]{1,0:T(8,128)(2,1)S(1)}, bf16[64,1024]{1,0:T(8,128)(2,1)}, u32[]{:S(2)}) copy-start(bf16[64,1024]{1,0:T(8,128)(2,1)} %values_ref.1) | copy-start | bytes 393220
  0.9 32.3 %copy-start.3 = (s32[4,16]{1,0:T(4,128)S(1)}, s32[4,16]{1,0:T(4,128)}, u32[]{:S(2)}) copy-start(s32[4,16]{1,0:T(4,128)} %ids_ref.1) | copy-start | bytes 772
  20.6 26.1 %collective-permute-start.3 = (bf16[1024,256]{1,0:T(8,128)(2,1)S(1)}, bf16[1024,256]{1,0:T(8,128)(2,1)S(1)}, u32[]{:S(2)}, u32[]{:S(2)}) collective-permute-start(bf16[1024,256]{1,0:T(8,128)(2,1)S(1)} %bitcast.8), channel_id=1, source_target_pairs={{0,48},{1,385},{2,50},{3,387},{4,52},{5,389},{6,54},{7,391},{8,56}... | collective-permute-start | bytes 1572872 | tf_op jit(solution)/shard_map/ppermute | solution.py:182
  31.3 20.0 %collective-permute-start.1 = (bf16[1024,256]{1,0:T(8,128)(2,1)S(1)}, bf16[1024,256]{1,0:T(8,128)(2,1)S(1)}, u32[]{:S(2)}, u32[]{:S(2)}) collective-permute-start(bf16[1024,256]{1,0:T(8,128)(2,1)S(1)} %bitcast.9), channel_id=1, source_target_pairs={{0,16},{1,129},{2,18},{3,131},{4,20},{5,133},{6,22},{7,135},{8,24}... | collective-permute-start | bytes 1572872 | tf_op jit(solution)/shard_map/ppermute | solution.py:182
  34.8 22.4 %all-to-all-start = ((bf16[8,64,896]{2,1,0:T(8,128)(2,1)}), bf16[8,64,896]{2,1,0:T(8,128)(2,1)S(1)}, u32[]{:S(2)}, u32[]{:S(2)}) async-start(bf16[8,64,896]{2,1,0:T(8,128)(2,1)} %shard_map.73), calls=%async_computation | async-start | bytes 1835008 | tf_op jit(solution)/shard_map/all_to_all | solution.py:229
  40.0 19.4 %collective-permute-start.6 = (bf16[1024,256]{1,0:T(8,128)(2,1)S(1)}, bf16[1024,256]{1,0:T(8,128)(2,1)S(1)}, u32[]{:S(2)}, u32[]{:S(2)}) collective-permute-start(bf16[1024,256]{1,0:T(8,128)(2,1)S(1)} %bitcast.10), channel_id=1, source_target_pairs={{0,56},{1,449},{2,58},{3,451},{4,60},{5,453},{6,62},{7,455},{8,0},... | collective-permute-start | bytes 1572872 | tf_op jit(solution)/shard_map/ppermute | solution.py:182
  44.7 14.7 %collective-permute-start = (bf16[1024,256]{1,0:T(8,128)(2,1)S(1)}, bf16[1024,256]{1,0:T(8,128)(2,1)S(1)}, u32[]{:S(2)}, u32[]{:S(2)}) collective-permute-start(bf16[1024,256]{1,0:T(8,128)(2,1)S(1)} %bitcast.11), channel_id=1, source_target_pairs={{0,8},{1,65},{2,10},{3,67},{4,12},{5,69},{6,14},{7,71},{8,16},{9,7... | collective-permute-start | bytes 1572872 | tf_op jit(solution)/shard_map/ppermute | solution.py:182
  46.7 16.3 %collective-permute-start.5 = (bf16[1024,256]{1,0:T(8,128)(2,1)S(1)}, bf16[1024,256]{1,0:T(8,128)(2,1)}, u32[]{:S(2)}, u32[]{:S(2)}) collective-permute-start(bf16[1024,256]{1,0:T(8,128)(2,1)S(1)} %collective-permute-done.3.refs_6_), channel_id=1, source_target_pairs={{0,56},{1,449},{2,58},{3,451},{4,60},{5,453},{6,62},{7,455},{8,0},... | collective-permute-start | bytes 1572872 | tf_op jit(solution)/shard_map/ppermute | solution.py:182
  52.1 5.2 %copy-start.4 = (f32[32]{0:T(128)S(1)}, f32[32]{0:T(128)}, u32[]{:S(2)}) copy-start(f32[32]{0:T(128)} %bias_ref.1) | copy-start | bytes 388
  52.1 12.8 %collective-permute-start.4 = (bf16[1024,256]{1,0:T(8,128)(2,1)}, bf16[1024,256]{1,0:T(8,128)(2,1)}, u32[]{:S(2)}, u32[]{:S(2)}) collective-permute-start(bf16[1024,256]{1,0:T(8,128)(2,1)} %broadcast_select_fusion), channel_id=1, source_target_pairs={{0,16},{1,129},{2,18},{3,131},{4,20},{5,133},{6,22},{7,135},{8,56}... | collective-permute-start | bytes 1572872 | tf_op jit(solution)/shard_map/ppermute | solution.py:182
  54.2 16.3 %collective-permute-start.2 = (bf16[1024,256]{1,0:T(8,128)(2,1)S(1)}, bf16[1024,256]{1,0:T(8,128)(2,1)}, u32[]{:S(2)}, u32[]{:S(2)}) collective-permute-start(bf16[1024,256]{1,0:T(8,128)(2,1)S(1)} %collective-permute-done.1.refs_2_), channel_id=1, source_target_pairs={{0,8},{1,65},{2,10},{3,67},{4,12},{5,69},{6,14},{7,71},{8,16},{9,7... | collective-permute-start | bytes 1572872 | tf_op jit(solution)/shard_map/ppermute | solution.py:182

commit v12 on v11

--- a/solution.py
+++ b/solution.py
@@ -226,11 +226,12 @@
         compiler_params=pltpu.CompilerParams(vmem_limit_bytes=8 << 20),
         cost_estimate=pl.CostEstimate(flops=0, bytes_accessed=2 << 20, transcendentals=0),
     )(block_ids, queries, local_keys, local_values)
-    qkv = lax.all_to_all(packed, "ctx", split_axis=0, concat_axis=0, tiled=True)
-    qkv = qkv.reshape(span, LANES + 3 * HEAD_DIM)
     chunk = lax.all_to_all(
         spread, BOTH, split_axis=0, concat_axis=0, tiled=True, axis_index_groups=first_groups()
     ).reshape(SIDE * rows, 2 * HEAD_DIM)
+    packed, chunk = lax.optimization_barrier((packed, chunk))
+    qkv = lax.all_to_all(packed, "ctx", split_axis=0, concat_axis=0, tiled=True)
+    qkv = qkv.reshape(span, LANES + 3 * HEAD_DIM)
     chunks = gathered(chunk)
     local_out, starts, gates = pl.pallas_call(
         functools.partial(local_kernel, rows // BLOCK, rows),

time: 92.2 us -> 91.5 us (level)
  blocking collectives: 35.6 us -> 15.9 us
  waiting for transfers between devices: 11.1 us -> 21.6 us
  starting transfers between devices: 34.1 us -> 41.9 us
    all_to_all x1 -> x0, blocking collectives: 19.7 us -> none  [body(): lax.all_to_all(spread, BOTH, split_axis=0, concat_axis=0, tiled=True, axi...]
    all_to_all x0 -> x1, waiting for transfers between devices: none -> 10.5 us  [body(): lax.all_to_all(spread, BOTH, split_axis=0, concat_axis=0, tiled=True, axi...]
    all_to_all x0 -> x1, starting transfers between devices: none -> 7.79 us  [body(): lax.all_to_all(spread, BOTH, split_axis=0, concat_axis=0, tiled=True, axi...]
  transfers between devices with their start and end apart: 8 -> 9, of which waited for: 3 -> 4; matrix products, arithmetic and copies ran while one was open for 1% -> 1% of each run, Pallas kernels for 4% -> 4%
where the time goes in v12:
time: 91.5 us; the launch traced here: 91 us
  starting transfers between devices  41.9 us (46%)
  waiting for transfers between devices  21.6 us (24%)
  blocking collectives  15.9 us (17%)
  Pallas kernels  8.16 us (9%)
  local copies, waits for them, and re-layouts  2.46 us (3%)
    ppermute x7, starting transfers between devices, moved(): return lax.ppermute(value, BOTH, pairs)  29 us
    all_to_all x1, blocking collectives, body(): lax.all_to_all(mixed.reshape(members, tokens, LANES), 'ctx', split_axis=0...  15.9 us
    ppermute x7, waiting for transfers between devices, moved(): return lax.ppermute(value, BOTH, pairs)  11.1 us
    all_to_all x1, waiting for transfers between devices, body(): lax.all_to_all(spread, BOTH, split_axis=0, concat_axis=0, tiled=True, axi...  10.5 us
    all_to_all x1, starting transfers between devices, body(): lax.all_to_all(spread, BOTH, split_axis=0, concat_axis=0, tiled=True, axi...  7.79 us
    all_to_all x1, starting transfers between devices, body(): qkv = lax.all_to_all(packed, 'ctx', split_axis=0, concat_axis=0, tiled=True)  5.13 us
    pallas_call x1, Pallas kernels, body(): pl.pallas_call(memory_kernel, out_shape=jax.ShapeDtypeStruct((span, LANES...  4.45 us
    pallas_call x1, Pallas kernels, body(): pl.pallas_call(functools.partial(local_kernel, rows // BLOCK, rows), out_...  2.11 us
  transfers between devices with their start and end apart: 9, of which 4 were waited for; matrix products, arithmetic and copies ran while one was open for 1% of the time, Pallas kernels for 4%

profile of v12, /device:TPU:1, one launch (start us, length us, event | category | flops | bytes accessed | tf_op | source)
XLA Modules:
  0.0 91.0 jit_solution(18094232991141871014)
XLA Ops:
  0.0 0.8 constant_dynamic-slice_fusion
  0.8 0.8 broadcast_in_dim.2
  1.6 7.8 %all-to-all-start = ((bf16[8,128,256]{2,1,0:T(8,128)(2,1)}), bf16[8,128,256]{2,1,0:T(8,128)(2,1)S(1)}, u32[]{:S(2)}, u32[]{:S(2)}) async-start(bf16[8,128,256]{2,1,0:T(8,128)(2,1)} %broadcast_in_dim.2), calls=%async_computation | async-start | bytes 1048576 | tf_op jit(solution)/shard_map/all_to_all | solution.py:229
  9.5 1.6 %shard_map.73 = bf16[8,64,896]{2,1,0:T(8,128)(2,1)} custom-call(s32[4,16]{1,0:T(4,128)S(1)} %copy-done.3, bf16[64,4096]{1,0:T(8,128)(2,1)S(1)} %copy-done, bf16[64,1024]{1,0:T(8,128)(2,1)S(1)} %copy-done.1, bf16[64,1024]{1,0:T(8,128)(2,1)S(1)} %copy-done.2), custom_call_target="tpu_custom_call" | custom-call | bytes 2097152 | tf_op jit(solution)/shard_map/pallas_call | solution.py:220
  11.1 10.5 %all-to-all-done = bf16[8,128,256]{2,1,0:T(8,128)(2,1)S(1)} async-done(((bf16[8,128,256]{2,1,0:T(8,128)(2,1)}), bf16[8,128,256]{2,1,0:T(8,128)(2,1)S(1)}, u32[]{:S(2)}, u32[]{:S(2)}) %all-to-all-start) | async-done | bytes 524320 | tf_op jit(solution)/shard_map/all_to_all | solution.py:229
  21.6 10.6 %collective-permute-start.3 = (bf16[1024,256]{1,0:T(8,128)(2,1)S(1)}, bf16[1024,256]{1,0:T(8,128)(2,1)S(1)}, u32[]{:S(2)}, u32[]{:S(2)}) collective-permute-start(bf16[1024,256]{1,0:T(8,128)(2,1)S(1)} %bitcast.8), channel_id=1, source_target_pairs={{0,48},{1,385},{2,50},{3,387},{4,52},{5,389},{6,54},{7,391},{8,56}... | collective-permute-start | bytes 1572872 | tf_op jit(solution)/shard_map/ppermute | solution.py:182
  32.2 1.9 %collective-permute-start.1 = (bf16[1024,256]{1,0:T(8,128)(2,1)S(1)}, bf16[1024,256]{1,0:T(8,128)(2,1)S(1)}, u32[]{:S(2)}, u32[]{:S(2)}) collective-permute-start(bf16[1024,256]{1,0:T(8,128)(2,1)S(1)} %bitcast.9), channel_id=1, source_target_pairs={{0,16},{1,129},{2,18},{3,131},{4,20},{5,133},{6,22},{7,135},{8,24}... | collective-permute-start | bytes 1572872 | tf_op jit(solution)/shard_map/ppermute | solution.py:182
  34.2 5.1 %all-to-all-start.1 = ((bf16[8,64,896]{2,1,0:T(8,128)(2,1)}), bf16[8,64,896]{2,1,0:T(8,128)(2,1)S(1)}, u32[]{:S(2)}, u32[]{:S(2)}) async-start(bf16[8,64,896]{2,1,0:T(8,128)(2,1)} %shard_map.73), calls=%async_computation.1 | async-start | bytes 1835008 | tf_op jit(solution)/shard_map/all_to_all | solution.py:233
  39.3 4.8 %collective-permute-start.6 = (bf16[1024,256]{1,0:T(8,128)(2,1)S(1)}, bf16[1024,256]{1,0:T(8,128)(2,1)S(1)}, u32[]{:S(2)}, u32[]{:S(2)}) collective-permute-start(bf16[1024,256]{1,0:T(8,128)(2,1)S(1)} %bitcast.10), channel_id=1, source_target_pairs={{0,56},{1,449},{2,58},{3,451},{4,60},{5,453},{6,62},{7,455},{8,0},... | collective-permute-start | bytes 1572872 | tf_op jit(solution)/shard_map/ppermute | solution.py:182
  44.1 1.9 %collective-permute-start = (bf16[1024,256]{1,0:T(8,128)(2,1)S(1)}, bf16[1024,256]{1,0:T(8,128)(2,1)S(1)}, u32[]{:S(2)}, u32[]{:S(2)}) collective-permute-start(bf16[1024,256]{1,0:T(8,128)(2,1)S(1)} %bitcast.11), channel_id=1, source_target_pairs={{0,8},{1,65},{2,10},{3,67},{4,12},{5,69},{6,14},{7,71},{8,16},{9,7... | collective-permute-start | bytes 1572872 | tf_op jit(solution)/shard_map/ppermute | solution.py:182
  46.0 0.0 collective-permute-done.3.refs_6_
  46.0 4.6 %collective-permute-start.5 = (bf16[1024,256]{1,0:T(8,128)(2,1)S(1)}, bf16[1024,256]{1,0:T(8,128)(2,1)}, u32[]{:S(2)}, u32[]{:S(2)}) collective-permute-start(bf16[1024,256]{1,0:T(8,128)(2,1)S(1)} %collective-permute-done.3.refs_6_), channel_id=1, source_target_pairs={{0,56},{1,449},{2,58},{3,451},{4,60},{5,453},{6,62},{7,455},{8,0},... | collective-permute-start | bytes 1572872 | tf_op jit(solution)/shard_map/ppermute | solution.py:182
  50.6 0.0 collective-permute-done.1.refs_2_
  50.6 0.9 broadcast_select_fusion
  51.4 2.0 %collective-permute-start.4 = (bf16[1024,256]{1,0:T(8,128)(2,1)}, bf16[1024,256]{1,0:T(8,128)(2,1)}, u32[]{:S(2)}, u32[]{:S(2)}) collective-permute-start(bf16[1024,256]{1,0:T(8,128)(2,1)} %broadcast_select_fusion), channel_id=1, source_target_pairs={{0,16},{1,129},{2,18},{3,131},{4,20},{5,133},{6,22},{7,135},{8,56}... | collective-permute-start | bytes 1572872 | tf_op jit(solution)/shard_map/ppermute | solution.py:182
  53.5 3.1 %collective-permute-start.2 = (bf16[1024,256]{1,0:T(8,128)(2,1)S(1)}, bf16[1024,256]{1,0:T(8,128)(2,1)}, u32[]{:S(2)}, u32[]{:S(2)}) collective-permute-start(bf16[1024,256]{1,0:T(8,128)(2,1)S(1)} %collective-permute-done.1.refs_2_), channel_id=1, source_target_pairs={{0,8},{1,65},{2,10},{3,67},{4,12},{5,69},{6,14},{7,71},{8,16},{9,7... | collective-permute-start | bytes 1572872 | tf_op jit(solution)/shard_map/ppermute | solution.py:182
  56.6 2.1 %shard_map.74 = (f32[512,512]{1,0:T(8,128)S(1)}, s32[4,128]{1,0:T(4,128)S(1)}, f32[4,128]{1,0:T(4,128)S(1)}) custom-call(f32[32]{0:T(128)S(1)} %copy-done.4, bf16[512,896]{1,0:T(8,128)(2,1)S(1)} %bitcast.6), custom_call_target="tpu_custom_call" | custom-call | flops 536870912 | bytes 2097152 | tf_op jit(solution)/shard_map/pallas_call | solution.py:236
  58.7 0.0 collective-permute-done.refs_1_
  58.7 3.6 %collective-permute-done.5.refs_5_ = bf16[1024,256]{1,0:T(8,128)(2,1)} collective-permute-done((bf16[1024,256]{1,0:T(8,128)(2,1)S(1)}, bf16[1024,256]{1,0:T(8,128)(2,1)}, u32[]{:S(2)}, u32[]{:S(2)}) %collective-permute-start.5) | collective-permute-done | bytes 524320 | tf_op jit(solution)/shard_map/ppermute | solution.py:182
  62.3 2.0 %collective-permute-done.4.refs_4_ = bf16[1024,256]{1,0:T(8,128)(2,1)} collective-permute-done((bf16[1024,256]{1,0:T(8,128)(2,1)}, bf16[1024,256]{1,0:T(8,128)(2,1)}, u32[]{:S(2)}, u32[]{:S(2)}) %collective-permute-start.4) | collective-permute-done | bytes 524320 | tf_op jit(solution)/shard_map/ppermute | solution.py:182
  64.2 5.6 %collective-permute-done.2.refs_3_ = bf16[1024,256]{1,0:T(8,128)(2,1)} collective-permute-done((bf16[1024,256]{1,0:T(8,128)(2,1)S(1)}, bf16[1024,256]{1,0:T(8,128)(2,1)}, u32[]{:S(2)}, u32[]{:S(2)}) %collective-permute-start.2) | collective-permute-done | bytes 524320 | tf_op jit(solution)/shard_map/ppermute | solution.py:182
  69.8 4.4 %shard_map.75 = bf16[512,512]{1,0:T(8,128)(2,1)S(1)} custom-call(s32[4,128]{1,0:T(4,128)S(1)} %get-tuple-element.11.starts_ref, f32[4,128]{1,0:T(4,128)S(1)} %get-tuple-element.12.gates_ref, bf16[512,896]{1,0:T(8,128)(2,1)S(1)} %bitcast.7, f32[512,512]{1,0:T(8,128)S(1)} %get-tuple-element.13.local_ref, bf16[1024,256]{1,0:T(8,128)(2,1)S(1)} %bitcast.12, ...), custom_call_target="tpu_custom_call" | custom-call | flops 536870912 | bytes 7340032 | tf_op jit(solution)/shard_map/pallas_call | solution.py:250
  74.3 15.9 %all_to_all.15 = bf16[8,64,512]{2,1,0:T(8,128)(2,1)S(1)} all-to-all(bf16[8,64,512]{2,1,0:T(8,128)(2,1)S(1)} %bitcast.13), channel_id=1, replica_groups=mesh['mem'=64,'ctx'=8] {'ctx'}, dimensions={0} | all-to-all | bytes 1048576 | tf_op jit(solution)/shard_map/all_to_all | solution.py:266
  90.1 0.8 copy.9
  (13 shorter events, 0.0 us)
Async XLA Ops:
  1.6 7.8 %copy-start = (bf16[64,4096]{1,0:T(8,128)(2,1)S(1)}, bf16[64,4096]{1,0:T(8,128)(2,1)}, u32[]{:S(2)}) copy-start(bf16[64,4096]{1,0:T(8,128)(2,1)} %queries_ref.1) | copy-start | bytes 1572868
  1.6 7.8 %copy-start.1 = (bf16[64,1024]{1,0:T(8,128)(2,1)S(1)}, bf16[64,1024]{1,0:T(8,128)(2,1)}, u32[]{:S(2)}) copy-start(bf16[64,1024]{1,0:T(8,128)(2,1)} %keys_ref.1) | copy-start | bytes 393220
  1.6 7.8 %copy-start.2 = (bf16[64,1024]{1,0:T(8,128)(2,1)S(1)}, bf16[64,1024]{1,0:T(8,128)(2,1)}, u32[]{:S(2)}) copy-start(bf16[64,1024]{1,0:T(8,128)(2,1)} %values_ref.1) | copy-start | bytes 393220
  1.6 7.8 %copy-start.3 = (s32[4,16]{1,0:T(4,128)S(1)}, s32[4,16]{1,0:T(4,128)}, u32[]{:S(2)}) copy-start(s32[4,16]{1,0:T(4,128)} %ids_ref.1) | copy-start | bytes 772
  1.6 19.9 %all-to-all-start = ((bf16[8,128,256]{2,1,0:T(8,128)(2,1)}), bf16[8,128,256]{2,1,0:T(8,128)(2,1)S(1)}, u32[]{:S(2)}, u32[]{:S(2)}) async-start(bf16[8,128,256]{2,1,0:T(8,128)(2,1)} %broadcast_in_dim.2), calls=%async_computation | async-start | bytes 1048576 | tf_op jit(solution)/shard_map/all_to_all | solution.py:229
  21.6 24.4 %collective-permute-start.3 = (bf16[1024,256]{1,0:T(8,128)(2,1)S(1)}, bf16[1024,256]{1,0:T(8,128)(2,1)S(1)}, u32[]{:S(2)}, u32[]{:S(2)}) collective-permute-start(bf16[1024,256]{1,0:T(8,128)(2,1)S(1)} %bitcast.8), channel_id=1, source_target_pairs={{0,48},{1,385},{2,50},{3,387},{4,52},{5,389},{6,54},{7,391},{8,56}... | collective-permute-start | bytes 1572872 | tf_op jit(solution)/shard_map/ppermute | solution.py:182
  32.2 18.4 %collective-permute-start.1 = (bf16[1024,256]{1,0:T(8,128)(2,1)S(1)}, bf16[1024,256]{1,0:T(8,128)(2,1)S(1)}, u32[]{:S(2)}, u32[]{:S(2)}) collective-permute-start(bf16[1024,256]{1,0:T(8,128)(2,1)S(1)} %bitcast.9), channel_id=1, source_target_pairs={{0,16},{1,129},{2,18},{3,131},{4,20},{5,133},{6,22},{7,135},{8,24}... | collective-permute-start | bytes 1572872 | tf_op jit(solution)/shard_map/ppermute | solution.py:182
  34.2 22.4 %all-to-all-start.1 = ((bf16[8,64,896]{2,1,0:T(8,128)(2,1)}), bf16[8,64,896]{2,1,0:T(8,128)(2,1)S(1)}, u32[]{:S(2)}, u32[]{:S(2)}) async-start(bf16[8,64,896]{2,1,0:T(8,128)(2,1)} %shard_map.73), calls=%async_computation.1 | async-start | bytes 1835008 | tf_op jit(solution)/shard_map/all_to_all | solution.py:233
  39.3 19.4 %collective-permute-start.6 = (bf16[1024,256]{1,0:T(8,128)(2,1)S(1)}, bf16[1024,256]{1,0:T(8,128)(2,1)S(1)}, u32[]{:S(2)}, u32[]{:S(2)}) collective-permute-start(bf16[1024,256]{1,0:T(8,128)(2,1)S(1)} %bitcast.10), channel_id=1, source_target_pairs={{0,56},{1,449},{2,58},{3,451},{4,60},{5,453},{6,62},{7,455},{8,0},... | collective-permute-start | bytes 1572872 | tf_op jit(solution)/shard_map/ppermute | solution.py:182
  44.1 14.7 %collective-permute-start = (bf16[1024,256]{1,0:T(8,128)(2,1)S(1)}, bf16[1024,256]{1,0:T(8,128)(2,1)S(1)}, u32[]{:S(2)}, u32[]{:S(2)}) collective-permute-start(bf16[1024,256]{1,0:T(8,128)(2,1)S(1)} %bitcast.11), channel_id=1, source_target_pairs={{0,8},{1,65},{2,10},{3,67},{4,12},{5,69},{6,14},{7,71},{8,16},{9,7... | collective-permute-start | bytes 1572872 | tf_op jit(solution)/shard_map/ppermute | solution.py:182
  46.0 16.3 %collective-permute-start.5 = (bf16[1024,256]{1,0:T(8,128)(2,1)S(1)}, bf16[1024,256]{1,0:T(8,128)(2,1)}, u32[]{:S(2)}, u32[]{:S(2)}) collective-permute-start(bf16[1024,256]{1,0:T(8,128)(2,1)S(1)} %collective-permute-done.3.refs_6_), channel_id=1, source_target_pairs={{0,56},{1,449},{2,58},{3,451},{4,60},{5,453},{6,62},{7,455},{8,0},... | collective-permute-start | bytes 1572872 | tf_op jit(solution)/shard_map/ppermute | solution.py:182
  51.4 5.2 %copy-start.4 = (f32[32]{0:T(128)S(1)}, f32[32]{0:T(128)}, u32[]{:S(2)}) copy-start(f32[32]{0:T(128)} %bias_ref.1) | copy-start | bytes 388
  51.4 12.8 %collective-permute-start.4 = (bf16[1024,256]{1,0:T(8,128)(2,1)}, bf16[1024,256]{1,0:T(8,128)(2,1)}, u32[]{:S(2)}, u32[]{:S(2)}) collective-permute-start(bf16[1024,256]{1,0:T(8,128)(2,1)} %broadcast_select_fusion), channel_id=1, source_target_pairs={{0,16},{1,129},{2,18},{3,131},{4,20},{5,133},{6,22},{7,135},{8,56}... | collective-permute-start | bytes 1572872 | tf_op jit(solution)/shard_map/ppermute | solution.py:182
  53.5 16.3 %collective-permute-start.2 = (bf16[1024,256]{1,0:T(8,128)(2,1)S(1)}, bf16[1024,256]{1,0:T(8,128)(2,1)}, u32[]{:S(2)}, u32[]{:S(2)}) collective-permute-start(bf16[1024,256]{1,0:T(8,128)(2,1)S(1)} %collective-permute-done.1.refs_2_), channel_id=1, source_target_pairs={{0,8},{1,65},{2,10},{3,67},{4,12},{5,69},{6,14},{7,71},{8,16},{9,7... | collective-permute-start | bytes 1572872 | tf_op jit(solution)/shard_map/ppermute | solution.py:182

commit v13 on v11

--- a/solution.py
+++ b/solution.py
@@ -243,7 +243,7 @@
         out_specs=(vmem, vmem, vmem),
         compiler_params=pltpu.CompilerParams(vmem_limit_bytes=12 << 20),
         cost_estimate=pl.CostEstimate(
-            flops=4 * span * LANES * span, bytes_accessed=2 << 20, transcendentals=span * span * 4
+            flops=64 * span * LANES * span, bytes_accessed=2 << 20, transcendentals=span * span * 4
         ),
     )(gate_bias, qkv)
     mixed = pl.pallas_call(

time: 92.2 us -> 95.8 us (1.039)
  blocking collectives: 35.6 us -> 16.3 us
  waiting for transfers between devices: 11.1 us -> 27.7 us
  starting transfers between devices: 34.1 us -> 39.5 us
    all_to_all x1 -> x0, blocking collectives: 19.7 us -> none  [body(): lax.all_to_all(spread, BOTH, split_axis=0, concat_axis=0, tiled=True, axi...]
    all_to_all x0 -> x1, waiting for transfers between devices: none -> 10.5 us  [body(): lax.all_to_all(spread, BOTH, split_axis=0, concat_axis=0, tiled=True, axi...]
    all_to_all x0 -> x1, starting transfers between devices: none -> 7.79 us  [body(): lax.all_to_all(spread, BOTH, split_axis=0, concat_axis=0, tiled=True, axi...]
    ppermute x7, starting transfers between devices: 29 us -> 22.1 us  [moved(): return lax.ppermute(value, BOTH, pairs)]
    ppermute x7, waiting for transfers between devices: 11.1 us -> 17.2 us  [moved(): return lax.ppermute(value, BOTH, pairs)]
    all_to_all x1, starting transfers between devices: 5.12 us -> 9.62 us  [body(): qkv = lax.all_to_all(packed, 'ctx', split_axis=0, concat_axis=0, tiled=True)]
  transfers between devices with their start and end apart: 8 -> 9, of which waited for: 3 -> 5; matrix products, arithmetic and copies ran while one was open for 1% -> 1% of each run, Pallas kernels for 4% -> 4%
where the time goes in v13:
time: 95.8 us; the launch traced here: 95.2 us
  starting transfers between devices  39.5 us (41%)
  waiting for transfers between devices  27.7 us (29%)
  blocking collectives  16.3 us (17%)
  Pallas kernels  8.16 us (9%)
  local copies, waits for them, and re-layouts  2.46 us (3%)
    ppermute x7, starting transfers between devices, moved(): return lax.ppermute(value, BOTH, pairs)  22.1 us
    ppermute x7, waiting for transfers between devices, moved(): return lax.ppermute(value, BOTH, pairs)  17.2 us
    all_to_all x1, blocking collectives, body(): lax.all_to_all(mixed.reshape(members, tokens, LANES), 'ctx', split_axis=0...  16.3 us
    all_to_all x1, waiting for transfers between devices, body(): lax.all_to_all(spread, BOTH, split_axis=0, concat_axis=0, tiled=True, axi...  10.5 us
    all_to_all x1, starting transfers between devices, body(): qkv = lax.all_to_all(packed, 'ctx', split_axis=0, concat_axis=0, tiled=True)  9.62 us
    all_to_all x1, starting transfers between devices, body(): lax.all_to_all(spread, BOTH, split_axis=0, concat_axis=0, tiled=True, axi...  7.79 us
    pallas_call x1, Pallas kernels, body(): pl.pallas_call(memory_kernel, out_shape=jax.ShapeDtypeStruct((span, LANES...  4.45 us
    pallas_call x1, Pallas kernels, body(): pl.pallas_call(functools.partial(local_kernel, rows // BLOCK, rows), out_...  2.11 us
  transfers between devices with their start and end apart: 9, of which 5 were waited for; matrix products, arithmetic and copies ran while one was open for 1% of the time, Pallas kernels for 4%

profile of v13, /device:TPU:1, one launch (start us, length us, event | category | flops | bytes accessed | tf_op | source)
XLA Modules:
  0.0 95.2 jit_solution(7165445417612027176)
XLA Ops:
  0.0 0.8 constant_dynamic-slice_fusion
  0.8 0.8 broadcast_in_dim.2
  1.6 7.8 %all-to-all-start.1 = ((bf16[8,128,256]{2,1,0:T(8,128)(2,1)}), bf16[8,128,256]{2,1,0:T(8,128)(2,1)S(1)}, u32[]{:S(2)}, u32[]{:S(2)}) async-start(bf16[8,128,256]{2,1,0:T(8,128)(2,1)} %broadcast_in_dim.2), calls=%async_computation.1 | async-start | bytes 1048576 | tf_op jit(solution)/shard_map/all_to_all | solution.py:231
  9.5 1.6 %shard_map.73 = bf16[8,64,896]{2,1,0:T(8,128)(2,1)} custom-call(s32[4,16]{1,0:T(4,128)S(1)} %copy-done.3, bf16[64,4096]{1,0:T(8,128)(2,1)S(1)} %copy-done, bf16[64,1024]{1,0:T(8,128)(2,1)S(1)} %copy-done.1, bf16[64,1024]{1,0:T(8,128)(2,1)S(1)} %copy-done.2), custom_call_target="tpu_custom_call" | custom-call | bytes 2097152 | tf_op jit(solution)/shard_map/pallas_call | solution.py:220
  11.1 10.5 %all-to-all-done.1 = bf16[8,128,256]{2,1,0:T(8,128)(2,1)S(1)} async-done(((bf16[8,128,256]{2,1,0:T(8,128)(2,1)}), bf16[8,128,256]{2,1,0:T(8,128)(2,1)S(1)}, u32[]{:S(2)}, u32[]{:S(2)}) %all-to-all-start.1) | async-done | bytes 524320 | tf_op jit(solution)/shard_map/all_to_all | solution.py:231
  21.6 9.6 %all-to-all-start = ((bf16[8,64,896]{2,1,0:T(8,128)(2,1)}), bf16[8,64,896]{2,1,0:T(8,128)(2,1)S(1)}, u32[]{:S(2)}, u32[]{:S(2)}) async-start(bf16[8,64,896]{2,1,0:T(8,128)(2,1)} %shard_map.73), calls=%async_computation | async-start | bytes 1835008 | tf_op jit(solution)/shard_map/all_to_all | solution.py:229
  31.2 5.4 %collective-permute-start.3 = (bf16[1024,256]{1,0:T(8,128)(2,1)S(1)}, bf16[1024,256]{1,0:T(8,128)(2,1)S(1)}, u32[]{:S(2)}, u32[]{:S(2)}) collective-permute-start(bf16[1024,256]{1,0:T(8,128)(2,1)S(1)} %bitcast.8), channel_id=1, source_target_pairs={{0,48},{1,385},{2,50},{3,387},{4,52},{5,389},{6,54},{7,391},{8,56}... | collective-permute-start | bytes 1572872 | tf_op jit(solution)/shard_map/ppermute | solution.py:182
  36.6 1.9 %collective-permute-start.1 = (bf16[1024,256]{1,0:T(8,128)(2,1)S(1)}, bf16[1024,256]{1,0:T(8,128)(2,1)S(1)}, u32[]{:S(2)}, u32[]{:S(2)}) collective-permute-start(bf16[1024,256]{1,0:T(8,128)(2,1)S(1)} %bitcast.9), channel_id=1, source_target_pairs={{0,16},{1,129},{2,18},{3,131},{4,20},{5,133},{6,22},{7,135},{8,24}... | collective-permute-start | bytes 1572872 | tf_op jit(solution)/shard_map/ppermute | solution.py:182
  38.6 5.5 %collective-permute-start.6 = (bf16[1024,256]{1,0:T(8,128)(2,1)S(1)}, bf16[1024,256]{1,0:T(8,128)(2,1)S(1)}, u32[]{:S(2)}, u32[]{:S(2)}) collective-permute-start(bf16[1024,256]{1,0:T(8,128)(2,1)S(1)} %bitcast.10), channel_id=1, source_target_pairs={{0,56},{1,449},{2,58},{3,451},{4,60},{5,453},{6,62},{7,455},{8,0},... | collective-permute-start | bytes 1572872 | tf_op jit(solution)/shard_map/ppermute | solution.py:182
  44.1 1.9 %collective-permute-start = (bf16[1024,256]{1,0:T(8,128)(2,1)S(1)}, bf16[1024,256]{1,0:T(8,128)(2,1)S(1)}, u32[]{:S(2)}, u32[]{:S(2)}) collective-permute-start(bf16[1024,256]{1,0:T(8,128)(2,1)S(1)} %bitcast.11), channel_id=1, source_target_pairs={{0,8},{1,65},{2,10},{3,67},{4,12},{5,69},{6,14},{7,71},{8,16},{9,7... | collective-permute-start | bytes 1572872 | tf_op jit(solution)/shard_map/ppermute | solution.py:182
  46.0 1.9 %collective-permute-done.3.refs_6_ = bf16[1024,256]{1,0:T(8,128)(2,1)S(1)} collective-permute-done((bf16[1024,256]{1,0:T(8,128)(2,1)S(1)}, bf16[1024,256]{1,0:T(8,128)(2,1)S(1)}, u32[]{:S(2)}, u32[]{:S(2)}) %collective-permute-start.3) | collective-permute-done | bytes 524320 | tf_op jit(solution)/shard_map/ppermute | solution.py:182
  48.0 6.4 %collective-permute-done.1.refs_2_ = bf16[1024,256]{1,0:T(8,128)(2,1)S(1)} collective-permute-done((bf16[1024,256]{1,0:T(8,128)(2,1)S(1)}, bf16[1024,256]{1,0:T(8,128)(2,1)S(1)}, u32[]{:S(2)}, u32[]{:S(2)}) %collective-permute-start.1) | collective-permute-done | bytes 524320 | tf_op jit(solution)/shard_map/ppermute | solution.py:182
  54.3 0.8 broadcast_select_fusion
  55.2 2.0 %collective-permute-start.4 = (bf16[1024,256]{1,0:T(8,128)(2,1)}, bf16[1024,256]{1,0:T(8,128)(2,1)}, u32[]{:S(2)}, u32[]{:S(2)}) collective-permute-start(bf16[1024,256]{1,0:T(8,128)(2,1)} %broadcast_select_fusion), channel_id=1, source_target_pairs={{0,16},{1,129},{2,18},{3,131},{4,20},{5,133},{6,22},{7,135},{8,56}... | collective-permute-start | bytes 1572872 | tf_op jit(solution)/shard_map/ppermute | solution.py:182
  57.2 2.5 %collective-permute-start.5 = (bf16[1024,256]{1,0:T(8,128)(2,1)S(1)}, bf16[1024,256]{1,0:T(8,128)(2,1)}, u32[]{:S(2)}, u32[]{:S(2)}) collective-permute-start(bf16[1024,256]{1,0:T(8,128)(2,1)S(1)} %collective-permute-done.3.refs_6_), channel_id=1, source_target_pairs={{0,56},{1,449},{2,58},{3,451},{4,60},{5,453},{6,62},{7,455},{8,0},... | collective-permute-start | bytes 1572872 | tf_op jit(solution)/shard_map/ppermute | solution.py:182
  59.7 2.8 %collective-permute-start.2 = (bf16[1024,256]{1,0:T(8,128)(2,1)S(1)}, bf16[1024,256]{1,0:T(8,128)(2,1)}, u32[]{:S(2)}, u32[]{:S(2)}) collective-permute-start(bf16[1024,256]{1,0:T(8,128)(2,1)S(1)} %collective-permute-done.1.refs_2_), channel_id=1, source_target_pairs={{0,8},{1,65},{2,10},{3,67},{4,12},{5,69},{6,14},{7,71},{8,16},{9,7... | collective-permute-start | bytes 1572872 | tf_op jit(solution)/shard_map/ppermute | solution.py:182
  62.6 2.1 %shard_map.74 = (f32[512,512]{1,0:T(8,128)S(1)}, s32[4,128]{1,0:T(4,128)S(1)}, f32[4,128]{1,0:T(4,128)S(1)}) custom-call(f32[32]{0:T(128)S(1)} %copy-done.4, bf16[512,896]{1,0:T(8,128)(2,1)S(1)} %bitcast.6), custom_call_target="tpu_custom_call" | custom-call | flops 8589934592 | bytes 2097152 | tf_op jit(solution)/shard_map/pallas_call | solution.py:235
  64.7 0.0 collective-permute-done.6.refs_7_
  64.7 0.0 collective-permute-done.refs_1_
  64.7 5.9 %collective-permute-done.5.refs_5_ = bf16[1024,256]{1,0:T(8,128)(2,1)} collective-permute-done((bf16[1024,256]{1,0:T(8,128)(2,1)S(1)}, bf16[1024,256]{1,0:T(8,128)(2,1)}, u32[]{:S(2)}, u32[]{:S(2)}) %collective-permute-start.5) | collective-permute-done | bytes 524320 | tf_op jit(solution)/shard_map/ppermute | solution.py:182
  70.6 3.0 %collective-permute-done.2.refs_3_ = bf16[1024,256]{1,0:T(8,128)(2,1)} collective-permute-done((bf16[1024,256]{1,0:T(8,128)(2,1)S(1)}, bf16[1024,256]{1,0:T(8,128)(2,1)}, u32[]{:S(2)}, u32[]{:S(2)}) %collective-permute-start.2) | collective-permute-done | bytes 524320 | tf_op jit(solution)/shard_map/ppermute | solution.py:182
  73.6 4.4 %shard_map.75 = bf16[512,512]{1,0:T(8,128)(2,1)S(1)} custom-call(s32[4,128]{1,0:T(4,128)S(1)} %get-tuple-element.8.starts_ref, f32[4,128]{1,0:T(4,128)S(1)} %get-tuple-element.9.gates_ref, bf16[512,896]{1,0:T(8,128)(2,1)S(1)} %bitcast.7, f32[512,512]{1,0:T(8,128)S(1)} %get-tuple-element.10.local_ref, bf16[1024,256]{1,0:T(8,128)(2,1)S(1)} %bitcast.12, ...), custom_call_target="tpu_custom_call" | custom-call | flops 536870912 | bytes 7340032 | tf_op jit(solution)/shard_map/pallas_call | solution.py:249
  78.0 16.3 %all_to_all.15 = bf16[8,64,512]{2,1,0:T(8,128)(2,1)S(1)} all-to-all(bf16[8,64,512]{2,1,0:T(8,128)(2,1)S(1)} %bitcast.13), channel_id=1, replica_groups=mesh['mem'=64,'ctx'=8] {'ctx'}, dimensions={0} | all-to-all | bytes 1048576 | tf_op jit(solution)/shard_map/all_to_all | solution.py:265
  94.4 0.8 copy.9
  (13 shorter events, 0.0 us)
Async XLA Ops:
  1.6 7.8 %copy-start = (bf16[64,4096]{1,0:T(8,128)(2,1)S(1)}, bf16[64,4096]{1,0:T(8,128)(2,1)}, u32[]{:S(2)}) copy-start(bf16[64,4096]{1,0:T(8,128)(2,1)} %queries_ref.1) | copy-start | bytes 1572868
  1.6 7.8 %copy-start.1 = (bf16[64,1024]{1,0:T(8,128)(2,1)S(1)}, bf16[64,1024]{1,0:T(8,128)(2,1)}, u32[]{:S(2)}) copy-start(bf16[64,1024]{1,0:T(8,128)(2,1)} %keys_ref.1) | copy-start | bytes 393220
  1.6 7.8 %copy-start.2 = (bf16[64,1024]{1,0:T(8,128)(2,1)S(1)}, bf16[64,1024]{1,0:T(8,128)(2,1)}, u32[]{:S(2)}) copy-start(bf16[64,1024]{1,0:T(8,128)(2,1)} %values_ref.1) | copy-start | bytes 393220
  1.6 7.8 %copy-start.3 = (s32[4,16]{1,0:T(4,128)S(1)}, s32[4,16]{1,0:T(4,128)}, u32[]{:S(2)}) copy-start(s32[4,16]{1,0:T(4,128)} %ids_ref.1) | copy-start | bytes 772
  1.6 19.9 %all-to-all-start.1 = ((bf16[8,128,256]{2,1,0:T(8,128)(2,1)}), bf16[8,128,256]{2,1,0:T(8,128)(2,1)S(1)}, u32[]{:S(2)}, u32[]{:S(2)}) async-start(bf16[8,128,256]{2,1,0:T(8,128)(2,1)} %broadcast_in_dim.2), calls=%async_computation.1 | async-start | bytes 1048576 | tf_op jit(solution)/shard_map/all_to_all | solution.py:231
  21.6 41.0 %all-to-all-start = ((bf16[8,64,896]{2,1,0:T(8,128)(2,1)}), bf16[8,64,896]{2,1,0:T(8,128)(2,1)S(1)}, u32[]{:S(2)}, u32[]{:S(2)}) async-start(bf16[8,64,896]{2,1,0:T(8,128)(2,1)} %shard_map.73), calls=%async_computation | async-start | bytes 1835008 | tf_op jit(solution)/shard_map/all_to_all | solution.py:229
  31.2 16.8 %collective-permute-start.3 = (bf16[1024,256]{1,0:T(8,128)(2,1)S(1)}, bf16[1024,256]{1,0:T(8,128)(2,1)S(1)}, u32[]{:S(2)}, u32[]{:S(2)}) collective-permute-start(bf16[1024,256]{1,0:T(8,128)(2,1)S(1)} %bitcast.8), channel_id=1, source_target_pairs={{0,48},{1,385},{2,50},{3,387},{4,52},{5,389},{6,54},{7,391},{8,56}... | collective-permute-start | bytes 1572872 | tf_op jit(solution)/shard_map/ppermute | solution.py:182
  36.6 17.7 %collective-permute-start.1 = (bf16[1024,256]{1,0:T(8,128)(2,1)S(1)}, bf16[1024,256]{1,0:T(8,128)(2,1)S(1)}, u32[]{:S(2)}, u32[]{:S(2)}) collective-permute-start(bf16[1024,256]{1,0:T(8,128)(2,1)S(1)} %bitcast.9), channel_id=1, source_target_pairs={{0,16},{1,129},{2,18},{3,131},{4,20},{5,133},{6,22},{7,135},{8,24}... | collective-permute-start | bytes 1572872 | tf_op jit(solution)/shard_map/ppermute | solution.py:182
  38.6 26.1 %collective-permute-start.6 = (bf16[1024,256]{1,0:T(8,128)(2,1)S(1)}, bf16[1024,256]{1,0:T(8,128)(2,1)S(1)}, u32[]{:S(2)}, u32[]{:S(2)}) collective-permute-start(bf16[1024,256]{1,0:T(8,128)(2,1)S(1)} %bitcast.10), channel_id=1, source_target_pairs={{0,56},{1,449},{2,58},{3,451},{4,60},{5,453},{6,62},{7,455},{8,0},... | collective-permute-start | bytes 1572872 | tf_op jit(solution)/shard_map/ppermute | solution.py:182
  44.1 20.6 %collective-permute-start = (bf16[1024,256]{1,0:T(8,128)(2,1)S(1)}, bf16[1024,256]{1,0:T(8,128)(2,1)S(1)}, u32[]{:S(2)}, u32[]{:S(2)}) collective-permute-start(bf16[1024,256]{1,0:T(8,128)(2,1)S(1)} %bitcast.11), channel_id=1, source_target_pairs={{0,8},{1,65},{2,10},{3,67},{4,12},{5,69},{6,14},{7,71},{8,16},{9,7... | collective-permute-start | bytes 1572872 | tf_op jit(solution)/shard_map/ppermute | solution.py:182
  55.2 7.4 %copy-start.4 = (f32[32]{0:T(128)S(1)}, f32[32]{0:T(128)}, u32[]{:S(2)}) copy-start(f32[32]{0:T(128)} %bias_ref.1) | copy-start | bytes 388
  55.2 15.4 %collective-permute-start.4 = (bf16[1024,256]{1,0:T(8,128)(2,1)}, bf16[1024,256]{1,0:T(8,128)(2,1)}, u32[]{:S(2)}, u32[]{:S(2)}) collective-permute-start(bf16[1024,256]{1,0:T(8,128)(2,1)} %broadcast_select_fusion), channel_id=1, source_target_pairs={{0,16},{1,129},{2,18},{3,131},{4,20},{5,133},{6,22},{7,135},{8,56}... | collective-permute-start | bytes 1572872 | tf_op jit(solution)/shard_map/ppermute | solution.py:182
  57.2 13.3 %collective-permute-start.5 = (bf16[1024,256]{1,0:T(8,128)(2,1)S(1)}, bf16[1024,256]{1,0:T(8,128)(2,1)}, u32[]{:S(2)}, u32[]{:S(2)}) collective-permute-start(bf16[1024,256]{1,0:T(8,128)(2,1)S(1)} %collective-permute-done.3.refs_6_), channel_id=1, source_target_pairs={{0,56},{1,449},{2,58},{3,451},{4,60},{5,453},{6,62},{7,455},{8,0},... | collective-permute-start | bytes 1572872 | tf_op jit(solution)/shard_map/ppermute | solution.py:182
  59.7 13.9 %collective-permute-start.2 = (bf16[1024,256]{1,0:T(8,128)(2,1)S(1)}, bf16[1024,256]{1,0:T(8,128)(2,1)}, u32[]{:S(2)}, u32[]{:S(2)}) collective-permute-start(bf16[1024,256]{1,0:T(8,128)(2,1)S(1)} %collective-permute-done.1.refs_2_), channel_id=1, source_target_pairs={{0,8},{1,65},{2,10},{3,67},{4,12},{5,69},{6,14},{7,71},{8,16},{9,7... | collective-permute-start | bytes 1572872 | tf_op jit(solution)/shard_map/ppermute | solution.py:182
